TPU v7x, 128 devices: a whole 4x4x4 slice. The times are simulated.
128 devices in a mesh: gx: 8 (over z, y_lo), gy: 16 (over x, y_hi, core).
Axes of the slice: x: 4, y: 4 (y_hi: 2, y_lo: 2; y = y_hi * 2 + y_lo), z: 4, core: 2. Of those that a mesh axis runs over, the one named last changes fastest.
Arguments:
- positions: float32 [3, 327680], P(None, ('gx', 'gy')), may hold values from 0 to 1
- velocities: float32 [3, 327680], P(None, ('gx', 'gy')), may hold values from -6 to 6
- block_order: int32 [128, 20], P(('gx', 'gy')), may hold values from 0 to 19, each once within a row
- flags: int32 [128, 20], P(('gx', 'gy')), may hold values from 0 to 1, as said below
- offsets: int32 [3, 3], replicated, may hold values from -1 to 1
- pixels: int32 [3, 327680], P(None, ('gx', 'gy')), may hold values from 0 to 1048575, as said below
Outputs:
- new_positions: float32 [3, 327680], P(None, ('gx', 'gy'))
- new_velocities: float32 [3, 327680], P(None, ('gx', 'gy'))
- maps: float32 [8192, 384], P(('gx', 'gy'))
Inputs may be any that keep to these rules, and one draw needn't show every extreme that they name: `flags`: each row holds 1 to 5 ones, and some row holds exactly 5. `block_order`: each row is a permutation. Among the 2560 columns of one slab cell and one replica, every strip of 8192 consecutive pixels is named exactly 2560 / 128 times.
All inputs are finite; a program needn't handle non-finite values.
Results may differ from a plain program's by a relative error of at most 0.0028.
Values may be sent and summed in bfloat16 or wider, within the bound.
A program may use at most 448 MiB of HBM per device.

v0:
```python
import jax
import jax.numpy as jnp
from jax import lax
from jax.sharding import PartitionSpec as P

MOVERS = 2
CROSS_MAX = 5
REPLICAS = 3
STRIP_ROWS = 64


time_step = 0.05
lane_count = 128


def passed_along(block, axis, distance):
    devices = range(lax.axis_size(axis))
    route = [((i - distance) % len(devices), i) for i in devices]
    return lax.ppermute(block, axis, route)


def sky_terms(shifted, speeds, live_mask):
    radius = jnp.sum(shifted * shifted, axis=1)
    weight = 1.0 / (1.0 + radius)
    radial = jnp.sum(speeds[None] * shifted, axis=1) / jnp.sqrt(1.0 + radius)
    energy = jnp.sum(speeds * speeds, axis=0) / 3.0
    return jnp.stack(
        [weight * live_mask, weight * radial * live_mask, weight * energy[None] * live_mask], axis=0
    ).astype(jnp.bfloat16)


def deposit(values, pixel_ids, target_of, row_total):
    entries = values.shape[0] * values.shape[2]
    flat_values = jnp.transpose(values, (0, 2, 1)).reshape(entries, 3)
    flat_ids = pixel_ids.reshape(entries)
    target = target_of(flat_ids // lane_count)
    lane_ids = flat_ids % lane_count
    row_hits = (target[None, :] == jnp.arange(row_total, dtype=jnp.int32)[:, None]).astype(
        jnp.bfloat16
    )
    lane_hits = (lane_ids[:, None] == jnp.arange(lane_count, dtype=jnp.int32)[None, :]).astype(
        jnp.bfloat16
    )
    spread = (flat_values[:, :, None] * lane_hits[:, None, :]).reshape(entries, 3 * lane_count)
    return jnp.dot(row_hits, spread, preferred_element_type=jnp.float32)


def on_device(positions, velocities, block_order, flags, offsets, pixels):
    blocks = block_order.shape[1]
    width = positions.shape[1] // blocks
    places = positions.reshape(3, blocks, width)
    speeds = velocities.reshape(3, blocks, width)
    places = places + time_step * speeds
    ordering = block_order[0]
    places = jnp.take(places, ordering, axis=1)
    speeds = jnp.take(speeds, ordering, axis=1)

    def leaving(which_set, component, sign_step):
        first_block = which_set * MOVERS
        moved_pos = places[:, first_block : first_block + MOVERS].at[component].add(sign_step)
        return (moved_pos, speeds[:, first_block : first_block + MOVERS])

    east_pos, east_vel = leaving(0, 0, -1.0)
    from_west = passed_along((east_pos, east_vel), "gx", 1)
    west_pos, west_vel = leaving(1, 0, 1.0)
    from_east = passed_along((west_pos, west_vel), "gx", -1)
    north_pos, north_vel = leaving(2, 1, -1.0)
    from_south = passed_along((north_pos, north_vel), "gy", 1)
    south_pos, south_vel = leaving(3, 1, 1.0)
    from_north = passed_along((south_pos, south_vel), "gy", -1)
    arrived = (from_west, from_east, from_south, from_north)
    new_places = jnp.concatenate(
        [places[:, 4 * MOVERS :]] + [received[0] for received in arrived], axis=1
    )
    new_speeds = jnp.concatenate(
        [speeds[:, 4 * MOVERS :]] + [received[1] for received in arrived], axis=1
    )
    count_x = lax.axis_size("gx")
    count_y = lax.axis_size("gy")
    cell_x = lax.axis_index("gx")
    cell_y = lax.axis_index("gy")
    owner_index = cell_x * count_y + cell_y
    flag_row = flags[0]
    ranking = (1 - flag_row) * blocks + jnp.arange(blocks, dtype=jnp.int32)
    chosen = jnp.argsort(ranking)[:CROSS_MAX]
    live_mask = jnp.take(flag_row, chosen).astype(jnp.float32).reshape(1, CROSS_MAX, 1)
    picked_pos = jnp.take(new_places, chosen, axis=1)
    picked_vel = jnp.take(new_speeds, chosen, axis=1)
    picked_ids = jnp.take(pixels.reshape(REPLICAS, blocks, width), chosen, axis=1)
    global_pos = jnp.stack(
        [
            (cell_x.astype(jnp.float32) + picked_pos[0]) / count_x,
            (cell_y.astype(jnp.float32) + picked_pos[1]) / count_y,
            picked_pos[2],
        ],
        axis=0,
    )
    shifted = global_pos[None] + offsets.astype(jnp.float32)[:, :, None, None]
    values = sky_terms(shifted, picked_vel, live_mask)
    send_values = jnp.transpose(values, (2, 0, 1, 3)).reshape(CROSS_MAX, 3, REPLICAS * width)
    send_ids = jnp.transpose(picked_ids, (1, 0, 2)).reshape(CROSS_MAX, REPLICAS * width)

    def in_strip(rows_global):
        return rows_global - owner_index * STRIP_ROWS

    maps = deposit(
        lax.all_gather(send_values, ("gx", "gy"), axis=0, tiled=True),
        lax.all_gather(send_ids, ("gx", "gy"), axis=0, tiled=True),
        in_strip,
        STRIP_ROWS,
    )
    return (new_places.reshape(3, blocks * width), new_speeds.reshape(3, blocks * width), maps)


def solution(mesh):
    in_specs = (
        P(None, ("gx", "gy")),
        P(None, ("gx", "gy")),
        P(("gx", "gy"), None),
        P(("gx", "gy"), None),
        P(),
        P(None, ("gx", "gy")),
    )
    out_specs = (P(None, ("gx", "gy")), P(None, ("gx", "gy")), P(("gx", "gy"), None))
    return jax.shard_map(
        on_device, mesh=mesh, in_specs=in_specs, out_specs=out_specs, check_vma=False
    )
```

profile of v0, /device:TPU:1, one launch (start us, length us, event | category | flops | bytes accessed | tf_op | source)
XLA Modules:
  0.0 567.8 jit_solution(4110377059390207661)
XLA Ops:
  7.2 0.0 copy-start
  7.2 0.0 all-gather.3.cloned.1.call-start
  7.2 0.7 compare_and_fusion
  7.9 0.7 compare_select_fusion
  8.6 0.8 bitcast_add_fusion
  9.4 1.4 gather_fusion.3
  10.7 0.6 gather_fusion.2
  11.3 0.1 select_bitcast_fusion
  11.4 1.5 collective-permute-start.7
  12.9 3.0 collective-permute-start.6
  15.9 4.5 collective-permute-start.5
  20.4 0.0 collective-permute-start.4
  20.4 0.9 collective-permute-start.2
  21.4 0.7 iota_add_fusion
  22.1 1.6 sort.17
  23.7 1.3 gather_fusion.1
  25.0 0.0 copy-done
  25.0 0.6 gather_fusion
  25.6 0.1 broadcast_select_fusion
  25.7 183.7 %all-gather = s32[128,5,384]{2,1,0:T(8,128)S(1)} all-gather(s32[1,5,384]{2,1,0:T(8,128)S(1)} %reshape.342), channel_id=1, replica_groups=mesh['gx'=8,'gy'=16] {'gx','gy'}, dimensions={0}, use_global_device_ids=true | all-gather | bytes 990720 | tf_op jit(solution)/shard_map/all_gather | solution.py:108
  209.4 0.2 reshape.286
  209.6 0.9 fusion.3
  210.4 0.7 convert_element_type.25
  211.2 0.0 collective-permute-done.4
  211.2 0.1 collective-permute-start
  211.3 0.0 collective-permute-done.5
  211.3 3.6 collective-permute-start.1
  214.9 0.0 collective-permute-done.6
  214.9 0.7 collective-permute-start.3
  215.6 0.0 collective-permute-done.7
  215.6 0.0 copy-start.3
  215.6 0.6 gather_fusion.5
  216.2 0.1 multiply_reduce_fusion
  216.3 0.0 collective-permute-done
  216.3 0.0 collective-permute-done.1
  216.4 0.0 collective-permute-done.2
  216.4 3.0 collective-permute-done.3
  219.4 0.0 copy-start.2
  219.4 0.6 gather_fusion.4
  220.0 0.1 select_bitcast_fusion.3
  220.1 0.1 fusion.7
  220.2 0.1 fusion.10
  220.3 0.6 reshape.287
  221.0 0.0 all-gather.3.cloned.1.call-update
  221.0 20.2 %fusion = bf16[245760,128]{0,1:T(8,128)(2,1)} fusion(s32[245760]{0:T(1024)S(1)} %get-tuple-element.62), kind=kLoop, calls=%fused_computation.7 | loop fusion | flops 62914560 | bytes 63897600 | tf_op jit(solution)/shard_map/convert_element_type | solution.py:41
  241.2 169.5 %all-gather.3.cloned.1.call-done = bf16[640,3,384]{2,1,0:T(4,128)(2,1)} async-done(((bf16[5,3,384]{2,1,0:T(4,128)(2,1)}), bf16[640,3,384]{2,1,0:T(4,128)(2,1)}) %all-gather.3.cloned.1.call-update) | async-done | bytes 1474576 | tf_op jit(solution)/shard_map/all_gather | solution.py:107
  410.7 81.4 %broadcast_multiply_fusion = bf16[245760,3,128]{0,2,1:T(8,128)(2,1)} fusion(bf16[245760,128]{0,1:T(8,128)(2,1)} %fusion, bf16[245760,3]{0,1:T(4,128)(2,1)} %bitcast.48), kind=kLoop, calls=%fused_computation.8 | loop fusion | flops 94371840 | bytes 253132800 | tf_op jit(solution)/shard_map/mul | solution.py:44
  492.1 0.0 copy-done.3
  492.2 0.0 copy-done.2
  492.2 0.0 copy-start.1
  492.2 68.8 %fusion.1 = f32[64,384]{1,0:T(8,128)} fusion(bf16[245760,384]{0,1:T(8,128)(2,1)} %bitcast.16, s32[245760]{0:T(1024)S(1)} %get-tuple-element.61), kind=kOutput, calls=%fused_computation.10 | convolution fusion | flops 12095324160 | bytes 189825024 | tf_op jit(solution)/shard_map/dot_general | solution.py:45
  560.9 0.0 copy-done.1
  (28 shorter events, 0.3 us)
Async XLA Ops:
  7.2 17.8 %copy-start = (s32[3,2560]{1,0:T(4,128)S(1)}, s32[3,2560]{1,0:T(4,128)}, u32[]{:S(2)}) copy-start(s32[3,2560]{1,0:T(4,128)} %param.23) | copy-start | bytes 92164
  7.2 403.5 %all-gather.3.cloned.1.call-start = ((), (), s32[]{:S(2)}) async-start(), calls=%async_computation | async-start | bytes 1981440 | tf_op jit(solution)/shard_map/all_gather | solution.py:107
  11.4 204.2 %collective-permute-start.7 = (f32[3,2,128]{2,0,1:T(4,128)S(1)}, f32[3,2,128]{2,0,1:T(4,128)S(1)}, u32[]{:S(2)}, u32[]{:S(2)}) collective-permute-start(f32[3,2,128]{2,0,1:T(4,128)S(1)} %get-tuple-element.63), channel_id=1, source_target_pairs={{1,0},{2,1},{3,2},{4,3},{5,4},{6,5},{7,6},{8,7},{9,8},{10,9},{11,1... | collective-permute-start | bytes 9224 | tf_op jit(solution)/shard_map/ppermute | solution.py:19
  12.9 202.0 %collective-permute-start.6 = (f32[3,2,128]{2,0,1:T(4,128)S(1)}, f32[3,2,128]{2,0,1:T(4,128)S(1)}, u32[]{:S(2)}, u32[]{:S(2)}) collective-permute-start(f32[3,2,128]{2,0,1:T(4,128)S(1)} %get-tuple-element.64), channel_id=1, source_target_pairs={{15,0},{0,1},{1,2},{2,3},{3,4},{4,5},{5,6},{6,7},{7,8},{8,9},{9,10... | collective-permute-start | bytes 9224 | tf_op jit(solution)/shard_map/ppermute | solution.py:19
  15.9 195.4 %collective-permute-start.5 = (f32[3,2,128]{2,0,1:T(4,128)S(1)}, f32[3,2,128]{2,0,1:T(4,128)S(1)}, u32[]{:S(2)}, u32[]{:S(2)}) collective-permute-start(f32[3,2,128]{2,0,1:T(4,128)S(1)} %get-tuple-element.65), channel_id=1, source_target_pairs={{16,0},{32,16},{48,32},{64,48},{80,64},{96,80},{112,96},{0,112},{1... | collective-permute-start | bytes 9224 | tf_op jit(solution)/shard_map/ppermute | solution.py:19
  20.4 190.9 %collective-permute-start.4 = (f32[3,2,128]{2,0,1:T(4,128)S(1)}, f32[3,2,128]{2,0,1:T(4,128)S(1)}, u32[]{:S(2)}, u32[]{:S(2)}) collective-permute-start(f32[3,2,128]{2,0,1:T(4,128)S(1)} %get-tuple-element.66), channel_id=1, source_target_pairs={{112,0},{0,16},{16,32},{32,48},{48,64},{64,80},{80,96},{96,112},{1... | collective-permute-start | bytes 9224 | tf_op jit(solution)/shard_map/ppermute | solution.py:19
  20.4 195.9 %collective-permute-start.2 = (f32[3,2,128]{2,0,1:T(4,128)S(1)}, f32[3,2,128]{2,0,1:T(4,128)S(1)}, u32[]{:S(2)}, u32[]{:S(2)}) collective-permute-start(f32[3,2,128]{2,0,1:T(4,128)S(1)} %scatter-add.16), channel_id=1, source_target_pairs={{15,0},{0,1},{1,2},{2,3},{3,4},{4,5},{5,6},{6,7},{7,8},{8,9},{9,10... | collective-permute-start | bytes 9224 | tf_op jit(solution)/shard_map/ppermute | solution.py:19
  211.2 5.1 collective-permute-start
  211.3 5.0 collective-permute-start.1
  214.9 4.5 collective-permute-start.3
  215.6 276.5 %copy-start.3 = (f32[3,20,128]{2,0,1:T(4,128)}, f32[3,20,128]{2,0,1:T(4,128)S(1)}, u32[]{:S(2)}) copy-start(f32[3,20,128]{2,0,1:T(4,128)S(1)} %constant_dynamic-update-slice_fusion.4) | copy-start | bytes 92164
  219.4 272.7 %copy-start.2 = (f32[3,20,128]{2,0,1:T(4,128)}, f32[3,20,128]{2,0,1:T(4,128)S(1)}, u32[]{:S(2)}) copy-start(f32[3,20,128]{2,0,1:T(4,128)S(1)} %constant_dynamic-update-slice_fusion) | copy-start | bytes 92164
  492.2 68.8 %copy-start.1 = (s32[3,2560]{1,0:T(4,128)S(1)}, s32[3,2560]{1,0:T(4,128)}, u32[]{:S(2)}) copy-start(s32[3,2560]{1,0:T(4,128)} %param.23) | copy-start | bytes 92164
Sparse Core Ops, SparseCore 0:
  221.1 189.5 all-gather.2
where the time goes:
time: 569 us; the launch traced here: 568 us
  blocking collectives  184 us (32%)
  waiting for transfers between devices  173 us (30%)
  other arithmetic  108 us (19%)
  matrix products  68.8 us (12%)
  starting transfers between devices  14.3 us (3%)
  between operations  14.3 us (3%)
  local copies, waits for them, and re-layouts  6.05 us (1%)
    all_gather x1, blocking collectives, on_device(): lax.all_gather(send_ids, ('gx', 'gy'), axis=0, tiled=True)  184 us
    all_gather x1, waiting for transfers between devices, on_device(): lax.all_gather(send_values, ('gx', 'gy'), axis=0, tiled=True)  170 us
    mul x1, other arithmetic, deposit(): flat_values[:, :, None] * lane_hits[:, None, :]  81.4 us
    dot_general x1, matrix products, deposit(): return jnp.dot(row_hits, spread, preferred_element_type=jnp.float32)  68.8 us
    convert_element_type x1, other arithmetic, deposit(): (lane_ids[:, None] == jnp.arange(lane_count, dtype=jnp.int32)[None, :]).a...  20.2 us
    ppermute x8, starting transfers between devices, passed_along(): return lax.ppermute(block, axis, route)  14.2 us
  transfers between devices with their start and end apart: 9, of which 2 were waited for; matrix products, arithmetic and copies ran while one was open for 5% of the time, Pallas kernels for 0%

commit v1 on v0

--- a/solution.py
+++ b/solution.py
@@ -27,22 +27,6 @@
     return jnp.stack(
         [weight * live_mask, weight * radial * live_mask, weight * energy[None] * live_mask], axis=0
     ).astype(jnp.bfloat16)
-
-
-def deposit(values, pixel_ids, target_of, row_total):
-    entries = values.shape[0] * values.shape[2]
-    flat_values = jnp.transpose(values, (0, 2, 1)).reshape(entries, 3)
-    flat_ids = pixel_ids.reshape(entries)
-    target = target_of(flat_ids // lane_count)
-    lane_ids = flat_ids % lane_count
-    row_hits = (target[None, :] == jnp.arange(row_total, dtype=jnp.int32)[:, None]).astype(
-        jnp.bfloat16
-    )
-    lane_hits = (lane_ids[:, None] == jnp.arange(lane_count, dtype=jnp.int32)[None, :]).astype(
-        jnp.bfloat16
-    )
-    spread = (flat_values[:, :, None] * lane_hits[:, None, :]).reshape(entries, 3 * lane_count)
-    return jnp.dot(row_hits, spread, preferred_element_type=jnp.float32)
 
 
 def on_device(positions, velocities, block_order, flags, offsets, pixels):
@@ -77,9 +61,9 @@
     )
     count_x = lax.axis_size("gx")
     count_y = lax.axis_size("gy")
+    devices = count_x * count_y
     cell_x = lax.axis_index("gx")
     cell_y = lax.axis_index("gy")
-    owner_index = cell_x * count_y + cell_y
     flag_row = flags[0]
     ranking = (1 - flag_row) * blocks + jnp.arange(blocks, dtype=jnp.int32)
     chosen = jnp.argsort(ranking)[:CROSS_MAX]
@@ -97,18 +81,36 @@
     )
     shifted = global_pos[None] + offsets.astype(jnp.float32)[:, :, None, None]
     values = sky_terms(shifted, picked_vel, live_mask)
-    send_values = jnp.transpose(values, (2, 0, 1, 3)).reshape(CROSS_MAX, 3, REPLICAS * width)
-    send_ids = jnp.transpose(picked_ids, (1, 0, 2)).reshape(CROSS_MAX, REPLICAS * width)
 
-    def in_strip(rows_global):
-        return rows_global - owner_index * STRIP_ROWS
+    strip_size = STRIP_ROWS * lane_count
+    per_replica = CROSS_MAX * width
+    ids = picked_ids.reshape(REPLICAS, per_replica)
+    dest = ids // strip_size
+    inside = ids % strip_size
+    order = jnp.arange(per_replica, dtype=jnp.int32)
+    same = (dest[:, :, None] == dest[:, None, :]) & (order[None, None, :] < order[None, :, None])
+    rank = jnp.sum(same.astype(jnp.int32), axis=2)
+    slots = REPLICAS * blocks
+    slot = dest * slots + jnp.arange(REPLICAS, dtype=jnp.int32)[:, None] * blocks + rank
+    fields = jnp.concatenate(
+        [
+            jnp.transpose(values.reshape(3, REPLICAS, per_replica), (1, 2, 0)),
+            (inside // lane_count).astype(jnp.bfloat16)[:, :, None],
+            (inside % lane_count).astype(jnp.bfloat16)[:, :, None],
+        ],
+        axis=2,
+    ).reshape(REPLICAS * per_replica, 5)
+    send = jnp.zeros((devices * slots, 5), jnp.bfloat16)
+    send = send.at[slot.reshape(-1)].set(fields, unique_indices=True, mode="promise_in_bounds")
+    send = send.reshape(devices, slots, 5)
+    got = lax.all_to_all(send, ("gx", "gy"), 0, 0, tiled=True).reshape(devices * slots, 5)
 
-    maps = deposit(
-        lax.all_gather(send_values, ("gx", "gy"), axis=0, tiled=True),
-        lax.all_gather(send_ids, ("gx", "gy"), axis=0, tiled=True),
-        in_strip,
-        STRIP_ROWS,
-    )
+    rows = got[:, 3].astype(jnp.int32)
+    lanes = got[:, 4].astype(jnp.int32)
+    row_hits = (rows[None, :] == jnp.arange(STRIP_ROWS, dtype=jnp.int32)[:, None]).astype(jnp.bfloat16)
+    lane_hits = (lanes[:, None] == jnp.arange(lane_count, dtype=jnp.int32)[None, :]).astype(jnp.bfloat16)
+    spread = (got[:, :3, None] * lane_hits[:, None, :]).reshape(devices * slots, 3 * lane_count)
+    maps = jnp.dot(row_hits, spread, preferred_element_type=jnp.float32)
     return (new_places.reshape(3, blocks * width), new_speeds.reshape(3, blocks * width), maps)
 
 

time: 569 us -> 65.8 us (0.12)
  waiting for transfers between devices: 173 us -> 2.86 us
  blocking collectives: 184 us -> 19.6 us
  other arithmetic: 108 us -> 7.5 us
  matrix products: 68.8 us -> 2.58 us
  between operations: 14.3 us -> 1.02 us
  local copies, waits for them, and re-layouts: 6.05 us -> 17 us
    all_gather x1 -> x0, blocking collectives: 184 us -> none  [on_device(): lax.all_gather(send_ids, ('gx', 'gy'), axis=0, tiled=True)]
    all_gather x1 -> x0, waiting for transfers between devices: 170 us -> none  [on_device(): lax.all_gather(send_values, ('gx', 'gy'), axis=0, tiled=True)]
    mul x1 -> x2, other arithmetic: 81.4 us -> 0.41 us  [the longest x1 0.41 us: on_device(): got[:, :3, None] * lane_hits[:, None, :]]
    dot_general x1, matrix products: 68.8 us -> 2.58 us  [on_device(): maps = jnp.dot(row_hits, spread, preferred_element_type=jnp.float32)]
    all_to_all x0 -> x1, blocking collectives: none -> 19.6 us  [on_device(): lax.all_to_all(send, ('gx', 'gy'), 0, 0, tiled=True)]
    convert_element_type x1 -> x4, other arithmetic: 20.2 us -> 0.59 us  [the longest x1 0.32 us: on_device(): (lanes[:, None] == jnp.arange(lane_count, dtype=jnp.int32)[None, :]).asty...]
    scatter x0 -> x2, local copies, waits for them, and re-layouts: none -> 9.78 us  [on_device(): send.at[slot.reshape(-1)]]
  transfers between devices with their start and end apart: 9 -> 8, of which waited for: 2 -> 1; matrix products, arithmetic and copies ran while one was open for 5% -> 11% of each run, Pallas kernels for 0% -> 0%
where the time goes in v1:
time: 65.8 us; the launch traced here: 65.5 us
  blocking collectives  19.6 us (30%)
  local copies, waits for them, and re-layouts  17 us (26%)
  starting transfers between devices  14.9 us (23%)
  other arithmetic  7.5 us (11%)
  waiting for transfers between devices  2.86 us (4%)
  matrix products  2.58 us (4%)
  between operations  1.02 us (2%)
    all_to_all x1, blocking collectives, on_device(): lax.all_to_all(send, ('gx', 'gy'), 0, 0, tiled=True)  19.6 us
    ppermute x8, starting transfers between devices, passed_along(): return lax.ppermute(block, axis, route)  14.9 us
    scatter x2, local copies, waits for them, and re-layouts, on_device(): send.at[slot.reshape(-1)]  9.78 us
    ppermute x8, waiting for transfers between devices, passed_along(): return lax.ppermute(block, axis, route)  2.86 us
    dot_general x1, matrix products, on_device(): maps = jnp.dot(row_hits, spread, preferred_element_type=jnp.float32)  2.58 us
    sort x1, other arithmetic, on_device(): chosen = jnp.argsort(ranking)[:CROSS_MAX]  1.61 us
    gather x1, local copies, waits for them, and re-layouts, on_device(): speeds = jnp.take(speeds, ordering, axis=1)  1.37 us
    reduce_sum x1, other arithmetic, on_device(): rank = jnp.sum(same.astype(jnp.int32), axis=2)  1.34 us
  transfers between devices with their start and end apart: 8, of which 1 were waited for; matrix products, arithmetic and copies ran while one was open for 11% of the time, Pallas kernels for 0%

profile of v1, /device:TPU:1, one launch (start us, length us, event | category | flops | bytes accessed | tf_op | source)
XLA Modules:
  0.0 65.5 jit_solution(11339426839900793238)
XLA Ops:
  0.6 0.0 copy-start
  0.6 0.0 copy-start.3
  0.7 0.7 %compare_and_fusion = pred[20]{0:T(512)(128)(4,1)S(1)} fusion(s32[1,20]{1,0:T(1,128)} %param.20), kind=kLoop, calls=%fused_computation.87 | loop fusion | flops 120 | bytes 100 | tf_op jit(solution)/shard_map/jit(_take)/and | solution.py:39
  1.3 0.7 %compare_select_fusion.9 = s32[20]{0:T(128)S(1)} fusion(s32[1,20]{1,0:T(1,128)} %param.20), kind=kLoop, calls=%fused_computation.80 | loop fusion | flops 60 | bytes 160 | tf_op jit(solution)/shard_map/jit(_take)/jit(_where)/select_n | solution.py:39
  2.0 0.8 %bitcast_add_fusion = f32[3,20,128]{2,0,1:T(4,128)S(1)} fusion(f32[3,2560]{1,0:T(4,128)} %param.18, f32[3,2560]{1,0:T(4,128)} %param.19), kind=kLoop, calls=%fused_computation.20 | loop fusion | flops 15360 | bytes 92160 | tf_op jit(solution)/shard_map/add | solution.py:37
  2.8 1.4 %gather_fusion.3 = f32[20,3,128]{2,1,0:T(4,128)S(1)} fusion(f32[3,20,128]{2,0,1:T(4,128)} %bitcast.75, s32[1024]{0:T(1024)S(1)} %pad_clamp_fusion.1), kind=kCustom, calls=%fused_computation.2.clone | custom fusion | bytes 61520 | tf_op jit(solution)/shard_map/jit(_take)/gather | solution.py:40
  4.2 0.6 gather_fusion.2
  4.8 0.1 select_bitcast_fusion
  4.9 1.5 %collective-permute-start.7 = (f32[3,2,128]{2,0,1:T(4,128)S(1)}, f32[3,2,128]{2,0,1:T(4,128)S(1)}, u32[]{:S(2)}, u32[]{:S(2)}) collective-permute-start(f32[3,2,128]{2,0,1:T(4,128)S(1)} %get-tuple-element.65), channel_id=1, source_target_pairs={{1,0},{2,1},{3,2},{4,3},{5,4},{6,5},{7,6},{8,7},{9,8},{10,9},{11,1... | collective-permute-start | bytes 9224 | tf_op jit(solution)/shard_map/ppermute | solution.py:19
  6.4 3.0 %collective-permute-start.6 = (f32[3,2,128]{2,0,1:T(4,128)S(1)}, f32[3,2,128]{2,0,1:T(4,128)S(1)}, u32[]{:S(2)}, u32[]{:S(2)}) collective-permute-start(f32[3,2,128]{2,0,1:T(4,128)S(1)} %get-tuple-element.66), channel_id=1, source_target_pairs={{15,0},{0,1},{1,2},{2,3},{3,4},{4,5},{5,6},{6,7},{7,8},{8,9},{9,10... | collective-permute-start | bytes 9224 | tf_op jit(solution)/shard_map/ppermute | solution.py:19
  9.3 4.5 %collective-permute-start.5 = (f32[3,2,128]{2,0,1:T(4,128)S(1)}, f32[3,2,128]{2,0,1:T(4,128)S(1)}, u32[]{:S(2)}, u32[]{:S(2)}) collective-permute-start(f32[3,2,128]{2,0,1:T(4,128)S(1)} %get-tuple-element.67), channel_id=1, source_target_pairs={{16,0},{32,16},{48,32},{64,48},{80,64},{96,80},{112,96},{0,112},{1... | collective-permute-start | bytes 9224 | tf_op jit(solution)/shard_map/ppermute | solution.py:19
  13.8 0.0 collective-permute-start.4
  13.9 0.9 %collective-permute-start.2 = (f32[3,2,128]{2,0,1:T(4,128)S(1)}, f32[3,2,128]{2,0,1:T(4,128)S(1)}, u32[]{:S(2)}, u32[]{:S(2)}) collective-permute-start(f32[3,2,128]{2,0,1:T(4,128)S(1)} %scatter-add.16), channel_id=1, source_target_pairs={{15,0},{0,1},{1,2},{2,3},{3,4},{4,5},{5,6},{6,7},{7,8},{8,9},{9,10... | collective-permute-start | bytes 9224 | tf_op jit(solution)/shard_map/ppermute | solution.py:19
  14.8 0.7 %iota_add_fusion = s32[20]{0:T(128)S(1)} fusion(s32[1,20]{1,0:T(1,128)} %param.21), kind=kLoop, calls=%fused_computation.96 | loop fusion | flops 60 | bytes 160 | tf_op jit(solution)/shard_map/add | solution.py:68
  15.5 1.6 %sort.17 = (s32[20]{0:T(128)}, s32[20]{0:T(128)S(1)}) sort(s32[20]{0:T(128)S(1)} %iota_add_fusion, s32[20]{0:T(128)S(1)} %iota.40), dimensions={0}, to_apply=%region_0.0 | sort | flops 100 | bytes 320 | tf_op jit(solution)/shard_map/jit(argsort)/sort | solution.py:69
  17.1 0.1 broadcast_bitcast_fusion.4
  17.2 0.1 iota_compare_fusion.3
  17.4 1.3 %gather_fusion.1 = s32[5]{0:T(128)S(1)} fusion(s32[20]{0:T(128)} %bitcast.71, s32[1024]{0:T(1024)S(1)} %pad_clamp_fusion), kind=kCustom, calls=%fused_computation.5 | custom fusion | bytes 60 | tf_op jit(solution)/shard_map/jit(_take)/gather | solution.py:70
  18.7 0.1 broadcast_bitcast_fusion
  18.8 0.0 copy-done
  18.8 0.6 gather_fusion
  19.4 1.3 %convert_reduce_fusion = s32[3,640]{1,0:T(4,128)S(1)} fusion(s32[3,640]{1,0:T(4,128)S(1)} %add_select_fusion, pred[640,640]{1,0:T(8,128)(4,1)S(1)} %iota_compare_fusion.3), kind=kLoop, calls=%fused_computation.7 | loop fusion | flops 4913280 | bytes 424960 | tf_op jit(solution)/shard_map/reduce_sum | solution.py:92
  20.8 0.1 and_select_fusion.2
  21.0 0.1 broadcast_bitcast_fusion.3
  21.1 0.0 copy-done.3
  21.2 0.0 collective-permute-done.4
  21.2 0.1 collective-permute-start
  21.3 0.0 collective-permute-done.5
  21.3 3.6 %collective-permute-start.1 = (f32[3,2,128]{2,0,1:T(4,128)S(1)}, f32[3,2,128]{2,0,1:T(4,128)S(1)}, u32[]{:S(2)}, u32[]{:S(2)}) collective-permute-start(f32[3,2,128]{2,0,1:T(4,128)S(1)} %scatter-add.15), channel_id=1, source_target_pairs={{16,0},{32,16},{48,32},{64,48},{80,64},{96,80},{112,96},{0,112},{1... | collective-permute-start | bytes 9224 | tf_op jit(solution)/shard_map/ppermute | solution.py:19
  24.8 0.0 collective-permute-done.6
  24.8 1.4 %collective-permute-start.3 = (f32[3,2,128]{2,0,1:T(4,128)S(1)}, f32[3,2,128]{2,0,1:T(4,128)S(1)}, u32[]{:S(2)}, u32[]{:S(2)}) collective-permute-start(f32[3,2,128]{2,0,1:T(4,128)S(1)} %scatter-add.19), channel_id=1, source_target_pairs={{1,0},{2,1},{3,2},{4,3},{5,4},{6,5},{7,6},{8,7},{9,8},{10,9},{11,1... | collective-permute-start | bytes 9224 | tf_op jit(solution)/shard_map/ppermute | solution.py:19
  26.3 0.0 collective-permute-done.7
  26.3 0.0 copy-start.2
  26.3 0.0 collective-permute-done
  26.3 0.0 collective-permute-done.1
  26.3 0.0 collective-permute-done.2
  26.3 0.6 gather_fusion.5
  26.9 2.8 %collective-permute-done.3 = f32[3,2,128]{2,0,1:T(4,128)S(1)} collective-permute-done((f32[3,2,128]{2,0,1:T(4,128)S(1)}, f32[3,2,128]{2,0,1:T(4,128)S(1)}, u32[]{:S(2)}, u32[]{:S(2)}) %collective-permute-start.3) | collective-permute-done | bytes 3104 | tf_op jit(solution)/shard_map/ppermute | solution.py:19
  29.8 0.0 copy-start.1
  29.8 0.6 gather_fusion.4
  30.3 0.1 select_bitcast_fusion.3
  30.4 0.1 multiply_reduce_fusion
  30.5 0.1 fusion.6
  30.8 0.3 copy.29
  31.1 8.9 %scatter_custom_fusion = bf16[7680,5]{1,0:T(8,128)(2,1)S(1)} fusion(s32[1920]{0:T(1024)S(1)} %get-tuple-element.86, bf16[1920,5]{1,0:T(8,128)(2,1)S(1)} %copy.29, bf16[]{:T(256)} %constant.206.clone.1), kind=kCustom, calls=%fused_computation.15 | custom fusion | bytes 76802 | tf_op jit(solution)/shard_map/scatter | solution.py:104
  40.0 0.9 %copy.30 = bf16[7680,5]{0,1:T(8,128)(2,1)S(1)} copy(bf16[7680,5]{1,0:T(8,128)(2,1)S(1)} %scatter_custom_fusion) | data formatting | bytes 153600 | tf_op jit(solution)/shard_map/scatter | solution.py:104
  40.9 0.0 copy-done.2
  40.9 0.0 copy-done.1
  40.9 0.5 reshape.644
  41.4 0.1 copy.39
  41.5 0.2 reshape.723
  41.7 19.6 %all_to_all.5 = bf16[128,2,150]{2,1,0:T(2,128)(2,1)S(1)} all-to-all(bf16[128,2,150]{2,1,0:T(2,128)(2,1)S(1)} %reshape.723), channel_id=1, replica_groups=mesh['gx'=8,'gy'=16] {'gx','gy'}, dimensions={0} | all-to-all | bytes 153600 | tf_op jit(solution)/shard_map/all_to_all | solution.py:106
  61.3 0.2 reshape.724
  61.6 0.3 reshape.645
  62.0 0.2 fusion.8
  62.2 0.3 fusion
  62.5 0.4 broadcast_multiply_fusion
  62.9 2.6 %fusion.1 = f32[64,384]{1,0:T(8,128)} fusion(bf16[7680,384]{0,1:T(8,128)(2,1)S(1)} %bitcast.72, s32[7680]{0:T(1024)S(1)} %get-tuple-element.55), kind=kOutput, calls=%fused_computation.12 | convolution fusion | flops 377978880 | bytes 6027264 | tf_op jit(solution)/shard_map/dot_general | solution.py:113
  (46 shorter events, 0.6 us)
Async XLA Ops:
  0.6 18.2 %copy-start = (s32[3,2560]{1,0:T(4,128)S(1)}, s32[3,2560]{1,0:T(4,128)}, u32[]{:S(2)}) copy-start(s32[3,2560]{1,0:T(4,128)} %param.23) | copy-start | bytes 92164
  0.6 20.4 %copy-start.3 = (s32[3,3]{1,0:T(4,128)S(1)}, s32[3,3]{1,0:T(4,128)}, u32[]{:S(2)}) copy-start(s32[3,3]{1,0:T(4,128)} %param.22) | copy-start | bytes 112
  4.9 21.4 %collective-permute-start.7 = (f32[3,2,128]{2,0,1:T(4,128)S(1)}, f32[3,2,128]{2,0,1:T(4,128)S(1)}, u32[]{:S(2)}, u32[]{:S(2)}) collective-permute-start(f32[3,2,128]{2,0,1:T(4,128)S(1)} %get-tuple-element.65), channel_id=1, source_target_pairs={{1,0},{2,1},{3,2},{4,3},{5,4},{6,5},{7,6},{8,7},{9,8},{10,9},{11,1... | collective-permute-start | bytes 9224 | tf_op jit(solution)/shard_map/ppermute | solution.py:19
  6.4 18.4 %collective-permute-start.6 = (f32[3,2,128]{2,0,1:T(4,128)S(1)}, f32[3,2,128]{2,0,1:T(4,128)S(1)}, u32[]{:S(2)}, u32[]{:S(2)}) collective-permute-start(f32[3,2,128]{2,0,1:T(4,128)S(1)} %get-tuple-element.66), channel_id=1, source_target_pairs={{15,0},{0,1},{1,2},{2,3},{3,4},{4,5},{5,6},{6,7},{7,8},{8,9},{9,10... | collective-permute-start | bytes 9224 | tf_op jit(solution)/shard_map/ppermute | solution.py:19
  9.3 11.9 %collective-permute-start.5 = (f32[3,2,128]{2,0,1:T(4,128)S(1)}, f32[3,2,128]{2,0,1:T(4,128)S(1)}, u32[]{:S(2)}, u32[]{:S(2)}) collective-permute-start(f32[3,2,128]{2,0,1:T(4,128)S(1)} %get-tuple-element.67), channel_id=1, source_target_pairs={{16,0},{32,16},{48,32},{64,48},{80,64},{96,80},{112,96},{0,112},{1... | collective-permute-start | bytes 9224 | tf_op jit(solution)/shard_map/ppermute | solution.py:19
  13.8 7.4 %collective-permute-start.4 = (f32[3,2,128]{2,0,1:T(4,128)S(1)}, f32[3,2,128]{2,0,1:T(4,128)S(1)}, u32[]{:S(2)}, u32[]{:S(2)}) collective-permute-start(f32[3,2,128]{2,0,1:T(4,128)S(1)} %get-tuple-element.68), channel_id=1, source_target_pairs={{112,0},{0,16},{16,32},{32,48},{48,64},{64,80},{80,96},{96,112},{1... | collective-permute-start | bytes 9224 | tf_op jit(solution)/shard_map/ppermute | solution.py:19
  13.9 12.4 %collective-permute-start.2 = (f32[3,2,128]{2,0,1:T(4,128)S(1)}, f32[3,2,128]{2,0,1:T(4,128)S(1)}, u32[]{:S(2)}, u32[]{:S(2)}) collective-permute-start(f32[3,2,128]{2,0,1:T(4,128)S(1)} %scatter-add.16), channel_id=1, source_target_pairs={{15,0},{0,1},{1,2},{2,3},{3,4},{4,5},{5,6},{6,7},{7,8},{8,9},{9,10... | collective-permute-start | bytes 9224 | tf_op jit(solution)/shard_map/ppermute | solution.py:19
  21.2 5.1 %collective-permute-start = (f32[3,2,128]{2,0,1:T(4,128)S(1)}, f32[3,2,128]{2,0,1:T(4,128)S(1)}, u32[]{:S(2)}, u32[]{:S(2)}) collective-permute-start(f32[3,2,128]{2,0,1:T(4,128)S(1)} %scatter-add.14), channel_id=1, source_target_pairs={{112,0},{0,16},{16,32},{32,48},{48,64},{64,80},{80,96},{96,112},{1... | collective-permute-start | bytes 9224 | tf_op jit(solution)/shard_map/ppermute | solution.py:19
  21.3 5.0 %collective-permute-start.1 = (f32[3,2,128]{2,0,1:T(4,128)S(1)}, f32[3,2,128]{2,0,1:T(4,128)S(1)}, u32[]{:S(2)}, u32[]{:S(2)}) collective-permute-start(f32[3,2,128]{2,0,1:T(4,128)S(1)} %scatter-add.15), channel_id=1, source_target_pairs={{16,0},{32,16},{48,32},{64,48},{80,64},{96,80},{112,96},{0,112},{1... | collective-permute-start | bytes 9224 | tf_op jit(solution)/shard_map/ppermute | solution.py:19
  24.8 4.9 %collective-permute-start.3 = (f32[3,2,128]{2,0,1:T(4,128)S(1)}, f32[3,2,128]{2,0,1:T(4,128)S(1)}, u32[]{:S(2)}, u32[]{:S(2)}) collective-permute-start(f32[3,2,128]{2,0,1:T(4,128)S(1)} %scatter-add.19), channel_id=1, source_target_pairs={{1,0},{2,1},{3,2},{4,3},{5,4},{6,5},{7,6},{8,7},{9,8},{10,9},{11,1... | collective-permute-start | bytes 9224 | tf_op jit(solution)/shard_map/ppermute | solution.py:19
  26.3 14.6 %copy-start.2 = (f32[3,20,128]{2,0,1:T(4,128)}, f32[3,20,128]{2,0,1:T(4,128)S(1)}, u32[]{:S(2)}) copy-start(f32[3,20,128]{2,0,1:T(4,128)S(1)} %constant_dynamic-update-slice_fusion.4) | copy-start | bytes 92164
  29.8 11.2 %copy-start.1 = (f32[3,20,128]{2,0,1:T(4,128)}, f32[3,20,128]{2,0,1:T(4,128)S(1)}, u32[]{:S(2)}) copy-start(f32[3,20,128]{2,0,1:T(4,128)S(1)} %constant_dynamic-update-slice_fusion) | copy-start | bytes 92164

commit v2 on v1

--- a/solution.py
+++ b/solution.py
@@ -44,15 +44,17 @@
         moved_pos = places[:, first_block : first_block + MOVERS].at[component].add(sign_step)
         return (moved_pos, speeds[:, first_block : first_block + MOVERS])
 
-    east_pos, east_vel = leaving(0, 0, -1.0)
-    from_west = passed_along((east_pos, east_vel), "gx", 1)
-    west_pos, west_vel = leaving(1, 0, 1.0)
-    from_east = passed_along((west_pos, west_vel), "gx", -1)
-    north_pos, north_vel = leaving(2, 1, -1.0)
-    from_south = passed_along((north_pos, north_vel), "gy", 1)
-    south_pos, south_vel = leaving(3, 1, 1.0)
-    from_north = passed_along((south_pos, south_vel), "gy", -1)
-    arrived = (from_west, from_east, from_south, from_north)
+    def moved(which_set, component, sign_step, axis, distance):
+        pos, vel = leaving(which_set, component, sign_step)
+        got = passed_along(jnp.concatenate([pos, vel], axis=0), axis, distance)
+        return got[:3], got[3:]
+
+    arrived = (
+        moved(0, 0, -1.0, "gx", 1),
+        moved(1, 0, 1.0, "gx", -1),
+        moved(2, 1, -1.0, "gy", 1),
+        moved(3, 1, 1.0, "gy", -1),
+    )
     new_places = jnp.concatenate(
         [places[:, 4 * MOVERS :]] + [received[0] for received in arrived], axis=1
     )
@@ -91,7 +93,6 @@
     same = (dest[:, :, None] == dest[:, None, :]) & (order[None, None, :] < order[None, :, None])
     rank = jnp.sum(same.astype(jnp.int32), axis=2)
     slots = REPLICAS * blocks
-    slot = dest * slots + jnp.arange(REPLICAS, dtype=jnp.int32)[:, None] * blocks + rank
     fields = jnp.concatenate(
         [
             jnp.transpose(values.reshape(3, REPLICAS, per_replica), (1, 2, 0)),
@@ -99,10 +100,14 @@
             (inside % lane_count).astype(jnp.bfloat16)[:, :, None],
         ],
         axis=2,
-    ).reshape(REPLICAS * per_replica, 5)
-    send = jnp.zeros((devices * slots, 5), jnp.bfloat16)
-    send = send.at[slot.reshape(-1)].set(fields, unique_indices=True, mode="promise_in_bounds")
-    send = send.reshape(devices, slots, 5)
+    )
+    dest_hits = (dest[:, :, None] == jnp.arange(devices, dtype=jnp.int32)).astype(jnp.bfloat16)
+    rank_hits = (rank[:, :, None] == jnp.arange(blocks, dtype=jnp.int32)).astype(jnp.bfloat16)
+    placed = (rank_hits[:, :, :, None] * fields[:, :, None, :]).reshape(REPLICAS, per_replica, blocks * 5)
+    send = lax.dot_general(
+        dest_hits, placed, (((1,), (1,)), ((0,), (0,))), preferred_element_type=jnp.float32
+    ).astype(jnp.bfloat16)
+    send = jnp.transpose(send, (1, 0, 2)).reshape(devices, slots, 5)
     got = lax.all_to_all(send, ("gx", "gy"), 0, 0, tiled=True).reshape(devices * slots, 5)
 
     rows = got[:, 3].astype(jnp.int32)

time: 65.8 us -> 49.2 us (0.75)
  local copies, waits for them, and re-layouts: 17 us -> 6.57 us
  starting transfers between devices: 14.9 us -> 9.99 us
  waiting for transfers between devices: 2.86 us -> 0.01 us
  other arithmetic: 7.5 us -> 8.24 us
    scatter x2 -> x0, local copies, waits for them, and re-layouts: 9.78 us -> none  [on_device(): send.at[slot.reshape(-1)]]
    ppermute x8 -> x4, starting transfers between devices: 14.9 us -> 9.99 us  [passed_along(): return lax.ppermute(block, axis, route)]
    ppermute x8 -> x4, waiting for transfers between devices: 2.86 us -> 0.01 us  [passed_along(): return lax.ppermute(block, axis, route)]
    convert_element_type x1, other arithmetic: 0.01 us -> 0.68 us  [on_device(): shifted = global_pos[None] + offsets.astype(jnp.float32)[:, :, None, None]]
  transfers between devices with their start and end apart: 8 -> 4, of which waited for: 1 -> 0; matrix products, arithmetic and copies ran while one was open for 11% -> 14% of each run, Pallas kernels for 0% -> 0%
where the time goes in v2:
time: 49.2 us; the launch traced here: 48.9 us
  blocking collectives  20 us (41%)
  starting transfers between devices  9.99 us (20%)
  other arithmetic  8.24 us (17%)
  local copies, waits for them, and re-layouts  6.57 us (13%)
  matrix products  3.09 us (6%)
  between operations  0.95 us (2%)
    all_to_all x1, blocking collectives, on_device(): lax.all_to_all(send, ('gx', 'gy'), 0, 0, tiled=True)  20 us
    ppermute x4, starting transfers between devices, passed_along(): return lax.ppermute(block, axis, route)  9.99 us
    dot_general x1, matrix products, on_device(): maps = jnp.dot(row_hits, spread, preferred_element_type=jnp.float32)  2.58 us
    sort x1, other arithmetic, on_device(): chosen = jnp.argsort(ranking)[:CROSS_MAX]  1.61 us
    gather x1, local copies, waits for them, and re-layouts, on_device(): speeds = jnp.take(speeds, ordering, axis=1)  1.37 us
    reduce_sum x1, other arithmetic, on_device(): rank = jnp.sum(same.astype(jnp.int32), axis=2)  1.34 us
    gather x1, local copies, waits for them, and re-layouts, on_device(): jnp.take(flag_row, chosen).astype(jnp.float32).reshape(1, CROSS_MAX, 1)  1.3 us
  transfers between devices with their start and end apart: 4, of which 0 were waited for; matrix products, arithmetic and copies ran while one was open for 14% of the time, Pallas kernels for 0%

profile of v2, /device:TPU:1, one launch (start us, length us, event | category | flops | bytes accessed | tf_op | source)
XLA Modules:
  0.0 48.9 jit_solution(12999348867190323960)
XLA Ops:
  0.6 0.0 copy-start
  0.6 0.7 %compare_and_fusion = pred[20]{0:T(512)(128)(4,1)S(1)} fusion(s32[1,20]{1,0:T(1,128)} %param.20), kind=kLoop, calls=%fused_computation.90 | loop fusion | flops 120 | bytes 100 | tf_op jit(solution)/shard_map/jit(_take)/and | solution.py:39
  1.3 0.7 %compare_select_fusion = s32[20]{0:T(128)S(1)} fusion(s32[1,20]{1,0:T(1,128)} %param.20), kind=kLoop, calls=%fused_computation.83 | loop fusion | flops 60 | bytes 160 | tf_op jit(solution)/shard_map/jit(_take)/jit(_where)/select_n | solution.py:39
  2.0 0.8 %bitcast_add_fusion = f32[3,20,128]{2,0,1:T(4,128)S(1)} fusion(f32[3,2560]{1,0:T(4,128)} %param.18, f32[3,2560]{1,0:T(4,128)} %param.19), kind=kLoop, calls=%fused_computation.23 | loop fusion | flops 15360 | bytes 92160 | tf_op jit(solution)/shard_map/add | solution.py:37
  2.8 1.4 %gather_fusion.3 = f32[20,3,128]{2,1,0:T(4,128)S(1)} fusion(f32[3,20,128]{2,0,1:T(4,128)} %bitcast.62, s32[1024]{0:T(1024)S(1)} %pad_clamp_fusion.1), kind=kCustom, calls=%fused_computation.2.clone | custom fusion | bytes 61520 | tf_op jit(solution)/shard_map/jit(_take)/gather | solution.py:40
  4.2 0.6 %gather_fusion.2 = f32[20,3,128]{2,1,0:T(4,128)S(1)} fusion(f32[3,20,128]{2,0,1:T(4,128)S(1)} %bitcast_add_fusion, s32[1024]{0:T(1024)S(1)} %pad_clamp_fusion.1), kind=kCustom, calls=%fused_computation.clone | custom fusion | bytes 61520 | tf_op jit(solution)/shard_map/jit(_take)/gather | solution.py:39
  4.8 0.1 select_bitcast_fusion
  4.9 1.5 %collective-permute-start.3 = (f32[6,2,128]{2,0,1:T(8,128)S(1)}, f32[6,2,128]{2,0,1:T(8,128)S(1)}, u32[]{:S(2)}, u32[]{:S(2)}) collective-permute-start(f32[6,2,128]{2,0,1:T(8,128)S(1)} %pad_maximum_fusion.5), channel_id=1, source_target_pairs={{1,0},{2,1},{3,2},{4,3},{5,4},{6,5},{7,6},{8,7},{9,8},{10,9},{11,1... | collective-permute-start | bytes 18440 | tf_op jit(solution)/shard_map/ppermute | solution.py:19
  6.5 4.9 %collective-permute-start.1 = (f32[6,2,128]{2,0,1:T(8,128)S(1)}, f32[6,2,128]{2,0,1:T(8,128)S(1)}, u32[]{:S(2)}, u32[]{:S(2)}) collective-permute-start(f32[6,2,128]{2,0,1:T(8,128)S(1)} %pad_maximum_fusion.3), channel_id=1, source_target_pairs={{16,0},{32,16},{48,32},{64,48},{80,64},{96,80},{112,96},{0,112},{1... | collective-permute-start | bytes 18440 | tf_op jit(solution)/shard_map/ppermute | solution.py:19
  11.4 0.1 collective-permute-start
  11.6 3.5 %collective-permute-start.2 = (f32[6,2,128]{2,0,1:T(8,128)S(1)}, f32[6,2,128]{2,0,1:T(8,128)S(1)}, u32[]{:S(2)}, u32[]{:S(2)}) collective-permute-start(f32[6,2,128]{2,0,1:T(8,128)S(1)} %pad_maximum_fusion.4), channel_id=1, source_target_pairs={{15,0},{0,1},{1,2},{2,3},{3,4},{4,5},{5,6},{6,7},{7,8},{8,9},{9,10... | collective-permute-start | bytes 18440 | tf_op jit(solution)/shard_map/ppermute | solution.py:19
  15.1 0.7 %iota_add_fusion = s32[20]{0:T(128)S(1)} fusion(s32[1,20]{1,0:T(1,128)} %param.21), kind=kLoop, calls=%fused_computation.98 | loop fusion | flops 60 | bytes 160 | tf_op jit(solution)/shard_map/add | solution.py:70
  15.7 1.6 %sort.17 = (s32[20]{0:T(128)}, s32[20]{0:T(128)S(1)}) sort(s32[20]{0:T(128)S(1)} %iota_add_fusion, s32[20]{0:T(128)S(1)} %iota.44), dimensions={0}, to_apply=%region_0.0 | sort | flops 100 | bytes 320 | tf_op jit(solution)/shard_map/jit(argsort)/sort | solution.py:71
  17.4 0.1 broadcast_bitcast_fusion.1
  17.4 0.0 copy-done
  17.4 0.6 %gather_fusion = s32[5,3,128]{2,1,0:T(4,128)S(1)} fusion(s32[3,20,128]{2,0,1:T(4,128)S(1)} %bitcast.57, s32[1024]{0:T(1024)S(1)} %pad_clamp_fusion), kind=kCustom, calls=%fused_computation.4 | custom fusion | bytes 15380 | tf_op jit(solution)/shard_map/jit(_take)/gather | solution.py:75
  18.1 0.1 iota_compare_fusion.3
  18.2 1.3 %gather_fusion.1 = s32[5]{0:T(128)S(1)} fusion(s32[20]{0:T(128)} %bitcast.58, s32[1024]{0:T(1024)S(1)} %pad_clamp_fusion), kind=kCustom, calls=%fused_computation.5 | custom fusion | bytes 60 | tf_op jit(solution)/shard_map/jit(_take)/gather | solution.py:72
  19.6 1.3 %convert_reduce_fusion = s32[3,640]{1,0:T(4,128)S(1)} fusion(s32[3,640]{1,0:T(4,128)S(1)} %add_select_fusion.3, pred[640,640]{1,0:T(8,128)(4,1)S(1)} %iota_compare_fusion.3), kind=kLoop, calls=%fused_computation.6 | loop fusion | flops 4913280 | bytes 424960 | tf_op jit(solution)/shard_map/reduce_sum | solution.py:94
  20.9 0.1 broadcast_bitcast_fusion
  21.0 0.7 %convert_element_type.78 = f32[3,3]{1,0:T(4,128)S(1)} convert(s32[3,3]{1,0:T(4,128)} %param.22) | non-fusion elementwise | flops 9 | bytes 72 | tf_op jit(solution)/shard_map/convert_element_type | solution.py:84
  21.7 0.0 collective-permute-done
  21.7 0.0 collective-permute-done.1
  21.7 0.0 collective-permute-done.2
  21.7 0.0 collective-permute-done.3
  21.8 0.0 copy-start.1
  21.8 0.0 copy-start.2
  21.8 0.6 %gather_fusion.5 = f32[5,3,128]{2,1,0:T(4,128)S(1)} fusion(f32[3,20,128]{2,0,1:T(4,128)S(1)} %get-tuple-element.85, s32[1024]{0:T(1024)S(1)} %pad_clamp_fusion), kind=kCustom, calls=%fused_computation.3.clone | custom fusion | bytes 15380 | tf_op jit(solution)/shard_map/jit(_take)/gather | solution.py:74
  22.4 0.1 multiply_reduce_fusion
  22.5 0.6 %gather_fusion.4 = f32[5,3,128]{2,1,0:T(4,128)S(1)} fusion(f32[3,20,128]{2,0,1:T(4,128)S(1)} %get-tuple-element.86, s32[1024]{0:T(1024)S(1)} %pad_clamp_fusion), kind=kCustom, calls=%fused_computation.1.clone | custom fusion | bytes 15380 | tf_op jit(solution)/shard_map/jit(_take)/gather | solution.py:73
  23.0 0.1 select_bitcast_fusion.3
  23.2 0.1 fusion.7
  23.4 0.1 broadcast_multiply_fusion.1
  23.5 0.2 mul.151
  23.7 0.5 %fusion.2 = bf16[128,3,100]{0,2,1:T(8,128)(2,1)S(1)} fusion(bf16[3,640,100]{1,2,0:T(8,128)(2,1)S(1)} %mul.151, s32[3,640]{1,0:T(4,128)S(1)} %add_select_fusion.3), kind=kOutput, calls=%fused_computation.14 | convolution fusion | flops 49436160 | bytes 468480 | tf_op jit(solution)/shard_map/dot_general | solution.py:107
  24.3 0.2 copy.26
  24.5 0.2 reshape.639
  24.7 20.0 %all_to_all.5 = bf16[128,2,150]{2,1,0:T(2,128)(2,1)S(1)} all-to-all(bf16[128,2,150]{2,1,0:T(2,128)(2,1)S(1)} %reshape.639), channel_id=1, replica_groups=mesh['gx'=8,'gy'=16] {'gx','gy'}, dimensions={0} | all-to-all | bytes 153600 | tf_op jit(solution)/shard_map/all_to_all | solution.py:111
  44.7 0.2 reshape.640
  44.9 0.3 reshape.572
  45.3 0.2 fusion.9
  45.5 0.3 fusion
  45.8 0.4 broadcast_multiply_fusion
  46.3 0.0 copy-done.1
  46.3 0.0 copy-done.2
  46.3 2.6 %fusion.1 = f32[64,384]{1,0:T(8,128)} fusion(bf16[7680,384]{0,1:T(8,128)(2,1)S(1)} %bitcast.59, s32[7680]{0:T(1024)S(1)} %get-tuple-element.55), kind=kOutput, calls=%fused_computation.11 | convolution fusion | flops 377978880 | bytes 6027264 | tf_op jit(solution)/shard_map/dot_general | solution.py:118
  (37 shorter events, 0.6 us)
Async XLA Ops:
  0.6 16.8 %copy-start = (s32[3,2560]{1,0:T(4,128)S(1)}, s32[3,2560]{1,0:T(4,128)}, u32[]{:S(2)}) copy-start(s32[3,2560]{1,0:T(4,128)} %param.23) | copy-start | bytes 92164
  4.9 16.8 %collective-permute-start.3 = (f32[6,2,128]{2,0,1:T(8,128)S(1)}, f32[6,2,128]{2,0,1:T(8,128)S(1)}, u32[]{:S(2)}, u32[]{:S(2)}) collective-permute-start(f32[6,2,128]{2,0,1:T(8,128)S(1)} %pad_maximum_fusion.5), channel_id=1, source_target_pairs={{1,0},{2,1},{3,2},{4,3},{5,4},{6,5},{7,6},{8,7},{9,8},{10,9},{11,1... | collective-permute-start | bytes 18440 | tf_op jit(solution)/shard_map/ppermute | solution.py:19
  6.5 15.2 %collective-permute-start.1 = (f32[6,2,128]{2,0,1:T(8,128)S(1)}, f32[6,2,128]{2,0,1:T(8,128)S(1)}, u32[]{:S(2)}, u32[]{:S(2)}) collective-permute-start(f32[6,2,128]{2,0,1:T(8,128)S(1)} %pad_maximum_fusion.3), channel_id=1, source_target_pairs={{16,0},{32,16},{48,32},{64,48},{80,64},{96,80},{112,96},{0,112},{1... | collective-permute-start | bytes 18440 | tf_op jit(solution)/shard_map/ppermute | solution.py:19
  11.4 10.3 %collective-permute-start = (f32[6,2,128]{2,0,1:T(8,128)S(1)}, f32[6,2,128]{2,0,1:T(8,128)S(1)}, u32[]{:S(2)}, u32[]{:S(2)}) collective-permute-start(f32[6,2,128]{2,0,1:T(8,128)S(1)} %pad_maximum_fusion.2), channel_id=1, source_target_pairs={{112,0},{0,16},{16,32},{32,48},{48,64},{64,80},{80,96},{96,112},{1... | collective-permute-start | bytes 18440 | tf_op jit(solution)/shard_map/ppermute | solution.py:19
  11.6 10.2 %collective-permute-start.2 = (f32[6,2,128]{2,0,1:T(8,128)S(1)}, f32[6,2,128]{2,0,1:T(8,128)S(1)}, u32[]{:S(2)}, u32[]{:S(2)}) collective-permute-start(f32[6,2,128]{2,0,1:T(8,128)S(1)} %pad_maximum_fusion.4), channel_id=1, source_target_pairs={{15,0},{0,1},{1,2},{2,3},{3,4},{4,5},{5,6},{6,7},{7,8},{8,9},{9,10... | collective-permute-start | bytes 18440 | tf_op jit(solution)/shard_map/ppermute | solution.py:19
  21.8 24.5 %copy-start.1 = (f32[3,20,128]{2,0,1:T(4,128)}, f32[3,20,128]{2,0,1:T(4,128)S(1)}, u32[]{:S(2)}) copy-start(f32[3,20,128]{2,0,1:T(4,128)S(1)} %get-tuple-element.85) | copy-start | bytes 92164
  21.8 24.5 %copy-start.2 = (f32[3,20,128]{2,0,1:T(4,128)}, f32[3,20,128]{2,0,1:T(4,128)S(1)}, u32[]{:S(2)}) copy-start(f32[3,20,128]{2,0,1:T(4,128)S(1)} %get-tuple-element.86) | copy-start | bytes 92164

commit v3 on v2

--- a/solution.py
+++ b/solution.py
@@ -1,6 +1,10 @@
+import functools
+
 import jax
 import jax.numpy as jnp
 from jax import lax
+from jax.experimental import pallas as pl
+from jax.experimental.pallas import tpu as pltpu
 from jax.sharding import PartitionSpec as P
 
 MOVERS = 2
@@ -11,6 +15,80 @@
 
 time_step = 0.05
 lane_count = 128
+FIELDS = 8
+MESH = pl.DeviceIdType.MESH
+
+
+def exchange_kernel(count_y, send_ref, maps_ref, recv, send_sem, recv_sem):
+    devices = send_ref.shape[0]
+    rows = maps_ref.shape[0]
+    me = lax.axis_index("gx") * count_y + lax.axis_index("gy")
+
+    def peer(offset):
+        other = lax.rem(me + offset, devices)
+        return other, (other // count_y, other % count_y)
+
+    barrier = pltpu.get_barrier_semaphore()
+
+    def greet(offset, carry):
+        pl.semaphore_signal(barrier, 1, device_id=peer(offset)[1], device_id_type=MESH)
+        return carry
+
+    lax.fori_loop(1, devices, greet, 0)
+    pl.semaphore_wait(barrier, devices - 1)
+    pltpu.make_async_copy(send_ref.at[me], recv.at[me], recv_sem).start()
+
+    def post(offset, carry):
+        other, where = peer(offset)
+        pltpu.make_async_remote_copy(
+            src_ref=send_ref.at[other],
+            dst_ref=recv.at[me],
+            send_sem=send_sem,
+            recv_sem=recv_sem,
+            device_id=where,
+            device_id_type=MESH,
+        ).start()
+        return carry
+
+    lax.fori_loop(1, devices, post, 0)
+    pltpu.make_async_copy(
+        send_ref.at[pl.ds(0, devices - 1)], recv.at[pl.ds(0, devices - 1)], send_sem
+    ).wait()
+    pltpu.make_async_copy(send_ref, recv, recv_sem).wait()
+
+    row_iota = lax.broadcasted_iota(jnp.int32, (rows, lane_count), 0)
+    lane_iota = lax.broadcasted_iota(jnp.int32, (lane_count, lane_count), 0)
+
+    def deposit(source, total):
+        chunk = recv[source]
+        row_hits = (chunk[3:4, :].astype(jnp.int32) == row_iota).astype(jnp.bfloat16)
+        lane_hits = chunk[4:5, :].astype(jnp.int32) == lane_iota
+        spread = jnp.concatenate(
+            [jnp.where(lane_hits, chunk[c : c + 1, :], 0.0) for c in range(3)], axis=0
+        ).astype(jnp.bfloat16)
+        return total + lax.dot_general(
+            row_hits, spread, (((1,), (1,)), ((), ())), preferred_element_type=jnp.float32
+        )
+
+    maps_ref[...] = lax.fori_loop(
+        0, devices, deposit, jnp.zeros(maps_ref.shape, jnp.float32)
+    )
+
+
+def exchange(send, count_y):
+    devices = send.shape[0]
+    return pl.pallas_call(
+        functools.partial(exchange_kernel, count_y),
+        out_shape=jax.ShapeDtypeStruct((STRIP_ROWS, 3 * lane_count), jnp.float32),
+        in_specs=[pl.BlockSpec(memory_space=pltpu.VMEM)],
+        out_specs=pl.BlockSpec(memory_space=pltpu.VMEM),
+        scratch_shapes=[
+            pltpu.VMEM(send.shape, jnp.float32),
+            pltpu.SemaphoreType.DMA(()),
+            pltpu.SemaphoreType.DMA(()),
+        ],
+        compiler_params=pltpu.CompilerParams(collective_id=0, has_side_effects=True),
+    )(send)
 
 
 def passed_along(block, axis, distance):
@@ -103,19 +181,14 @@
     )
     dest_hits = (dest[:, :, None] == jnp.arange(devices, dtype=jnp.int32)).astype(jnp.bfloat16)
     rank_hits = (rank[:, :, None] == jnp.arange(blocks, dtype=jnp.int32)).astype(jnp.bfloat16)
-    placed = (rank_hits[:, :, :, None] * fields[:, :, None, :]).reshape(REPLICAS, per_replica, blocks * 5)
+    placed = (fields[:, :, :, None] * rank_hits[:, :, None, :]).reshape(REPLICAS, per_replica, 5 * blocks)
     send = lax.dot_general(
         dest_hits, placed, (((1,), (1,)), ((0,), (0,))), preferred_element_type=jnp.float32
-    ).astype(jnp.bfloat16)
-    send = jnp.transpose(send, (1, 0, 2)).reshape(devices, slots, 5)
-    got = lax.all_to_all(send, ("gx", "gy"), 0, 0, tiled=True).reshape(devices * slots, 5)
-
-    rows = got[:, 3].astype(jnp.int32)
-    lanes = got[:, 4].astype(jnp.int32)
-    row_hits = (rows[None, :] == jnp.arange(STRIP_ROWS, dtype=jnp.int32)[:, None]).astype(jnp.bfloat16)
-    lane_hits = (lanes[:, None] == jnp.arange(lane_count, dtype=jnp.int32)[None, :]).astype(jnp.bfloat16)
-    spread = (got[:, :3, None] * lane_hits[:, None, :]).reshape(devices * slots, 3 * lane_count)
-    maps = jnp.dot(row_hits, spread, preferred_element_type=jnp.float32)
+    )
+    send = jnp.transpose(send.reshape(REPLICAS, devices, 5, blocks), (1, 2, 0, 3))
+    send = send.reshape(devices, 5, slots)
+    send = jnp.pad(send, ((0, 0), (0, FIELDS - 5), (0, lane_count - slots)))
+    maps = exchange(send, count_y)
     return (new_places.reshape(3, blocks * width), new_speeds.reshape(3, blocks * width), maps)
 
 

time: 49.2 us -> 67.5 us (1.37)
  Pallas kernels: 0 us -> 41.8 us
  blocking collectives: 20 us -> 0 us
  other arithmetic: 8.24 us -> 5.9 us
  matrix products: 3.09 us -> 0.96 us
  local copies, waits for them, and re-layouts: 6.57 us -> 7.47 us
    pallas_call x0 -> x1, Pallas kernels: none -> 41.8 us  [exchange(): pl.pallas_call(functools.partial(exchange_kernel, count_y), out_shape=jax...]
    all_to_all x1 -> x0, blocking collectives: 20 us -> none  [on_device(): lax.all_to_all(send, ('gx', 'gy'), 0, 0, tiled=True)]
    dot_general x1 -> x0, matrix products: 2.58 us -> none  [on_device(): maps = jnp.dot(row_hits, spread, preferred_element_type=jnp.float32)]
    unnamed x12 -> x15, local copies, waits for them, and re-layouts: 0.46 us -> 1.62 us
    pad x0 -> x1, local copies, waits for them, and re-layouts: none -> 0.84 us  [on_device(): send = jnp.pad(send, ((0, 0), (0, FIELDS - 5), (0, lane_count - slots)))]
    convert_element_type x1, other arithmetic: 0.68 us -> 0.01 us  [on_device(): shifted = global_pos[None] + offsets.astype(jnp.float32)[:, :, None, None]]
  transfers between devices with their start and end apart: 4 -> 4, of which waited for: 0 -> 0; matrix products, arithmetic and copies ran while one was open for 14% -> 7% of each run, Pallas kernels for 0% -> 0%
where the time goes in v3:
time: 67.5 us; the launch traced here: 67.1 us
  Pallas kernels  41.8 us (62%)
  starting transfers between devices  9.99 us (15%)
  local copies, waits for them, and re-layouts  7.47 us (11%)
  other arithmetic  5.9 us (9%)
  matrix products  0.96 us (1%)
  between operations  0.95 us (1%)
    pallas_call x1, Pallas kernels, exchange(): pl.pallas_call(functools.partial(exchange_kernel, count_y), out_shape=jax...  41.8 us
    ppermute x4, starting transfers between devices, passed_along(): return lax.ppermute(block, axis, route)  9.99 us
    unnamed x15, local copies, waits for them, and re-layouts  1.62 us
    sort x1, other arithmetic, on_device(): chosen = jnp.argsort(ranking)[:CROSS_MAX]  1.61 us
    gather x1, local copies, waits for them, and re-layouts, on_device(): speeds = jnp.take(speeds, ordering, axis=1)  1.37 us
  transfers between devices with their start and end apart: 4, of which 0 were waited for; matrix products, arithmetic and copies ran while one was open for 7% of the time, Pallas kernels for 0%

profile of v3, /device:TPU:1, one launch (start us, length us, event | category | flops | bytes accessed | tf_op | source)
XLA Modules:
  0.0 67.1 jit_solution(7683134371810540851)
XLA Ops:
  0.6 0.0 copy-start
  0.6 0.0 copy-start.1
  0.7 0.7 %compare_and_fusion = pred[20]{0:T(512)(128)(4,1)S(1)} fusion(s32[1,20]{1,0:T(1,128)} %param.20), kind=kLoop, calls=%fused_computation.80 | loop fusion | flops 120 | bytes 100 | tf_op jit(solution)/shard_map/jit(_take)/and | solution.py:117
  1.3 0.7 compare_select_fusion
  2.0 0.8 %bitcast_add_fusion = f32[3,20,128]{2,0,1:T(4,128)S(1)} fusion(f32[3,2560]{1,0:T(4,128)} %param.18, f32[3,2560]{1,0:T(4,128)} %param.19), kind=kLoop, calls=%fused_computation.17 | loop fusion | flops 15360 | bytes 92160 | tf_op jit(solution)/shard_map/add | solution.py:115
  2.8 1.4 %gather_fusion.3 = f32[20,3,128]{2,1,0:T(4,128)S(1)} fusion(f32[3,20,128]{2,0,1:T(4,128)} %bitcast.57, s32[1024]{0:T(1024)S(1)} %pad_clamp_fusion.1), kind=kCustom, calls=%fused_computation.2.clone | custom fusion | bytes 61520 | tf_op jit(solution)/shard_map/jit(_take)/gather | solution.py:118
  4.2 0.6 gather_fusion.2
  4.8 0.1 select_bitcast_fusion
  5.0 1.5 %collective-permute-start.3 = (f32[6,2,128]{2,0,1:T(8,128)S(1)}, f32[6,2,128]{2,0,1:T(8,128)S(1)}, u32[]{:S(2)}, u32[]{:S(2)}) collective-permute-start(f32[6,2,128]{2,0,1:T(8,128)S(1)} %pad_maximum_fusion.5), channel_id=1, source_target_pairs={{1,0},{2,1},{3,2},{4,3},{5,4},{6,5},{7,6},{8,7},{9,8},{10,9},{11,1... | collective-permute-start | bytes 18440 | tf_op jit(solution)/shard_map/ppermute | solution.py:97
  6.5 4.9 %collective-permute-start.1 = (f32[6,2,128]{2,0,1:T(8,128)S(1)}, f32[6,2,128]{2,0,1:T(8,128)S(1)}, u32[]{:S(2)}, u32[]{:S(2)}) collective-permute-start(f32[6,2,128]{2,0,1:T(8,128)S(1)} %pad_maximum_fusion.3), channel_id=1, source_target_pairs={{16,0},{32,16},{48,32},{64,48},{80,64},{96,80},{112,96},{0,112},{1... | collective-permute-start | bytes 18440 | tf_op jit(solution)/shard_map/ppermute | solution.py:97
  11.4 0.1 collective-permute-start
  11.6 3.5 %collective-permute-start.2 = (f32[6,2,128]{2,0,1:T(8,128)S(1)}, f32[6,2,128]{2,0,1:T(8,128)S(1)}, u32[]{:S(2)}, u32[]{:S(2)}) collective-permute-start(f32[6,2,128]{2,0,1:T(8,128)S(1)} %pad_maximum_fusion.4), channel_id=1, source_target_pairs={{15,0},{0,1},{1,2},{2,3},{3,4},{4,5},{5,6},{6,7},{7,8},{8,9},{9,10... | collective-permute-start | bytes 18440 | tf_op jit(solution)/shard_map/ppermute | solution.py:97
  15.1 0.0 copy-done.1
  15.1 1.6 %sort.17 = (s32[20]{0:T(128)}, s32[20]{0:T(128)S(1)}) sort(s32[20]{0:T(128)S(1)} %iota_add_fusion, s32[20]{0:T(128)S(1)} %iota.33), dimensions={0}, to_apply=%region_0.0 | sort | flops 100 | bytes 320 | tf_op jit(solution)/shard_map/jit(argsort)/sort | solution.py:149
  16.7 0.1 broadcast_bitcast_fusion.1
  16.8 0.0 copy-done
  16.8 0.6 gather_fusion
  17.5 0.1 iota_compare_fusion
  17.6 0.0 copy-start.4
  17.6 0.6 gather_fusion.1
  18.3 1.3 %convert_reduce_fusion = s32[3,640]{1,0:T(4,128)S(1)} fusion(s32[3,640]{1,0:T(4,128)S(1)} %add_select_fusion.3, pred[640,640]{1,0:T(8,128)(4,1)S(1)} %iota_compare_fusion), kind=kLoop, calls=%fused_computation.6 | loop fusion | flops 4913280 | bytes 424960 | tf_op jit(solution)/shard_map/reduce_sum | solution.py:172
  19.6 0.1 broadcast_bitcast_fusion
  19.7 0.0 copy-done.4
  19.7 0.0 collective-permute-done
  19.7 0.0 collective-permute-done.1
  19.8 0.0 collective-permute-done.2
  19.8 0.0 collective-permute-done.3
  19.8 0.0 copy-start.2
  19.8 0.0 copy-start.3
  19.8 0.6 gather_fusion.5
  20.4 0.1 multiply_reduce_fusion
  20.5 0.6 gather_fusion.4
  21.1 0.1 select_bitcast_fusion.3
  21.2 0.1 fusion.4
  21.5 0.0 copy-done.2
  21.5 0.0 copy-done.3
  21.5 0.1 mul.134
  21.6 1.0 %fusion = f32[3,128,100]{1,2,0:T(8,128)S(1)} fusion(bf16[3,640,100]{1,2,0:T(8,128)(2,1)S(1)} %mul.134, s32[3,640]{1,0:T(4,128)S(1)} %add_select_fusion.3), kind=kOutput, calls=%fused_computation.9 | convolution fusion | flops 49397760 | bytes 545280 | tf_op jit(solution)/shard_map/dot_general | solution.py:185
  22.6 0.2 copy.19
  22.9 0.8 %pad.12.send_ref = f32[128,8,128]{2,1,0:T(8,128)} pad(f32[128,5,60]{2,1,0:T(8,128)S(1)} %copy.19, f32[]{:T(128)} %constant.213.clone.1), padding=0_0x0_3x0_68 | pad | bytes 677892 | tf_op jit(solution)/shard_map/jit(_pad)/pad | solution.py:190
  23.7 41.8 %shard_map.85 = f32[64,384]{1,0:T(8,128)} custom-call(f32[128,8,128]{2,1,0:T(8,128)} %pad.12.send_ref), custom_call_target="tpu_custom_call" | custom-call | tf_op jit(solution)/shard_map/pallas_call | solution.py:80
  65.5 1.5 %copy.35 = f32[64,384]{1,0:T(8,128)} copy(f32[64,384]{1,0:T(8,128)} %shard_map.85) | data formatting | bytes 196608
  (40 shorter events, 0.6 us)
Async XLA Ops:
  0.6 16.2 %copy-start = (s32[3,2560]{1,0:T(4,128)S(1)}, s32[3,2560]{1,0:T(4,128)}, u32[]{:S(2)}) copy-start(s32[3,2560]{1,0:T(4,128)} %param.23) | copy-start | bytes 92164
  0.6 14.5 %copy-start.1 = (s32[1,20]{1,0:T(1,128)S(1)}, s32[1,20]{1,0:T(1,128)}, u32[]{:S(2)}) copy-start(s32[1,20]{1,0:T(1,128)} %param.21) | copy-start | bytes 244
  5.0 14.8 %collective-permute-start.3 = (f32[6,2,128]{2,0,1:T(8,128)S(1)}, f32[6,2,128]{2,0,1:T(8,128)S(1)}, u32[]{:S(2)}, u32[]{:S(2)}) collective-permute-start(f32[6,2,128]{2,0,1:T(8,128)S(1)} %pad_maximum_fusion.5), channel_id=1, source_target_pairs={{1,0},{2,1},{3,2},{4,3},{5,4},{6,5},{7,6},{8,7},{9,8},{10,9},{11,1... | collective-permute-start | bytes 18440 | tf_op jit(solution)/shard_map/ppermute | solution.py:97
  6.5 13.2 %collective-permute-start.1 = (f32[6,2,128]{2,0,1:T(8,128)S(1)}, f32[6,2,128]{2,0,1:T(8,128)S(1)}, u32[]{:S(2)}, u32[]{:S(2)}) collective-permute-start(f32[6,2,128]{2,0,1:T(8,128)S(1)} %pad_maximum_fusion.3), channel_id=1, source_target_pairs={{16,0},{32,16},{48,32},{64,48},{80,64},{96,80},{112,96},{0,112},{1... | collective-permute-start | bytes 18440 | tf_op jit(solution)/shard_map/ppermute | solution.py:97
  11.4 8.3 %collective-permute-start = (f32[6,2,128]{2,0,1:T(8,128)S(1)}, f32[6,2,128]{2,0,1:T(8,128)S(1)}, u32[]{:S(2)}, u32[]{:S(2)}) collective-permute-start(f32[6,2,128]{2,0,1:T(8,128)S(1)} %pad_maximum_fusion.2), channel_id=1, source_target_pairs={{112,0},{0,16},{16,32},{32,48},{48,64},{64,80},{80,96},{96,112},{1... | collective-permute-start | bytes 18440 | tf_op jit(solution)/shard_map/ppermute | solution.py:97
  11.6 8.2 %collective-permute-start.2 = (f32[6,2,128]{2,0,1:T(8,128)S(1)}, f32[6,2,128]{2,0,1:T(8,128)S(1)}, u32[]{:S(2)}, u32[]{:S(2)}) collective-permute-start(f32[6,2,128]{2,0,1:T(8,128)S(1)} %pad_maximum_fusion.4), channel_id=1, source_target_pairs={{15,0},{0,1},{1,2},{2,3},{3,4},{4,5},{5,6},{6,7},{7,8},{8,9},{9,10... | collective-permute-start | bytes 18440 | tf_op jit(solution)/shard_map/ppermute | solution.py:97
  17.6 2.1 %copy-start.4 = (s32[3,3]{1,0:T(4,128)S(1)}, s32[3,3]{1,0:T(4,128)}, u32[]{:S(2)}) copy-start(s32[3,3]{1,0:T(4,128)} %param.22) | copy-start | bytes 112
  19.8 1.7 %copy-start.2 = (f32[3,20,128]{2,0,1:T(4,128)}, f32[3,20,128]{2,0,1:T(4,128)S(1)}, u32[]{:S(2)}) copy-start(f32[3,20,128]{2,0,1:T(4,128)S(1)} %get-tuple-element.83) | copy-start | bytes 92164
  19.8 1.7 %copy-start.3 = (f32[3,20,128]{2,0,1:T(4,128)}, f32[3,20,128]{2,0,1:T(4,128)S(1)}, u32[]{:S(2)}) copy-start(f32[3,20,128]{2,0,1:T(4,128)S(1)} %get-tuple-element.84) | copy-start | bytes 92164

commit v4 on v3

--- a/solution.py
+++ b/solution.py
@@ -15,13 +15,11 @@
 
 time_step = 0.05
 lane_count = 128
-FIELDS = 8
 MESH = pl.DeviceIdType.MESH
 
 
-def exchange_kernel(count_y, send_ref, maps_ref, recv, send_sem, recv_sem):
+def exchange_kernel(count_y, send_ref, out_ref, recv, send_sem, recv_sem):
     devices = send_ref.shape[0]
-    rows = maps_ref.shape[0]
     me = lax.axis_index("gx") * count_y + lax.axis_index("gy")
 
     def peer(offset):
@@ -56,30 +54,14 @@
     ).wait()
     pltpu.make_async_copy(send_ref, recv, recv_sem).wait()
 
-    row_iota = lax.broadcasted_iota(jnp.int32, (rows, lane_count), 0)
-    lane_iota = lax.broadcasted_iota(jnp.int32, (lane_count, lane_count), 0)
-
-    def deposit(source, total):
-        chunk = recv[source]
-        row_hits = (chunk[3:4, :].astype(jnp.int32) == row_iota).astype(jnp.bfloat16)
-        lane_hits = chunk[4:5, :].astype(jnp.int32) == lane_iota
-        spread = jnp.concatenate(
-            [jnp.where(lane_hits, chunk[c : c + 1, :], 0.0) for c in range(3)], axis=0
-        ).astype(jnp.bfloat16)
-        return total + lax.dot_general(
-            row_hits, spread, (((1,), (1,)), ((), ())), preferred_element_type=jnp.float32
-        )
-
-    maps_ref[...] = lax.fori_loop(
-        0, devices, deposit, jnp.zeros(maps_ref.shape, jnp.float32)
-    )
+    out_ref[...] = recv[...]
 
 
 def exchange(send, count_y):
     devices = send.shape[0]
     return pl.pallas_call(
         functools.partial(exchange_kernel, count_y),
-        out_shape=jax.ShapeDtypeStruct((STRIP_ROWS, 3 * lane_count), jnp.float32),
+        out_shape=jax.ShapeDtypeStruct(send.shape, jnp.float32),
         in_specs=[pl.BlockSpec(memory_space=pltpu.VMEM)],
         out_specs=pl.BlockSpec(memory_space=pltpu.VMEM),
         scratch_shapes=[
@@ -187,8 +169,28 @@
     )
     send = jnp.transpose(send.reshape(REPLICAS, devices, 5, blocks), (1, 2, 0, 3))
     send = send.reshape(devices, 5, slots)
-    send = jnp.pad(send, ((0, 0), (0, FIELDS - 5), (0, lane_count - slots)))
-    maps = exchange(send, count_y)
+    pixel = send[:, 3] * lane_count + send[:, 4]
+    half = lane_count // 2
+    pad = ((0, 0), (0, half - slots))
+    send = jnp.stack(
+        [
+            jnp.concatenate([jnp.pad(send[:, 0], pad), jnp.pad(send[:, 1], pad)], axis=1),
+            jnp.concatenate([jnp.pad(send[:, 2], pad), jnp.pad(pixel, pad)], axis=1),
+        ],
+        axis=1,
+    )
+    got = exchange(send, count_y)
+    got_values = jnp.stack([got[:, 0, :half], got[:, 0, half:], got[:, 1, :half]], axis=1)
+    got_values = got_values.reshape(devices, 3, half).transpose(0, 2, 1).reshape(devices * half, 3)
+    got_pixel = got[:, 1, half:].reshape(devices * half).astype(jnp.int32)
+    rows = got_pixel // lane_count
+    lanes = got_pixel % lane_count
+    row_hits = (rows[None, :] == jnp.arange(STRIP_ROWS, dtype=jnp.int32)[:, None]).astype(jnp.bfloat16)
+    lane_hits = (lanes[:, None] == jnp.arange(lane_count, dtype=jnp.int32)[None, :]).astype(jnp.bfloat16)
+    spread = (got_values.astype(jnp.bfloat16)[:, :, None] * lane_hits[:, None, :]).reshape(
+        devices * half, 3 * lane_count
+    )
+    maps = jnp.dot(row_hits, spread, preferred_element_type=jnp.float32)
     return (new_places.reshape(3, blocks * width), new_speeds.reshape(3, blocks * width), maps)
 
 

time: 67.5 us -> 50.5 us (0.75)
  Pallas kernels: 41.8 us -> 17.4 us
  other arithmetic: 5.9 us -> 11.2 us
  matrix products: 0.96 us -> 3.64 us
    pallas_call x1, Pallas kernels: 41.8 us -> 17.4 us  [exchange(): pl.pallas_call(functools.partial(exchange_kernel, count_y), out_shape=jax...]
    dot_general x0 -> x1, matrix products: none -> 2.68 us  [on_device(): maps = jnp.dot(row_hits, spread, preferred_element_type=jnp.float32)]
    another operation x1 -> x3, other arithmetic: 0.01 us -> 1.73 us
    convert_element_type x0 -> x3, other arithmetic: none -> 1.61 us  [the longest x1 1.17 us: on_device(): got_pixel = got[:, 1, half:].reshape(devices * half).astype(jnp.int32)]
    unnamed x15, local copies, waits for them, and re-layouts: 1.62 us -> 0.57 us
    pad x1 -> x0, local copies, waits for them, and re-layouts: 0.84 us -> none  [on_device(): send = jnp.pad(send, ((0, 0), (0, FIELDS - 5), (0, lane_count - slots)))]
    convert_element_type x1, other arithmetic: 0.01 us -> 0.68 us  [on_device(): shifted = global_pos[None] + offsets.astype(jnp.float32)[:, :, None, None]]
  transfers between devices with their start and end apart: 4 -> 4, of which waited for: 0 -> 0; matrix products, arithmetic and copies ran while one was open for 7% -> 13% of each run, Pallas kernels for 0% -> 0%
where the time goes in v4:
time: 50.5 us; the launch traced here: 50.1 us
  Pallas kernels  17.4 us (34%)
  other arithmetic  11.2 us (22%)
  starting transfers between devices  9.99 us (20%)
  local copies, waits for them, and re-layouts  6.8 us (13%)
  matrix products  3.64 us (7%)
  between operations  1.04 us (2%)
    pallas_call x1, Pallas kernels, exchange(): pl.pallas_call(functools.partial(exchange_kernel, count_y), out_shape=jax...  17.4 us
    ppermute x4, starting transfers between devices, passed_along(): return lax.ppermute(block, axis, route)  9.99 us
    dot_general x1, matrix products, on_device(): maps = jnp.dot(row_hits, spread, preferred_element_type=jnp.float32)  2.68 us
    sort x1, other arithmetic, on_device(): chosen = jnp.argsort(ranking)[:CROSS_MAX]  1.61 us
    gather x1, local copies, waits for them, and re-layouts, on_device(): speeds = jnp.take(speeds, ordering, axis=1)  1.37 us
    reduce_sum x1, other arithmetic, on_device(): rank = jnp.sum(same.astype(jnp.int32), axis=2)  1.34 us
    gather x1, local copies, waits for them, and re-layouts, on_device(): jnp.take(flag_row, chosen).astype(jnp.float32).reshape(1, CROSS_MAX, 1)  1.3 us
    convert_element_type x1, other arithmetic, on_device(): got_pixel = got[:, 1, half:].reshape(devices * half).astype(jnp.int32)  1.17 us
  transfers between devices with their start and end apart: 4, of which 0 were waited for; matrix products, arithmetic and copies ran while one was open for 13% of the time, Pallas kernels for 0%

profile of v4, /device:TPU:1, one launch (start us, length us, event | category | flops | bytes accessed | tf_op | source)
XLA Modules:
  0.0 50.1 jit_solution(18190291919056648916)
XLA Ops:
  0.6 0.0 copy-start
  0.6 0.7 %compare_and_fusion = pred[20]{0:T(512)(128)(4,1)S(1)} fusion(s32[1,20]{1,0:T(1,128)} %param.20), kind=kLoop, calls=%fused_computation.102 | loop fusion | flops 120 | bytes 100 | tf_op jit(solution)/shard_map/jit(_take)/and | solution.py:99
  1.3 0.7 %compare_select_fusion = s32[20]{0:T(128)S(1)} fusion(s32[1,20]{1,0:T(1,128)} %param.20), kind=kLoop, calls=%fused_computation.95 | loop fusion | flops 60 | bytes 160 | tf_op jit(solution)/shard_map/jit(_take)/jit(_where)/select_n | solution.py:99
  2.0 0.8 %bitcast_add_fusion = f32[3,20,128]{2,0,1:T(4,128)S(1)} fusion(f32[3,2560]{1,0:T(4,128)} %param.18, f32[3,2560]{1,0:T(4,128)} %param.19), kind=kLoop, calls=%fused_computation.36 | loop fusion | flops 15360 | bytes 92160 | tf_op jit(solution)/shard_map/add | solution.py:97
  2.8 1.4 %gather_fusion.3 = f32[20,3,128]{2,1,0:T(4,128)S(1)} fusion(f32[3,20,128]{2,0,1:T(4,128)} %bitcast.76, s32[1024]{0:T(1024)S(1)} %pad_clamp_fusion.1), kind=kCustom, calls=%fused_computation.2.clone | custom fusion | bytes 61520 | tf_op jit(solution)/shard_map/jit(_take)/gather | solution.py:100
  4.2 0.6 %gather_fusion.2 = f32[20,3,128]{2,1,0:T(4,128)S(1)} fusion(f32[3,20,128]{2,0,1:T(4,128)S(1)} %bitcast_add_fusion, s32[1024]{0:T(1024)S(1)} %pad_clamp_fusion.1), kind=kCustom, calls=%fused_computation.clone | custom fusion | bytes 61520 | tf_op jit(solution)/shard_map/jit(_take)/gather | solution.py:99
  4.8 0.1 select_bitcast_fusion
  4.9 1.5 %collective-permute-start.3 = (f32[6,2,128]{2,0,1:T(8,128)S(1)}, f32[6,2,128]{2,0,1:T(8,128)S(1)}, u32[]{:S(2)}, u32[]{:S(2)}) collective-permute-start(f32[6,2,128]{2,0,1:T(8,128)S(1)} %pad_maximum_fusion.6), channel_id=1, source_target_pairs={{1,0},{2,1},{3,2},{4,3},{5,4},{6,5},{7,6},{8,7},{9,8},{10,9},{11,1... | collective-permute-start | bytes 18440 | tf_op jit(solution)/shard_map/ppermute | solution.py:79
  6.5 4.9 %collective-permute-start.1 = (f32[6,2,128]{2,0,1:T(8,128)S(1)}, f32[6,2,128]{2,0,1:T(8,128)S(1)}, u32[]{:S(2)}, u32[]{:S(2)}) collective-permute-start(f32[6,2,128]{2,0,1:T(8,128)S(1)} %pad_maximum_fusion.4), channel_id=1, source_target_pairs={{16,0},{32,16},{48,32},{64,48},{80,64},{96,80},{112,96},{0,112},{1... | collective-permute-start | bytes 18440 | tf_op jit(solution)/shard_map/ppermute | solution.py:79
  11.4 0.1 collective-permute-start
  11.6 3.5 %collective-permute-start.2 = (f32[6,2,128]{2,0,1:T(8,128)S(1)}, f32[6,2,128]{2,0,1:T(8,128)S(1)}, u32[]{:S(2)}, u32[]{:S(2)}) collective-permute-start(f32[6,2,128]{2,0,1:T(8,128)S(1)} %pad_maximum_fusion.5), channel_id=1, source_target_pairs={{15,0},{0,1},{1,2},{2,3},{3,4},{4,5},{5,6},{6,7},{7,8},{8,9},{9,10... | collective-permute-start | bytes 18440 | tf_op jit(solution)/shard_map/ppermute | solution.py:79
  15.1 0.7 %iota_add_fusion = s32[20]{0:T(128)S(1)} fusion(s32[1,20]{1,0:T(1,128)} %param.21), kind=kLoop, calls=%fused_computation.110 | loop fusion | flops 60 | bytes 160 | tf_op jit(solution)/shard_map/add | solution.py:130
  15.7 1.6 %sort.17 = (s32[20]{0:T(128)}, s32[20]{0:T(128)S(1)}) sort(s32[20]{0:T(128)S(1)} %iota_add_fusion, s32[20]{0:T(128)S(1)} %iota.44), dimensions={0}, to_apply=%region_0.0 | sort | flops 100 | bytes 320 | tf_op jit(solution)/shard_map/jit(argsort)/sort | solution.py:131
  17.4 0.1 broadcast_bitcast_fusion.1
  17.4 0.0 copy-done
  17.4 0.6 %gather_fusion = s32[5,3,128]{2,1,0:T(4,128)S(1)} fusion(s32[3,20,128]{2,0,1:T(4,128)S(1)} %bitcast.67, s32[1024]{0:T(1024)S(1)} %pad_clamp_fusion), kind=kCustom, calls=%fused_computation.4 | custom fusion | bytes 15380 | tf_op jit(solution)/shard_map/jit(_take)/gather | solution.py:135
  18.1 0.1 iota_compare_fusion.3
  18.2 1.3 %gather_fusion.1 = s32[5]{0:T(128)S(1)} fusion(s32[20]{0:T(128)} %bitcast.68, s32[1024]{0:T(1024)S(1)} %pad_clamp_fusion), kind=kCustom, calls=%fused_computation.5 | custom fusion | bytes 60 | tf_op jit(solution)/shard_map/jit(_take)/gather | solution.py:132
  19.6 1.3 %convert_reduce_fusion = s32[3,640]{1,0:T(4,128)S(1)} fusion(s32[3,640]{1,0:T(4,128)S(1)} %add_select_fusion.5, pred[640,640]{1,0:T(8,128)(4,1)S(1)} %iota_compare_fusion.3), kind=kLoop, calls=%fused_computation.6 | loop fusion | flops 4913280 | bytes 424960 | tf_op jit(solution)/shard_map/reduce_sum | solution.py:154
  20.9 0.1 broadcast_bitcast_fusion
  21.0 0.7 %convert_element_type.87 = f32[3,3]{1,0:T(4,128)S(1)} convert(s32[3,3]{1,0:T(4,128)} %param.22) | non-fusion elementwise | flops 9 | bytes 72 | tf_op jit(solution)/shard_map/convert_element_type | solution.py:144
  21.7 0.0 collective-permute-done
  21.7 0.0 collective-permute-done.1
  21.7 0.0 collective-permute-done.2
  21.8 0.0 collective-permute-done.3
  21.8 0.0 copy-start.1
  21.8 0.0 copy-start.2
  21.8 0.6 %gather_fusion.5 = f32[5,3,128]{2,1,0:T(4,128)S(1)} fusion(f32[3,20,128]{2,0,1:T(4,128)S(1)} %get-tuple-element.93, s32[1024]{0:T(1024)S(1)} %pad_clamp_fusion), kind=kCustom, calls=%fused_computation.3.clone | custom fusion | bytes 15380 | tf_op jit(solution)/shard_map/jit(_take)/gather | solution.py:134
  22.4 0.1 multiply_reduce_fusion
  22.5 0.6 %gather_fusion.4 = f32[5,3,128]{2,1,0:T(4,128)S(1)} fusion(f32[3,20,128]{2,0,1:T(4,128)S(1)} %get-tuple-element.94, s32[1024]{0:T(1024)S(1)} %pad_clamp_fusion), kind=kCustom, calls=%fused_computation.1.clone | custom fusion | bytes 15380 | tf_op jit(solution)/shard_map/jit(_take)/gather | solution.py:133
  23.0 0.1 select_bitcast_fusion.3
  23.2 0.1 fusion.8
  23.5 0.1 mul.158
  23.5 1.0 %fusion.3 = f32[3,128,100]{1,2,0:T(8,128)S(1)} fusion(bf16[3,640,100]{1,2,0:T(8,128)(2,1)S(1)} %mul.158, s32[3,640]{1,0:T(4,128)S(1)} %add_select_fusion.5), kind=kOutput, calls=%fused_computation.15 | convolution fusion | flops 49397760 | bytes 545280 | tf_op jit(solution)/shard_map/dot_general | solution.py:167
  24.6 0.1 copy.47
  24.7 0.1 copy.50
  24.8 0.1 copy.49
  24.9 0.1 copy.48
  25.0 0.1 copy.51
  25.1 0.1 select_maximum_fusion.1
  25.2 0.1 select_maximum_fusion
  25.3 0.8 %pad_maximum_fusion.send_ref = f32[128,2,128]{2,1,0:T(2,128)} fusion(f32[128,1,128]{2,1,0:T(1,128)S(1)} %bitcast.75, f32[128,1,128]{2,1,0:T(1,128)S(1)} %bitcast.74), kind=kLoop, calls=%fused_computation.21 | loop fusion | flops 32768 | bytes 262144 | tf_op jit(solution)/shard_map/stack | solution.py:175
  26.1 17.4 %shard_map.85 = f32[128,2,128]{2,1,0:T(2,128)} custom-call(f32[128,2,128]{2,1,0:T(2,128)} %pad_maximum_fusion.send_ref), custom_call_target="tpu_custom_call" | custom-call | tf_op jit(solution)/shard_map/pallas_call | solution.py:62
  43.5 1.0 %convert.20 = bf16[128,2,128]{2,1,0:T(2,128)(2,1)S(1)} convert(f32[128,2,128]{2,1,0:T(2,128)} %shard_map.85) | non-fusion elementwise | flops 32768 | bytes 196608 | tf_op jit(solution)/shard_map/convert.5
  44.4 1.2 %convert_reduce_fusion.1 = s32[128,64]{1,0:T(8,128)S(1)} fusion(f32[128,2,128]{2,1,0:T(2,128)} %shard_map.85), kind=kLoop, calls=%fused_computation.26 | loop fusion | flops 8192 | bytes 65536 | tf_op jit(solution)/shard_map/convert_element_type | solution.py:185
  45.6 0.1 convert_element_type.94
  45.7 0.2 fusion.19
  45.9 0.1 copy.43
  46.0 0.1 copy.45
  46.1 0.1 copy.44
  46.2 0.1 copy.46
  46.4 0.1 convert_element_type.96
  46.5 0.4 fusion
  46.9 0.0 copy-done.1
  46.9 0.0 copy-done.2
  46.9 0.4 broadcast_multiply_fusion
  47.4 2.7 %fusion.1 = f32[64,384]{1,0:T(8,128)} fusion(bf16[8192,384]{0,1:T(8,128)(2,1)S(1)} %bitcast.69, s32[8192]{0:T(1024)S(1)} %get-tuple-element.83), kind=kOutput, calls=%fused_computation.11 | convolution fusion | flops 403177472 | bytes 6422528 | tf_op jit(solution)/shard_map/dot_general | solution.py:193
  (42 shorter events, 0.6 us)
Async XLA Ops:
  0.6 16.8 %copy-start = (s32[3,2560]{1,0:T(4,128)S(1)}, s32[3,2560]{1,0:T(4,128)}, u32[]{:S(2)}) copy-start(s32[3,2560]{1,0:T(4,128)} %param.23) | copy-start | bytes 92164
  4.9 16.8 %collective-permute-start.3 = (f32[6,2,128]{2,0,1:T(8,128)S(1)}, f32[6,2,128]{2,0,1:T(8,128)S(1)}, u32[]{:S(2)}, u32[]{:S(2)}) collective-permute-start(f32[6,2,128]{2,0,1:T(8,128)S(1)} %pad_maximum_fusion.6), channel_id=1, source_target_pairs={{1,0},{2,1},{3,2},{4,3},{5,4},{6,5},{7,6},{8,7},{9,8},{10,9},{11,1... | collective-permute-start | bytes 18440 | tf_op jit(solution)/shard_map/ppermute | solution.py:79
  6.5 15.2 %collective-permute-start.1 = (f32[6,2,128]{2,0,1:T(8,128)S(1)}, f32[6,2,128]{2,0,1:T(8,128)S(1)}, u32[]{:S(2)}, u32[]{:S(2)}) collective-permute-start(f32[6,2,128]{2,0,1:T(8,128)S(1)} %pad_maximum_fusion.4), channel_id=1, source_target_pairs={{16,0},{32,16},{48,32},{64,48},{80,64},{96,80},{112,96},{0,112},{1... | collective-permute-start | bytes 18440 | tf_op jit(solution)/shard_map/ppermute | solution.py:79
  11.4 10.3 %collective-permute-start = (f32[6,2,128]{2,0,1:T(8,128)S(1)}, f32[6,2,128]{2,0,1:T(8,128)S(1)}, u32[]{:S(2)}, u32[]{:S(2)}) collective-permute-start(f32[6,2,128]{2,0,1:T(8,128)S(1)} %pad_maximum_fusion.3), channel_id=1, source_target_pairs={{112,0},{0,16},{16,32},{32,48},{48,64},{64,80},{80,96},{96,112},{1... | collective-permute-start | bytes 18440 | tf_op jit(solution)/shard_map/ppermute | solution.py:79
  11.6 10.2 %collective-permute-start.2 = (f32[6,2,128]{2,0,1:T(8,128)S(1)}, f32[6,2,128]{2,0,1:T(8,128)S(1)}, u32[]{:S(2)}, u32[]{:S(2)}) collective-permute-start(f32[6,2,128]{2,0,1:T(8,128)S(1)} %pad_maximum_fusion.5), channel_id=1, source_target_pairs={{15,0},{0,1},{1,2},{2,3},{3,4},{4,5},{5,6},{6,7},{7,8},{8,9},{9,10... | collective-permute-start | bytes 18440 | tf_op jit(solution)/shard_map/ppermute | solution.py:79
  21.8 25.1 %copy-start.1 = (f32[3,20,128]{2,0,1:T(4,128)}, f32[3,20,128]{2,0,1:T(4,128)S(1)}, u32[]{:S(2)}) copy-start(f32[3,20,128]{2,0,1:T(4,128)S(1)} %get-tuple-element.93) | copy-start | bytes 92164
  21.8 25.1 %copy-start.2 = (f32[3,20,128]{2,0,1:T(4,128)}, f32[3,20,128]{2,0,1:T(4,128)S(1)}, u32[]{:S(2)}) copy-start(f32[3,20,128]{2,0,1:T(4,128)S(1)} %get-tuple-element.94) | copy-start | bytes 92164

commit v5 on v4

--- a/solution.py
+++ b/solution.py
@@ -57,6 +57,54 @@
     out_ref[...] = recv[...]
 
 
+def migrate_kernel(send_ref, out_ref, recv, send_sem, recv_sem):
+    count_x = lax.axis_size("gx")
+    count_y = lax.axis_size("gy")
+    x = lax.axis_index("gx")
+    y = lax.axis_index("gy")
+    faces = (
+        (lax.rem(x + 1, count_x), y),
+        (lax.rem(x + count_x - 1, count_x), y),
+        (x, lax.rem(y + 1, count_y)),
+        (x, lax.rem(y + count_y - 1, count_y)),
+    )
+    barrier = pltpu.get_barrier_semaphore()
+    for where in faces:
+        pl.semaphore_signal(barrier, 1, device_id=where, device_id_type=MESH)
+    pl.semaphore_wait(barrier, len(faces))
+    copies = []
+    for face, where in enumerate(faces):
+        copy = pltpu.make_async_remote_copy(
+            src_ref=send_ref.at[face],
+            dst_ref=recv.at[face],
+            send_sem=send_sem.at[face],
+            recv_sem=recv_sem.at[face],
+            device_id=where,
+            device_id_type=MESH,
+        )
+        copy.start()
+        copies.append(copy)
+    for copy in copies:
+        copy.wait()
+    out_ref[...] = recv[...]
+
+
+def migrate(leaving):
+    faces = leaving.shape[0]
+    return pl.pallas_call(
+        migrate_kernel,
+        out_shape=jax.ShapeDtypeStruct(leaving.shape, jnp.float32),
+        in_specs=[pl.BlockSpec(memory_space=pltpu.VMEM)],
+        out_specs=pl.BlockSpec(memory_space=pltpu.VMEM),
+        scratch_shapes=[
+            pltpu.VMEM(leaving.shape, jnp.float32),
+            pltpu.SemaphoreType.DMA((faces,)),
+            pltpu.SemaphoreType.DMA((faces,)),
+        ],
+        compiler_params=pltpu.CompilerParams(collective_id=1, has_side_effects=True),
+    )(leaving)
+
+
 def exchange(send, count_y):
     devices = send.shape[0]
     return pl.pallas_call(
@@ -73,12 +121,6 @@
     )(send)
 
 
-def passed_along(block, axis, distance):
-    devices = range(lax.axis_size(axis))
-    route = [((i - distance) % len(devices), i) for i in devices]
-    return lax.ppermute(block, axis, route)
-
-
 def sky_terms(shifted, speeds, live_mask):
     radius = jnp.sum(shifted * shifted, axis=1)
     weight = 1.0 / (1.0 + radius)
@@ -104,17 +146,12 @@
         moved_pos = places[:, first_block : first_block + MOVERS].at[component].add(sign_step)
         return (moved_pos, speeds[:, first_block : first_block + MOVERS])
 
-    def moved(which_set, component, sign_step, axis, distance):
-        pos, vel = leaving(which_set, component, sign_step)
-        got = passed_along(jnp.concatenate([pos, vel], axis=0), axis, distance)
-        return got[:3], got[3:]
-
-    arrived = (
-        moved(0, 0, -1.0, "gx", 1),
-        moved(1, 0, 1.0, "gx", -1),
-        moved(2, 1, -1.0, "gy", 1),
-        moved(3, 1, 1.0, "gy", -1),
-    )
+    leaving_sets = ((0, 0, -1.0), (1, 0, 1.0), (2, 1, -1.0), (3, 1, 1.0))
+    leaving_blocks = jnp.stack(
+        [jnp.concatenate(leaving(*face), axis=0) for face in leaving_sets], axis=0
+    ).reshape(4, 6, MOVERS * width)
+    got_faces = migrate(leaving_blocks).reshape(4, 6, MOVERS, width)
+    arrived = [(got_faces[face, :3], got_faces[face, 3:]) for face in range(4)]
     new_places = jnp.concatenate(
         [places[:, 4 * MOVERS :]] + [received[0] for received in arrived], axis=1
     )
@@ -180,17 +217,18 @@
         axis=1,
     )
     got = exchange(send, count_y)
-    got_values = jnp.stack([got[:, 0, :half], got[:, 0, half:], got[:, 1, :half]], axis=1)
-    got_values = got_values.reshape(devices, 3, half).transpose(0, 2, 1).reshape(devices * half, 3)
-    got_pixel = got[:, 1, half:].reshape(devices * half).astype(jnp.int32)
-    rows = got_pixel // lane_count
-    lanes = got_pixel % lane_count
-    row_hits = (rows[None, :] == jnp.arange(STRIP_ROWS, dtype=jnp.int32)[:, None]).astype(jnp.bfloat16)
-    lane_hits = (lanes[:, None] == jnp.arange(lane_count, dtype=jnp.int32)[None, :]).astype(jnp.bfloat16)
-    spread = (got_values.astype(jnp.bfloat16)[:, :, None] * lane_hits[:, None, :]).reshape(
-        devices * half, 3 * lane_count
-    )
-    maps = jnp.dot(row_hits, spread, preferred_element_type=jnp.float32)
+    got_values = [got[:, 0, :half], got[:, 0, half:], got[:, 1, :half]]
+    got_pixel = got[:, 1, half:].astype(jnp.int32).reshape(1, devices * half)
+    row_hits = (got_pixel // lane_count == jnp.arange(STRIP_ROWS, dtype=jnp.int32)[:, None]).astype(
+        jnp.bfloat16
+    )
+    lane_hits = got_pixel % lane_count == jnp.arange(lane_count, dtype=jnp.int32)[:, None]
+    spread = jnp.concatenate(
+        [jnp.where(lane_hits, value.reshape(1, devices * half), 0.0) for value in got_values], axis=0
+    ).astype(jnp.bfloat16)
+    maps = lax.dot_general(
+        row_hits, spread, (((1,), (1,)), ((), ())), preferred_element_type=jnp.float32
+    )
     return (new_places.reshape(3, blocks * width), new_speeds.reshape(3, blocks * width), maps)
 
 

time: 50.5 us -> 54.9 us (1.087)
  starting transfers between devices: 9.99 us -> 0 us
  Pallas kernels: 17.4 us -> 26.6 us
  local copies, waits for them, and re-layouts: 6.8 us -> 11.9 us
    pallas_call x0 -> x1, Pallas kernels: none -> 12.3 us  [migrate(): pl.pallas_call(migrate_kernel, out_shape=jax.ShapeDtypeStruct(leaving.sha...]
    ppermute x4 -> x0, starting transfers between devices: 9.99 us -> none  [passed_along(): return lax.ppermute(block, axis, route)]
    unnamed x15 -> x16, local copies, waits for them, and re-layouts: 0.57 us -> 3.64 us
    pallas_call x1, Pallas kernels: 17.4 us -> 14.3 us  [exchange(): pl.pallas_call(functools.partial(exchange_kernel, count_y), out_shape=jax...]
    slice x4 -> x2, local copies, waits for them, and re-layouts: 0.47 us -> 1.68 us  [the longest x1 1.68 us: on_device(): got_values = [got[:, 0, :half], got[:, 0, half:], got[:, 1, :half]]]
    another operation x2 -> x7, other arithmetic: 0.96 us -> 1.84 us
    concatenate x1, local copies, waits for them, and re-layouts: 0.01 us -> 0.78 us  [on_device(): jnp.concatenate([speeds[:, 4 * MOVERS:]] + [received[1] for received in a...]
    convert_element_type x3 -> x1, other arithmetic: 1.61 us -> 1.17 us  [on_device(): got_pixel = got[:, 1, half:].astype(jnp.int32).reshape(1, devices * half)]
  transfers between devices with their start and end apart: 4 -> 0, of which waited for: 0 -> 0; matrix products, arithmetic and copies ran while one was open for 13% -> 0% of each run, Pallas kernels for 0% -> 0%
where the time goes in v5:
time: 54.9 us; the launch traced here: 54.3 us
  Pallas kernels  26.6 us (48%)
  local copies, waits for them, and re-layouts  11.9 us (22%)
  other arithmetic  11.1 us (20%)
  matrix products  3.64 us (7%)
  between operations  0.97 us (2%)
    pallas_call x1, Pallas kernels, exchange(): pl.pallas_call(functools.partial(exchange_kernel, count_y), out_shape=jax...  14.3 us
    pallas_call x1, Pallas kernels, migrate(): pl.pallas_call(migrate_kernel, out_shape=jax.ShapeDtypeStruct(leaving.sha...  12.3 us
    unnamed x16, local copies, waits for them, and re-layouts  3.64 us
    dot_general x1, matrix products, on_device(): lax.dot_general(row_hits, spread, (((1,), (1,)), ((), ())), preferred_ele...  2.68 us
    slice x1, local copies, waits for them, and re-layouts, on_device(): got_values = [got[:, 0, :half], got[:, 0, half:], got[:, 1, :half]]  1.68 us
    sort x1, other arithmetic, on_device(): chosen = jnp.argsort(ranking)[:CROSS_MAX]  1.61 us
    gather x1, local copies, waits for them, and re-layouts, on_device(): speeds = jnp.take(speeds, ordering, axis=1)  1.37 us
    reduce_sum x1, other arithmetic, on_device(): rank = jnp.sum(same.astype(jnp.int32), axis=2)  1.34 us

profile of v5, /device:TPU:1, one launch (start us, length us, event | category | flops | bytes accessed | tf_op | source)
XLA Modules:
  0.0 54.3 jit_solution(834134941662958092)
XLA Ops:
  0.6 0.0 copy-start
  0.7 0.8 %copy-done = s32[3,2560]{1,0:T(4,128)S(1)} copy-done((s32[3,2560]{1,0:T(4,128)S(1)}, s32[3,2560]{1,0:T(4,128)}, u32[]{:S(2)}) %copy-start) | copy-done | bytes 30744
  1.4 0.7 %compare_and_fusion = pred[20]{0:T(512)(128)(4,1)S(1)} fusion(s32[1,20]{1,0:T(1,128)} %param.20), kind=kLoop, calls=%fused_computation.119 | loop fusion | flops 120 | bytes 100 | tf_op jit(solution)/shard_map/jit(_take)/and | solution.py:141
  2.1 0.7 %compare_select_fusion = s32[20]{0:T(128)S(1)} fusion(s32[1,20]{1,0:T(1,128)} %param.20), kind=kLoop, calls=%fused_computation.112 | loop fusion | flops 60 | bytes 160 | tf_op jit(solution)/shard_map/jit(_take)/jit(_where)/select_n | solution.py:141
  2.7 0.7 %iota_add_fusion = s32[20]{0:T(128)S(1)} fusion(s32[1,20]{1,0:T(1,128)} %param.21), kind=kLoop, calls=%fused_computation.127 | loop fusion | flops 60 | bytes 160 | tf_op jit(solution)/shard_map/add | solution.py:167
  3.4 1.6 %sort.17 = (s32[20]{0:T(128)}, s32[20]{0:T(128)S(1)}) sort(s32[20]{0:T(128)S(1)} %iota_add_fusion, s32[20]{0:T(128)S(1)} %iota.41), dimensions={0}, to_apply=%region_0.0 | sort | flops 100 | bytes 320 | tf_op jit(solution)/shard_map/jit(argsort)/sort | solution.py:168
  5.0 0.1 broadcast_bitcast_fusion.1
  5.1 0.7 %convert_element_type.83 = f32[3,3]{1,0:T(4,128)S(1)} convert(s32[3,3]{1,0:T(4,128)} %param.22) | non-fusion elementwise | flops 9 | bytes 72 | tf_op jit(solution)/shard_map/convert_element_type | solution.py:181
  5.8 1.3 %gather_fusion.1 = s32[5]{0:T(128)S(1)} fusion(s32[20]{0:T(128)} %bitcast.103, s32[1024]{0:T(1024)S(1)} %get-tuple-element.106), kind=kCustom, calls=%fused_computation.5 | custom fusion | bytes 60 | tf_op jit(solution)/shard_map/jit(_take)/gather | solution.py:169
  7.1 0.1 broadcast_bitcast_fusion
  7.2 0.6 %gather_fusion = s32[5,3,128]{2,1,0:T(4,128)S(1)} fusion(s32[3,20,128]{2,0,1:T(4,128)S(1)} %bitcast.102, s32[1024]{0:T(1024)S(1)} %get-tuple-element.106), kind=kCustom, calls=%fused_computation.4 | custom fusion | bytes 15380 | tf_op jit(solution)/shard_map/jit(_take)/gather | solution.py:172
  7.8 1.4 %gather_fusion.3 = f32[20,3,128]{2,1,0:T(4,128)S(1)} fusion(f32[3,20,128]{2,0,1:T(4,128)} %bitcast.110, s32[1024]{0:T(1024)S(1)} %get-tuple-element.107), kind=kCustom, calls=%fused_computation.2.clone | custom fusion | bytes 61520 | tf_op jit(solution)/shard_map/jit(_take)/gather | solution.py:142
  9.2 0.8 %bitcast_add_fusion = f32[3,20,128]{2,0,1:T(4,128)S(1)} fusion(f32[3,2560]{1,0:T(4,128)} %param.18, f32[3,2560]{1,0:T(4,128)} %param.19), kind=kLoop, calls=%fused_computation.44 | loop fusion | flops 15360 | bytes 92160 | tf_op jit(solution)/shard_map/add | solution.py:139
  10.0 0.6 %gather_fusion.2 = f32[20,3,128]{2,1,0:T(4,128)S(1)} fusion(f32[3,20,128]{2,0,1:T(4,128)S(1)} %bitcast_add_fusion, s32[1024]{0:T(1024)S(1)} %get-tuple-element.107), kind=kCustom, calls=%fused_computation.clone | custom fusion | bytes 61520 | tf_op jit(solution)/shard_map/jit(_take)/gather | solution.py:141
  10.6 0.1 select_bitcast_fusion
  11.0 0.6 %pad_maximum_fusion.1.send_ref = f32[4,6,256]{2,1,0:T(8,128)} fusion(f32[1,6,256]{2,1,0:T(8,128)S(1)} %maximum_bitcast_fusion.4, f32[1,6,256]{2,1,0:T(8,128)S(1)} %maximum_bitcast_fusion.3, f32[1,6,256]{2,1,0:T(8,128)S(1)} %maximum_bitcast_fusion.2, f32[1,6,256]{2,1,0:T(8,128)S(1)} %maximum_bitcast_fusion.1), kind=kLoop, calls=%fused_computation.47 | loop fusion | flops 18432 | bytes 49152 | tf_op jit(solution)/shard_map/stack | solution.py:150
  11.6 12.3 %shard_map.85 = f32[4,6,256]{2,1,0:T(8,128)} custom-call(f32[4,6,256]{2,1,0:T(8,128)} %pad_maximum_fusion.1.send_ref), custom_call_target="tpu_custom_call" | custom-call | tf_op jit(solution)/shard_map/pallas_call | solution.py:94
  23.9 0.8 %constant_dynamic-update-slice_fusion.7 = (f32[3,20,128]{2,0,1:T(4,128)S(1)}, f32[3,20,128]{2,0,1:T(4,128)S(1)}) fusion(f32[3,20,128]{2,0,1:T(4,128)S(1)} %slice_dynamic-update-slice_fusion, f32[4,6,2,128]{3,1,2,0:T(8,128)} %bitcast.111, f32[3,20,128]{2,0,1:T(4,128)S(1)} %slice_dynamic-update-slice_fusion.1), kind=kLoop, calls=%fused_computation.63 | loop fusion | bytes 14336
  24.7 0.8 %constant_dynamic-update-slice_fusion.6 = (f32[3,20,128]{2,0,1:T(4,128)S(1)}, f32[3,20,128]{2,0,1:T(4,128)S(1)}) fusion(f32[3,20,128]{2,0,1:T(4,128)S(1)} %get-tuple-element.94, f32[4,6,2,128]{3,1,2,0:T(8,128)} %bitcast.112, f32[3,20,128]{2,0,1:T(4,128)S(1)} %get-tuple-element.95), kind=kLoop, calls=%fused_computation.62 | loop fusion | bytes 14336
  25.4 0.8 %constant_dynamic-update-slice_fusion.5 = (f32[3,20,128]{2,0,1:T(4,128)S(1)}, f32[3,20,128]{2,0,1:T(4,128)S(1)}) fusion(f32[3,20,128]{2,0,1:T(4,128)S(1)} %get-tuple-element.92, f32[4,6,2,128]{3,1,2,0:T(8,128)} %bitcast.113, f32[3,20,128]{2,0,1:T(4,128)S(1)} %get-tuple-element.93), kind=kLoop, calls=%fused_computation.61 | loop fusion | bytes 14336
  26.2 0.8 %constant_dynamic-update-slice_fusion.4 = (f32[3,20,128]{2,0,1:T(4,128)S(1)}, f32[3,20,128]{2,0,1:T(4,128)S(1)}) fusion(f32[3,20,128]{2,0,1:T(4,128)S(1)} %get-tuple-element.90, f32[4,6,2,128]{3,1,2,0:T(8,128)} %bitcast.114, f32[3,20,128]{2,0,1:T(4,128)S(1)} %get-tuple-element.91), kind=kLoop, calls=%fused_computation.60 | loop fusion | bytes 14336 | tf_op jit(solution)/shard_map/concatenate | solution.py:158
  27.0 0.0 copy-start.1
  27.0 0.0 copy-start.2
  27.0 0.6 %gather_fusion.5 = f32[5,3,128]{2,1,0:T(4,128)S(1)} fusion(f32[3,20,128]{2,0,1:T(4,128)S(1)} %get-tuple-element.88, s32[1024]{0:T(1024)S(1)} %get-tuple-element.106), kind=kCustom, calls=%fused_computation.3.clone | custom fusion | bytes 15380 | tf_op jit(solution)/shard_map/jit(_take)/gather | solution.py:171
  27.6 0.1 multiply_reduce_fusion
  27.7 0.6 %gather_fusion.4 = f32[5,3,128]{2,1,0:T(4,128)S(1)} fusion(f32[3,20,128]{2,0,1:T(4,128)S(1)} %get-tuple-element.89, s32[1024]{0:T(1024)S(1)} %get-tuple-element.106), kind=kCustom, calls=%fused_computation.1.clone | custom fusion | bytes 15380 | tf_op jit(solution)/shard_map/jit(_take)/gather | solution.py:170
  28.3 0.1 select_bitcast_fusion.3
  28.4 0.1 fusion.12
  28.6 0.1 iota_compare_fusion.3
  28.8 1.3 %convert_reduce_fusion = s32[3,640]{1,0:T(4,128)S(1)} fusion(s32[3,640]{1,0:T(4,128)S(1)} %add_select_fusion.5, pred[640,640]{1,0:T(8,128)(4,1)S(1)} %iota_compare_fusion.3), kind=kLoop, calls=%fused_computation.12 | loop fusion | flops 4913280 | bytes 424960 | tf_op jit(solution)/shard_map/reduce_sum | solution.py:191
  30.2 0.1 mul.141
  30.3 1.0 %fusion.7 = f32[3,128,100]{1,2,0:T(8,128)S(1)} fusion(bf16[3,640,100]{1,2,0:T(8,128)(2,1)S(1)} %mul.141, s32[3,640]{1,0:T(4,128)S(1)} %add_select_fusion.5), kind=kOutput, calls=%fused_computation.21 | convolution fusion | flops 49397760 | bytes 545280 | tf_op jit(solution)/shard_map/dot_general | solution.py:204
  31.3 0.0 copy-done.1
  31.3 0.0 copy-done.2
  31.3 0.1 copy.56
  31.4 0.1 copy.59
  31.5 0.1 copy.58
  31.6 0.1 copy.57
  31.7 0.1 select_maximum_fusion.1
  31.8 0.1 copy.60
  31.9 0.1 select_maximum_fusion
  32.0 0.8 %pad_maximum_fusion.send_ref = f32[128,2,128]{2,1,0:T(2,128)} fusion(f32[128,1,128]{2,1,0:T(1,128)S(1)} %bitcast.109, f32[128,1,128]{2,1,0:T(1,128)S(1)} %bitcast.108), kind=kLoop, calls=%fused_computation.27 | loop fusion | flops 32768 | bytes 262144 | tf_op jit(solution)/shard_map/stack | solution.py:212
  32.8 14.3 %shard_map.86 = f32[128,2,128]{2,1,0:T(2,128)} custom-call(f32[128,2,128]{2,1,0:T(2,128)} %pad_maximum_fusion.send_ref), custom_call_target="tpu_custom_call" | custom-call | tf_op jit(solution)/shard_map/pallas_call | solution.py:110
  47.1 1.2 %convert_reduce_fusion.1 = s32[128,64]{1,0:T(8,128)S(1)} fusion(f32[128,2,128]{2,1,0:T(2,128)} %shard_map.86), kind=kLoop, calls=%fused_computation.35 | loop fusion | flops 8192 | bytes 65536 | tf_op jit(solution)/shard_map/convert_element_type | solution.py:221
  48.3 0.1 convert_element_type.90
  48.4 1.7 %slice_reduce_fusion.2 = (bf16[128,64]{1,0:T(8,128)(2,1)S(1)}, bf16[128,64]{1,0:T(8,128)(2,1)S(1)}, bf16[128,64]{1,0:T(8,128)(2,1)S(1)}) fusion(f32[128,2,128]{2,1,0:T(2,128)} %shard_map.86), kind=kLoop, calls=%fused_computation.34 | loop fusion | bytes 147456 | tf_op jit(solution)/shard_map/slice | solution.py:220
  50.1 0.1 broadcast_in_dim.95
  50.2 0.1 broadcast_in_dim.100
  50.3 0.1 broadcast_in_dim.98
  50.4 1.2 %select_convert_fusion.2 = (bf16[128,8192]{1,0:T(8,128)(2,1)S(1)}, bf16[128,8192]{1,0:T(8,128)(2,1)S(1)}, bf16[128,8192]{1,0:T(8,128)(2,1)S(1)}) fusion(bf16[8192]{0:T(1024)(128)(2,1)S(1)} %broadcast_in_dim.95, s32[8192]{0:T(1024)S(1)} %get-tuple-element.84, bf16[8192]{0:T(1024)(128)(2,1)S(1)} %broadcast_in_dim.100, bf16[8192]{0:T(1024)(128)(2,1)S(1)} %broadcast_in_dim.98), kind=kLoop, calls=%fused_computation.15 | loop fusion | flops 4194304 | bytes 6373376 | tf_op jit(solution)/shard_map/convert
  51.6 2.7 %fusion = f32[64,384]{1,0:T(8,128)} fusion(bf16[128,8192]{1,0:T(8,128)(2,1)S(1)} %get-tuple-element.86, bf16[128,8192]{1,0:T(8,128)(2,1)S(1)} %get-tuple-element.87, bf16[128,8192]{1,0:T(8,128)(2,1)S(1)} %get-tuple-element.85, s32[8192]{0:T(1024)S(1)} %get-tuple-element.83), kind=kOutput, calls=%fused_computation.6 | convolution fusion | flops 422051840 | bytes 6422528 | tf_op jit(solution)/shard_map/dot_general | solution.py:229
  (38 shorter events, 0.6 us)
Async XLA Ops:
  0.6 0.8 %copy-start = (s32[3,2560]{1,0:T(4,128)S(1)}, s32[3,2560]{1,0:T(4,128)}, u32[]{:S(2)}) copy-start(s32[3,2560]{1,0:T(4,128)} %param.23) | copy-start | bytes 92164
  27.0 4.3 %copy-start.1 = (f32[3,20,128]{2,0,1:T(4,128)}, f32[3,20,128]{2,0,1:T(4,128)S(1)}, u32[]{:S(2)}) copy-start(f32[3,20,128]{2,0,1:T(4,128)S(1)} %get-tuple-element.88) | copy-start | bytes 92164
  27.0 4.3 %copy-start.2 = (f32[3,20,128]{2,0,1:T(4,128)}, f32[3,20,128]{2,0,1:T(4,128)S(1)}, u32[]{:S(2)}) copy-start(f32[3,20,128]{2,0,1:T(4,128)S(1)} %get-tuple-element.89) | copy-start | bytes 92164

commit v6 on v4

--- a/solution.py
+++ b/solution.py
@@ -1,5 +1,3 @@
-import functools
-
 import jax
 import jax.numpy as jnp
 from jax import lax
@@ -18,61 +16,86 @@
 MESH = pl.DeviceIdType.MESH
 
 
-def exchange_kernel(count_y, send_ref, out_ref, recv, send_sem, recv_sem):
-    devices = send_ref.shape[0]
-    me = lax.axis_index("gx") * count_y + lax.axis_index("gy")
-
-    def peer(offset):
-        other = lax.rem(me + offset, devices)
-        return other, (other // count_y, other % count_y)
-
+def exchange_kernel(send_ref, out_ref, middle, recv, send_sems, recv_sems):
+    count_x, count_y = send_ref.shape[0], send_ref.shape[1]
+    x = lax.axis_index("gx")
+    y = lax.axis_index("gy")
     barrier = pltpu.get_barrier_semaphore()
 
-    def greet(offset, carry):
-        pl.semaphore_signal(barrier, 1, device_id=peer(offset)[1], device_id_type=MESH)
-        return carry
-
-    lax.fori_loop(1, devices, greet, 0)
-    pl.semaphore_wait(barrier, devices - 1)
-    pltpu.make_async_copy(send_ref.at[me], recv.at[me], recv_sem).start()
-
-    def post(offset, carry):
-        other, where = peer(offset)
+    def greet_y(offset, carry):
+        where = (x, lax.rem(y + offset, count_y))
+        pl.semaphore_signal(barrier, 1, device_id=where, device_id_type=MESH)
+        return carry
+
+    def greet_x(offset, carry):
+        where = (lax.rem(x + offset, count_x), y)
+        pl.semaphore_signal(barrier, 1, device_id=where, device_id_type=MESH)
+        return carry
+
+    lax.fori_loop(1, count_y, greet_y, 0)
+    lax.fori_loop(1, count_x, greet_x, 0)
+    pl.semaphore_wait(barrier, count_x + count_y - 2)
+
+    pltpu.make_async_copy(send_ref.at[:, y], middle.at[y], recv_sems.at[0]).start()
+
+    def post_y(offset, carry):
+        other = lax.rem(y + offset, count_y)
         pltpu.make_async_remote_copy(
-            src_ref=send_ref.at[other],
-            dst_ref=recv.at[me],
-            send_sem=send_sem,
-            recv_sem=recv_sem,
-            device_id=where,
+            src_ref=send_ref.at[:, other],
+            dst_ref=middle.at[y],
+            send_sem=send_sems.at[0],
+            recv_sem=recv_sems.at[0],
+            device_id=(x, other),
             device_id_type=MESH,
         ).start()
         return carry
 
-    lax.fori_loop(1, devices, post, 0)
+    lax.fori_loop(1, count_y, post_y, 0)
+    pltpu.make_async_copy(middle, middle, recv_sems.at[0]).wait()
+
+    pltpu.make_async_copy(middle.at[:, x], recv.at[x], recv_sems.at[1]).start()
+
+    def post_x(offset, carry):
+        other = lax.rem(x + offset, count_x)
+        pltpu.make_async_remote_copy(
+            src_ref=middle.at[:, other],
+            dst_ref=recv.at[x],
+            send_sem=send_sems.at[1],
+            recv_sem=recv_sems.at[1],
+            device_id=(other, y),
+            device_id_type=MESH,
+        ).start()
+        return carry
+
+    lax.fori_loop(1, count_x, post_x, 0)
+    pltpu.make_async_copy(recv, recv, recv_sems.at[1]).wait()
     pltpu.make_async_copy(
-        send_ref.at[pl.ds(0, devices - 1)], recv.at[pl.ds(0, devices - 1)], send_sem
+        middle.at[pl.ds(0, count_y - 1)], middle.at[pl.ds(0, count_y - 1)], send_sems.at[0]
     ).wait()
-    pltpu.make_async_copy(send_ref, recv, recv_sem).wait()
-
+    pltpu.make_async_copy(
+        recv.at[pl.ds(0, count_x - 1)], recv.at[pl.ds(0, count_x - 1)], send_sems.at[1]
+    ).wait()
     out_ref[...] = recv[...]
 
 
-def exchange(send, count_y):
+def exchange(send, count_x, count_y):
     devices = send.shape[0]
-    return pl.pallas_call(
-        functools.partial(exchange_kernel, count_y),
-        out_shape=jax.ShapeDtypeStruct(send.shape, jnp.float32),
+    grid = send.reshape(count_x, count_y, *send.shape[1:])
+    middle = (count_y, count_x) + send.shape[1:]
+    got = pl.pallas_call(
+        exchange_kernel,
+        out_shape=jax.ShapeDtypeStruct(grid.shape, jnp.float32),
         in_specs=[pl.BlockSpec(memory_space=pltpu.VMEM)],
         out_specs=pl.BlockSpec(memory_space=pltpu.VMEM),
         scratch_shapes=[
-            pltpu.VMEM(send.shape, jnp.float32),
-            pltpu.SemaphoreType.DMA(()),
-            pltpu.SemaphoreType.DMA(()),
+            pltpu.VMEM(middle, jnp.float32),
+            pltpu.VMEM(grid.shape, jnp.float32),
+            pltpu.SemaphoreType.DMA((2,)),
+            pltpu.SemaphoreType.DMA((2,)),
         ],
         compiler_params=pltpu.CompilerParams(collective_id=0, has_side_effects=True),
-    )(send)
-
-
+    )(grid)
+    return got.reshape(send.shape)
 def passed_along(block, axis, distance):
     devices = range(lax.axis_size(axis))
     route = [((i - distance) % len(devices), i) for i in devices]
@@ -179,7 +202,7 @@
         ],
         axis=1,
     )
-    got = exchange(send, count_y)
+    got = exchange(send, count_x, count_y)
     got_values = jnp.stack([got[:, 0, :half], got[:, 0, half:], got[:, 1, :half]], axis=1)
     got_values = got_values.reshape(devices, 3, half).transpose(0, 2, 1).reshape(devices * half, 3)
     got_pixel = got[:, 1, half:].reshape(devices * half).astype(jnp.int32)

time: 50.5 us -> 48.3 us (0.956)
  other arithmetic: 11.2 us -> 9.04 us
  local copies, waits for them, and re-layouts: 6.8 us -> 7.78 us
  Pallas kernels: 17.4 us -> 16.5 us
    reshape x0 -> x2, local copies, waits for them, and re-layouts: none -> 1.83 us  [exchange(): return got.reshape(send.shape)]
    convert_element_type x1, other arithmetic: 1.17 us -> 0.08 us  [on_device(): got_pixel = got[:, 1, half:].reshape(devices * half).astype(jnp.int32)]
    another operation x2 -> x1, other arithmetic: 0.96 us -> 0.01 us
    pallas_call x1, Pallas kernels: 17.4 us -> 16.5 us  [exchange(): pl.pallas_call(exchange_kernel, out_shape=jax.ShapeDtypeStruct(grid.shape...]
  transfers between devices with their start and end apart: 4 -> 4, of which waited for: 0 -> 0; matrix products, arithmetic and copies ran while one was open for 13% -> 14% of each run, Pallas kernels for 0% -> 0%
where the time goes in v6:
time: 48.3 us; the launch traced here: 47.9 us
  Pallas kernels  16.5 us (34%)
  starting transfers between devices  9.99 us (21%)
  other arithmetic  9.04 us (19%)
  local copies, waits for them, and re-layouts  7.78 us (16%)
  matrix products  3.64 us (8%)
  between operations  1 us (2%)
    pallas_call x1, Pallas kernels, exchange(): pl.pallas_call(exchange_kernel, out_shape=jax.ShapeDtypeStruct(grid.shape...  16.5 us
    ppermute x4, starting transfers between devices, passed_along(): return lax.ppermute(block, axis, route)  9.99 us
    dot_general x1, matrix products, on_device(): maps = jnp.dot(row_hits, spread, preferred_element_type=jnp.float32)  2.68 us
    reshape x2, local copies, waits for them, and re-layouts, exchange(): return got.reshape(send.shape)  1.83 us
    sort x1, other arithmetic, on_device(): chosen = jnp.argsort(ranking)[:CROSS_MAX]  1.61 us
    gather x1, local copies, waits for them, and re-layouts, on_device(): speeds = jnp.take(speeds, ordering, axis=1)  1.37 us
    reduce_sum x1, other arithmetic, on_device(): rank = jnp.sum(same.astype(jnp.int32), axis=2)  1.34 us
    gather x1, local copies, waits for them, and re-layouts, on_device(): jnp.take(flag_row, chosen).astype(jnp.float32).reshape(1, CROSS_MAX, 1)  1.3 us
  transfers between devices with their start and end apart: 4, of which 0 were waited for; matrix products, arithmetic and copies ran while one was open for 14% of the time, Pallas kernels for 0%

profile of v6, /device:TPU:1, one launch (start us, length us, event | category | flops | bytes accessed | tf_op | source)
XLA Modules:
  0.0 47.9 jit_solution(5156107112289852807)
XLA Ops:
  0.6 0.0 copy-start
  0.6 0.7 %compare_and_fusion = pred[20]{0:T(512)(128)(4,1)S(1)} fusion(s32[1,20]{1,0:T(1,128)} %param.20), kind=kLoop, calls=%fused_computation.107 | loop fusion | flops 120 | bytes 100 | tf_op jit(solution)/shard_map/jit(_take)/and | solution.py:122
  1.3 0.7 %compare_select_fusion = s32[20]{0:T(128)S(1)} fusion(s32[1,20]{1,0:T(1,128)} %param.20), kind=kLoop, calls=%fused_computation.100 | loop fusion | flops 60 | bytes 160 | tf_op jit(solution)/shard_map/jit(_take)/jit(_where)/select_n | solution.py:122
  2.0 0.8 %bitcast_add_fusion = f32[3,20,128]{2,0,1:T(4,128)S(1)} fusion(f32[3,2560]{1,0:T(4,128)} %param.18, f32[3,2560]{1,0:T(4,128)} %param.19), kind=kLoop, calls=%fused_computation.35 | loop fusion | flops 15360 | bytes 92160 | tf_op jit(solution)/shard_map/add | solution.py:120
  2.8 1.4 %gather_fusion.3 = f32[20,3,128]{2,1,0:T(4,128)S(1)} fusion(f32[3,20,128]{2,0,1:T(4,128)} %bitcast.81, s32[1024]{0:T(1024)S(1)} %pad_clamp_fusion.1), kind=kCustom, calls=%fused_computation.2.clone | custom fusion | bytes 61520 | tf_op jit(solution)/shard_map/jit(_take)/gather | solution.py:123
  4.2 0.6 %gather_fusion.2 = f32[20,3,128]{2,1,0:T(4,128)S(1)} fusion(f32[3,20,128]{2,0,1:T(4,128)S(1)} %bitcast_add_fusion, s32[1024]{0:T(1024)S(1)} %pad_clamp_fusion.1), kind=kCustom, calls=%fused_computation.clone | custom fusion | bytes 61520 | tf_op jit(solution)/shard_map/jit(_take)/gather | solution.py:122
  4.8 0.1 select_bitcast_fusion
  4.9 1.5 %collective-permute-start.3 = (f32[6,2,128]{2,0,1:T(8,128)S(1)}, f32[6,2,128]{2,0,1:T(8,128)S(1)}, u32[]{:S(2)}, u32[]{:S(2)}) collective-permute-start(f32[6,2,128]{2,0,1:T(8,128)S(1)} %pad_maximum_fusion.6), channel_id=1, source_target_pairs={{1,0},{2,1},{3,2},{4,3},{5,4},{6,5},{7,6},{8,7},{9,8},{10,9},{11,1... | collective-permute-start | bytes 18440 | tf_op jit(solution)/shard_map/ppermute | solution.py:102
  6.5 4.9 %collective-permute-start.1 = (f32[6,2,128]{2,0,1:T(8,128)S(1)}, f32[6,2,128]{2,0,1:T(8,128)S(1)}, u32[]{:S(2)}, u32[]{:S(2)}) collective-permute-start(f32[6,2,128]{2,0,1:T(8,128)S(1)} %pad_maximum_fusion.4), channel_id=1, source_target_pairs={{16,0},{32,16},{48,32},{64,48},{80,64},{96,80},{112,96},{0,112},{1... | collective-permute-start | bytes 18440 | tf_op jit(solution)/shard_map/ppermute | solution.py:102
  11.4 0.1 collective-permute-start
  11.6 3.5 %collective-permute-start.2 = (f32[6,2,128]{2,0,1:T(8,128)S(1)}, f32[6,2,128]{2,0,1:T(8,128)S(1)}, u32[]{:S(2)}, u32[]{:S(2)}) collective-permute-start(f32[6,2,128]{2,0,1:T(8,128)S(1)} %pad_maximum_fusion.5), channel_id=1, source_target_pairs={{15,0},{0,1},{1,2},{2,3},{3,4},{4,5},{5,6},{6,7},{7,8},{8,9},{9,10... | collective-permute-start | bytes 18440 | tf_op jit(solution)/shard_map/ppermute | solution.py:102
  15.1 0.7 %iota_add_fusion = s32[20]{0:T(128)S(1)} fusion(s32[1,20]{1,0:T(1,128)} %param.21), kind=kLoop, calls=%fused_computation.115 | loop fusion | flops 60 | bytes 160 | tf_op jit(solution)/shard_map/add | solution.py:153
  15.7 1.6 %sort.17 = (s32[20]{0:T(128)}, s32[20]{0:T(128)S(1)}) sort(s32[20]{0:T(128)S(1)} %iota_add_fusion, s32[20]{0:T(128)S(1)} %iota.44), dimensions={0}, to_apply=%region_0.0 | sort | flops 100 | bytes 320 | tf_op jit(solution)/shard_map/jit(argsort)/sort | solution.py:154
  17.4 0.1 broadcast_bitcast_fusion.1
  17.4 0.0 copy-done
  17.4 0.6 %gather_fusion = s32[5,3,128]{2,1,0:T(4,128)S(1)} fusion(s32[3,20,128]{2,0,1:T(4,128)S(1)} %bitcast.73, s32[1024]{0:T(1024)S(1)} %pad_clamp_fusion), kind=kCustom, calls=%fused_computation.4 | custom fusion | bytes 15380 | tf_op jit(solution)/shard_map/jit(_take)/gather | solution.py:158
  18.1 0.1 iota_compare_fusion.3
  18.2 1.3 %gather_fusion.1 = s32[5]{0:T(128)S(1)} fusion(s32[20]{0:T(128)} %bitcast.74, s32[1024]{0:T(1024)S(1)} %pad_clamp_fusion), kind=kCustom, calls=%fused_computation.5 | custom fusion | bytes 60 | tf_op jit(solution)/shard_map/jit(_take)/gather | solution.py:155
  19.6 1.3 %convert_reduce_fusion = s32[3,640]{1,0:T(4,128)S(1)} fusion(s32[3,640]{1,0:T(4,128)S(1)} %add_select_fusion.5, pred[640,640]{1,0:T(8,128)(4,1)S(1)} %iota_compare_fusion.3), kind=kLoop, calls=%fused_computation.6 | loop fusion | flops 4913280 | bytes 424960 | tf_op jit(solution)/shard_map/reduce_sum | solution.py:177
  20.9 0.1 broadcast_bitcast_fusion
  21.0 0.7 %convert_element_type.87 = f32[3,3]{1,0:T(4,128)S(1)} convert(s32[3,3]{1,0:T(4,128)} %param.22) | non-fusion elementwise | flops 9 | bytes 72 | tf_op jit(solution)/shard_map/convert_element_type | solution.py:167
  21.7 0.0 collective-permute-done
  21.7 0.0 collective-permute-done.1
  21.7 0.0 collective-permute-done.2
  21.7 0.0 collective-permute-done.3
  21.8 0.0 copy-start.1
  21.8 0.0 copy-start.2
  21.8 0.6 %gather_fusion.5 = f32[5,3,128]{2,1,0:T(4,128)S(1)} fusion(f32[3,20,128]{2,0,1:T(4,128)S(1)} %get-tuple-element.92, s32[1024]{0:T(1024)S(1)} %pad_clamp_fusion), kind=kCustom, calls=%fused_computation.3.clone | custom fusion | bytes 15380 | tf_op jit(solution)/shard_map/jit(_take)/gather | solution.py:157
  22.4 0.1 multiply_reduce_fusion
  22.5 0.6 %gather_fusion.4 = f32[5,3,128]{2,1,0:T(4,128)S(1)} fusion(f32[3,20,128]{2,0,1:T(4,128)S(1)} %get-tuple-element.93, s32[1024]{0:T(1024)S(1)} %pad_clamp_fusion), kind=kCustom, calls=%fused_computation.1.clone | custom fusion | bytes 15380 | tf_op jit(solution)/shard_map/jit(_take)/gather | solution.py:156
  23.0 0.1 select_bitcast_fusion.3
  23.2 0.1 fusion.9
  23.5 0.1 mul.158
  23.5 1.0 %fusion.3 = f32[3,128,100]{1,2,0:T(8,128)S(1)} fusion(bf16[3,640,100]{1,2,0:T(8,128)(2,1)S(1)} %mul.158, s32[3,640]{1,0:T(4,128)S(1)} %add_select_fusion.5), kind=kOutput, calls=%fused_computation.15 | convolution fusion | flops 49397760 | bytes 545280 | tf_op jit(solution)/shard_map/dot_general | solution.py:190
  24.6 0.1 copy.22
  24.7 0.1 copy.23
  24.8 0.8 %pad_maximum_fusion.send_ref = f32[8,16,2,128]{3,2,1,0:T(2,128)} fusion(f32[8,16,1,128]{3,2,1,0:T(1,128)S(1)} %bitcast.80, f32[8,16,1,128]{3,2,1,0:T(1,128)S(1)} %bitcast.79), kind=kLoop, calls=%fused_computation.21 | loop fusion | flops 32768 | bytes 262144 | tf_op jit(solution)/shard_map/stack | solution.py:198
  25.6 16.5 %shard_map.85 = f32[8,16,2,128]{3,2,1,0:T(2,128)} custom-call(f32[8,16,2,128]{3,2,1,0:T(2,128)} %pad_maximum_fusion.send_ref), custom_call_target="tpu_custom_call" | custom-call | tf_op jit(solution)/shard_map/pallas_call | solution.py:85
  42.1 0.9 %copy.28 = bf16[128,2,128]{2,0,1:T(8,128)(2,1)S(1)} copy(f32[128,2,128]{2,1,0:T(2,128)} %bitcast.76) | data formatting | bytes 196608 | tf_op jit(solution)/shard_map/reshape | solution.py:98
  43.0 0.9 %copy.24 = f32[128,2,128]{2,0,1:T(8,128)S(1)} copy(f32[128,2,128]{2,1,0:T(2,128)} %bitcast.77) | data formatting | bytes 262144 | tf_op jit(solution)/shard_map/reshape | solution.py:98
  43.9 0.1 slice_convert_fusion
  44.0 0.1 convert_element_type.94
  44.1 0.1 fusion.19
  44.2 0.1 convert_element_type.96
  44.4 0.4 fusion
  44.8 0.0 copy-done.1
  44.8 0.0 copy-done.2
  44.8 0.5 broadcast_multiply_fusion
  45.3 2.7 %fusion.1 = f32[64,384]{1,0:T(8,128)} fusion(bf16[8192,384]{0,1:T(8,128)(2,1)S(1)} %bitcast.75, s32[8192]{0:T(1024)S(1)} %get-tuple-element.82), kind=kOutput, calls=%fused_computation.11 | convolution fusion | flops 403177472 | bytes 6422528 | tf_op jit(solution)/shard_map/dot_general | solution.py:216
  (43 shorter events, 0.7 us)
Async XLA Ops:
  0.6 16.8 %copy-start = (s32[3,2560]{1,0:T(4,128)S(1)}, s32[3,2560]{1,0:T(4,128)}, u32[]{:S(2)}) copy-start(s32[3,2560]{1,0:T(4,128)} %param.23) | copy-start | bytes 92164
  4.9 16.8 %collective-permute-start.3 = (f32[6,2,128]{2,0,1:T(8,128)S(1)}, f32[6,2,128]{2,0,1:T(8,128)S(1)}, u32[]{:S(2)}, u32[]{:S(2)}) collective-permute-start(f32[6,2,128]{2,0,1:T(8,128)S(1)} %pad_maximum_fusion.6), channel_id=1, source_target_pairs={{1,0},{2,1},{3,2},{4,3},{5,4},{6,5},{7,6},{8,7},{9,8},{10,9},{11,1... | collective-permute-start | bytes 18440 | tf_op jit(solution)/shard_map/ppermute | solution.py:102
  6.5 15.2 %collective-permute-start.1 = (f32[6,2,128]{2,0,1:T(8,128)S(1)}, f32[6,2,128]{2,0,1:T(8,128)S(1)}, u32[]{:S(2)}, u32[]{:S(2)}) collective-permute-start(f32[6,2,128]{2,0,1:T(8,128)S(1)} %pad_maximum_fusion.4), channel_id=1, source_target_pairs={{16,0},{32,16},{48,32},{64,48},{80,64},{96,80},{112,96},{0,112},{1... | collective-permute-start | bytes 18440 | tf_op jit(solution)/shard_map/ppermute | solution.py:102
  11.4 10.3 %collective-permute-start = (f32[6,2,128]{2,0,1:T(8,128)S(1)}, f32[6,2,128]{2,0,1:T(8,128)S(1)}, u32[]{:S(2)}, u32[]{:S(2)}) collective-permute-start(f32[6,2,128]{2,0,1:T(8,128)S(1)} %pad_maximum_fusion.3), channel_id=1, source_target_pairs={{112,0},{0,16},{16,32},{32,48},{48,64},{64,80},{80,96},{96,112},{1... | collective-permute-start | bytes 18440 | tf_op jit(solution)/shard_map/ppermute | solution.py:102
  11.6 10.2 %collective-permute-start.2 = (f32[6,2,128]{2,0,1:T(8,128)S(1)}, f32[6,2,128]{2,0,1:T(8,128)S(1)}, u32[]{:S(2)}, u32[]{:S(2)}) collective-permute-start(f32[6,2,128]{2,0,1:T(8,128)S(1)} %pad_maximum_fusion.5), channel_id=1, source_target_pairs={{15,0},{0,1},{1,2},{2,3},{3,4},{4,5},{5,6},{6,7},{7,8},{8,9},{9,10... | collective-permute-start | bytes 18440 | tf_op jit(solution)/shard_map/ppermute | solution.py:102
  21.8 23.0 %copy-start.1 = (f32[3,20,128]{2,0,1:T(4,128)}, f32[3,20,128]{2,0,1:T(4,128)S(1)}, u32[]{:S(2)}) copy-start(f32[3,20,128]{2,0,1:T(4,128)S(1)} %get-tuple-element.92) | copy-start | bytes 92164
  21.8 23.0 %copy-start.2 = (f32[3,20,128]{2,0,1:T(4,128)}, f32[3,20,128]{2,0,1:T(4,128)S(1)}, u32[]{:S(2)}) copy-start(f32[3,20,128]{2,0,1:T(4,128)S(1)} %get-tuple-element.93) | copy-start | bytes 92164

commit v7 on v6

--- a/solution.py
+++ b/solution.py
@@ -112,60 +112,34 @@
     ).astype(jnp.bfloat16)
 
 
+def pick(data, hits):
+    chosen = jnp.where(hits[:, :, None], data[..., None, :, :], jnp.zeros((), data.dtype))
+    return jnp.sum(chosen, axis=-2)
+
+
 def on_device(positions, velocities, block_order, flags, offsets, pixels):
     blocks = block_order.shape[1]
     width = positions.shape[1] // blocks
-    places = positions.reshape(3, blocks, width)
-    speeds = velocities.reshape(3, blocks, width)
-    places = places + time_step * speeds
-    ordering = block_order[0]
-    places = jnp.take(places, ordering, axis=1)
-    speeds = jnp.take(speeds, ordering, axis=1)
-
-    def leaving(which_set, component, sign_step):
-        first_block = which_set * MOVERS
-        moved_pos = places[:, first_block : first_block + MOVERS].at[component].add(sign_step)
-        return (moved_pos, speeds[:, first_block : first_block + MOVERS])
-
-    def moved(which_set, component, sign_step, axis, distance):
-        pos, vel = leaving(which_set, component, sign_step)
-        got = passed_along(jnp.concatenate([pos, vel], axis=0), axis, distance)
-        return got[:3], got[3:]
-
-    arrived = (
-        moved(0, 0, -1.0, "gx", 1),
-        moved(1, 0, 1.0, "gx", -1),
-        moved(2, 1, -1.0, "gy", 1),
-        moved(3, 1, 1.0, "gy", -1),
-    )
-    new_places = jnp.concatenate(
-        [places[:, 4 * MOVERS :]] + [received[0] for received in arrived], axis=1
-    )
-    new_speeds = jnp.concatenate(
-        [speeds[:, 4 * MOVERS :]] + [received[1] for received in arrived], axis=1
-    )
+    block_ids = jnp.arange(blocks, dtype=jnp.int32)
+    order_hits = block_order[0][:, None] == block_ids[None, :]
+    places = pick(positions.reshape(3, blocks, width) + time_step * velocities.reshape(3, blocks, width), order_hits)
+    speeds = pick(velocities.reshape(3, blocks, width), order_hits)
+
+    flag_row = flags[0]
+    earlier = block_ids[None, :] <= block_ids[:, None]
+    flagged_upto = jnp.sum(jnp.where(earlier, flag_row[None, :], 0), axis=1)
+    flagged = jnp.sum(flag_row)
+    place = jnp.where(flag_row == 1, flagged_upto - 1, flagged + block_ids - flagged_upto)
+    chosen_hits = place[None, :] == jnp.arange(CROSS_MAX, dtype=jnp.int32)[:, None]
+    live_mask = jnp.sum(jnp.where(chosen_hits, flag_row[None, :], 0), axis=1)
+    live_mask = live_mask.astype(jnp.float32).reshape(1, CROSS_MAX, 1)
+    picked_ids = pick(pixels.reshape(REPLICAS, blocks, width), chosen_hits)
+
     count_x = lax.axis_size("gx")
     count_y = lax.axis_size("gy")
     devices = count_x * count_y
     cell_x = lax.axis_index("gx")
     cell_y = lax.axis_index("gy")
-    flag_row = flags[0]
-    ranking = (1 - flag_row) * blocks + jnp.arange(blocks, dtype=jnp.int32)
-    chosen = jnp.argsort(ranking)[:CROSS_MAX]
-    live_mask = jnp.take(flag_row, chosen).astype(jnp.float32).reshape(1, CROSS_MAX, 1)
-    picked_pos = jnp.take(new_places, chosen, axis=1)
-    picked_vel = jnp.take(new_speeds, chosen, axis=1)
-    picked_ids = jnp.take(pixels.reshape(REPLICAS, blocks, width), chosen, axis=1)
-    global_pos = jnp.stack(
-        [
-            (cell_x.astype(jnp.float32) + picked_pos[0]) / count_x,
-            (cell_y.astype(jnp.float32) + picked_pos[1]) / count_y,
-            picked_pos[2],
-        ],
-        axis=0,
-    )
-    shifted = global_pos[None] + offsets.astype(jnp.float32)[:, :, None, None]
-    values = sky_terms(shifted, picked_vel, live_mask)
 
     strip_size = STRIP_ROWS * lane_count
     per_replica = CROSS_MAX * width
@@ -175,17 +149,42 @@
     order = jnp.arange(per_replica, dtype=jnp.int32)
     same = (dest[:, :, None] == dest[:, None, :]) & (order[None, None, :] < order[None, :, None])
     rank = jnp.sum(same.astype(jnp.int32), axis=2)
+    dest_hits = (dest[:, :, None] == jnp.arange(devices, dtype=jnp.int32)).astype(jnp.bfloat16)
+    rank_hits = (rank[:, :, None] == block_ids).astype(jnp.bfloat16)
+    where_in_strip = jnp.stack(
+        [(inside // lane_count).astype(jnp.bfloat16), (inside % lane_count).astype(jnp.bfloat16)], axis=2
+    )
+
+    def leaving(which_set, component, sign_step):
+        first_block = which_set * MOVERS
+        moved_pos = places[:, first_block : first_block + MOVERS].at[component].add(sign_step)
+        return jnp.concatenate([moved_pos, speeds[:, first_block : first_block + MOVERS]], axis=0)
+
+    outgoing = [leaving(0, 0, -1.0), leaving(1, 0, 1.0), leaving(2, 1, -1.0), leaving(3, 1, 1.0)]
+    outgoing, places, speeds, dest_hits, rank_hits, where_in_strip, live_mask = lax.optimization_barrier(
+        (outgoing, places, speeds, dest_hits, rank_hits, where_in_strip, live_mask)
+    )
+    routes = (("gx", 1), ("gx", -1), ("gy", 1), ("gy", -1))
+    arrived = [passed_along(block, *route) for block, route in zip(outgoing, routes)]
+    new_places = jnp.concatenate([places[:, 4 * MOVERS :]] + [got[:3] for got in arrived], axis=1)
+    new_speeds = jnp.concatenate([speeds[:, 4 * MOVERS :]] + [got[3:] for got in arrived], axis=1)
+    picked_pos = pick(new_places, chosen_hits)
+    picked_vel = pick(new_speeds, chosen_hits)
+    global_pos = jnp.stack(
+        [
+            (cell_x.astype(jnp.float32) + picked_pos[0]) / count_x,
+            (cell_y.astype(jnp.float32) + picked_pos[1]) / count_y,
+            picked_pos[2],
+        ],
+        axis=0,
+    )
+    shifted = global_pos[None] + offsets.astype(jnp.float32)[:, :, None, None]
+    values = sky_terms(shifted, picked_vel, live_mask)
+
     slots = REPLICAS * blocks
     fields = jnp.concatenate(
-        [
-            jnp.transpose(values.reshape(3, REPLICAS, per_replica), (1, 2, 0)),
-            (inside // lane_count).astype(jnp.bfloat16)[:, :, None],
-            (inside % lane_count).astype(jnp.bfloat16)[:, :, None],
-        ],
-        axis=2,
-    )
-    dest_hits = (dest[:, :, None] == jnp.arange(devices, dtype=jnp.int32)).astype(jnp.bfloat16)
-    rank_hits = (rank[:, :, None] == jnp.arange(blocks, dtype=jnp.int32)).astype(jnp.bfloat16)
+        [jnp.transpose(values.reshape(3, REPLICAS, per_replica), (1, 2, 0)), where_in_strip], axis=2
+    )
     placed = (fields[:, :, :, None] * rank_hits[:, :, None, :]).reshape(REPLICAS, per_replica, 5 * blocks)
     send = lax.dot_general(
         dest_hits, placed, (((1,), (1,)), ((0,), (0,))), preferred_element_type=jnp.float32

time: 48.3 us -> 48.9 us (1.012)
  waiting for transfers between devices: 0.01 us -> 3.79 us
  local copies, waits for them, and re-layouts: 7.78 us -> 6.29 us
  Pallas kernels: 16.5 us -> 15.4 us
  starting transfers between devices: 9.99 us -> 8.92 us
  other arithmetic: 9.04 us -> 10.1 us
  matrix products: 3.64 us -> 2.97 us
    gather x6 -> x0, local copies, waits for them, and re-layouts: 4.98 us -> none  [the longest x1 1.37 us: on_device(): speeds = jnp.take(speeds, ordering, axis=1)]
    ppermute x4, waiting for transfers between devices: 0.01 us -> 3.79 us  [passed_along(): return lax.ppermute(block, axis, route)]
    reduce_sum x0 -> x6, other arithmetic: none -> 3.42 us  [the longest x1 1.3 us: on_device(): flagged = jnp.sum(flag_row)]
    eq x0 -> x3, other arithmetic: none -> 2.05 us  [the longest x2 1.31 us: on_device(): place[None, :] == jnp.arange(CROSS_MAX, dtype=jnp.int32)[:, None]]
    sort x1 -> x0, other arithmetic: 1.61 us -> none  [on_device(): chosen = jnp.argsort(ranking)[:CROSS_MAX]]
    reshape x0 -> x3, local copies, waits for them, and re-layouts: none -> 1.61 us  [the longest x1 0.8 us: on_device(): positions.reshape(3, blocks, width)]
    add x3 -> x1, other arithmetic: 1.48 us -> 0.01 us  [on_device(): positions.reshape(3, blocks, width)]
    unnamed x10 -> x2, local copies, waits for them, and re-layouts: 0.07 us -> 1.26 us
  transfers between devices with their start and end apart: 4 -> 4, of which waited for: 0 -> 1; matrix products, arithmetic and copies ran while one was open for 14% -> 2% of each run, Pallas kernels for 0% -> 0%
where the time goes in v7:
time: 48.9 us; the launch traced here: 48.5 us
  Pallas kernels  15.4 us (31%)
  other arithmetic  10.1 us (21%)
  starting transfers between devices  8.92 us (18%)
  local copies, waits for them, and re-layouts  6.29 us (13%)
  waiting for transfers between devices  3.79 us (8%)
  matrix products  2.97 us (6%)
  between operations  1.03 us (2%)
    pallas_call x1, Pallas kernels, exchange(): pl.pallas_call(exchange_kernel, out_shape=jax.ShapeDtypeStruct(grid.shape...  15.4 us
    ppermute x4, starting transfers between devices, passed_along(): return lax.ppermute(block, axis, route)  8.92 us
    ppermute x4, waiting for transfers between devices, passed_along(): return lax.ppermute(block, axis, route)  3.79 us
    dot_general x1, matrix products, on_device(): maps = jnp.dot(row_hits, spread, preferred_element_type=jnp.float32)  2.68 us
    reshape x2, local copies, waits for them, and re-layouts, exchange(): return got.reshape(send.shape)  1.83 us
    reduce_sum x1, other arithmetic, on_device(): rank = jnp.sum(same.astype(jnp.int32), axis=2)  1.32 us
    eq x2, other arithmetic, on_device(): place[None, :] == jnp.arange(CROSS_MAX, dtype=jnp.int32)[:, None]  1.31 us
    reduce_sum x1, other arithmetic, on_device(): flagged = jnp.sum(flag_row)  1.3 us
  transfers between devices with their start and end apart: 4, of which 1 were waited for; matrix products, arithmetic and copies ran while one was open for 2% of the time, Pallas kernels for 0%

profile of v7, /device:TPU:1, one launch (start us, length us, event | category | flops | bytes accessed | tf_op | source)
XLA Modules:
  0.0 48.5 jit_solution(14104551889100947515)
XLA Ops:
  0.6 0.1 iota_compare_fusion.3
  0.8 0.8 %select_reduce_fusion.5 = s32[20]{0:T(128)S(1)} fusion(s32[20]{0:T(128)} %bitcast.88), kind=kLoop, calls=%fused_computation.64 | loop fusion | flops 1180 | bytes 160 | tf_op jit(solution)/shard_map/reduce_sum | solution.py:130
  1.5 1.3 %reduce_sum.114 = s32[]{:T(128)} reduce(s32[1,20]{1,0:T(1,128)} %param.17, s32[]{:T(128)} %constant.174.clone.1), dimensions={0,1}, to_apply=%region_3.4 | reduce | flops 19 | bytes 88 | tf_op jit(solution)/shard_map/reduce_sum | solution.py:131
  2.8 1.3 %fusion.23 = s32[20]{0:T(128)S(1)} fusion(s32[1,20]{1,0:T(1,128)} %param.17, s32[20]{0:T(128)S(1)} %select_reduce_fusion.5, s32[]{:T(128)} %reduce_sum.114), kind=kLoop, calls=%fused_computation.104 | loop fusion | flops 100 | bytes 244 | tf_op jit(solution)/shard_map/eq | solution.py:133
  4.1 0.8 %select_reduce_fusion.6 = s32[5]{0:T(128)S(1)} fusion(s32[20]{0:T(128)} %bitcast.89, s32[20]{0:T(128)S(1)} %fusion.23), kind=kLoop, calls=%fused_computation.92 | loop fusion | flops 295 | bytes 180 | tf_op jit(solution)/shard_map/reduce_sum | solution.py:134
  4.9 0.8 %reshape.581 = f32[3,20,128]{2,1,0:T(8,128)S(1)} reshape(f32[3,2560]{1,0:T(4,128)} %param.15) | data formatting | bytes 61440 | tf_op jit(solution)/shard_map/reshape | solution.py:125
  5.7 0.8 %reshape.580 = f32[3,20,128]{2,1,0:T(8,128)S(1)} reshape(f32[3,2560]{1,0:T(4,128)} %param.14) | data formatting | bytes 61440 | tf_op jit(solution)/shard_map/reshape | solution.py:125
  6.5 0.7 %iota_compare_fusion.9 = pred[20,20]{1,0:T(8,128)(4,1)S(1)} fusion(s32[20]{0:T(128)} %bitcast.86), kind=kLoop, calls=%fused_computation.66 | loop fusion | flops 400 | bytes 480 | tf_op jit(solution)/shard_map/eq | solution.py:124
  7.2 0.8 %broadcast_in_dim.145 = s32[3,20,128]{2,1,0:T(8,128)S(1)} reshape(s32[3,2560]{1,0:T(4,128)} %param.19) | data formatting | bytes 61440 | tf_op jit(solution)/shard_map/jit(_where)/broadcast_in_dim | solution.py:116
  8.0 0.1 select_reduce_fusion.4
  8.2 0.3 fusion.3
  8.6 1.3 %convert_reduce_fusion = s32[3,640]{1,0:T(4,128)S(1)} fusion(s32[3,640]{1,0:T(4,128)S(1)} %add_select_fusion.5, pred[640,640]{1,0:T(8,128)(4,1)S(1)} %iota_compare_fusion.3), kind=kLoop, calls=%fused_computation | loop fusion | flops 4913280 | bytes 424960 | tf_op jit(solution)/shard_map/reduce_sum | solution.py:151
  9.9 0.3 select_reduce_fusion.1
  10.4 1.5 %collective-permute-start.3 = (f32[6,2,128]{2,1,0:T(2,128)S(1)}, f32[6,2,128]{2,1,0:T(2,128)S(1)}, u32[]{:S(2)}, u32[]{:S(2)}) collective-permute-start(f32[6,2,128]{2,1,0:T(2,128)S(1)} %pad_maximum_fusion.7), channel_id=1, source_target_pairs={{1,0},{2,1},{3,2},{4,3},{5,4},{6,5},{7,6},{8,7},{9,8},{10,9},{11,1... | collective-permute-start | bytes 18440 | tf_op jit(solution)/shard_map/ppermute | solution.py:102
  11.9 3.0 %collective-permute-start.2 = (f32[6,2,128]{2,1,0:T(2,128)S(1)}, f32[6,2,128]{2,1,0:T(2,128)S(1)}, u32[]{:S(2)}, u32[]{:S(2)}) collective-permute-start(f32[6,2,128]{2,1,0:T(2,128)S(1)} %pad_maximum_fusion.6), channel_id=1, source_target_pairs={{15,0},{0,1},{1,2},{2,3},{3,4},{4,5},{5,6},{6,7},{7,8},{8,9},{9,10... | collective-permute-start | bytes 18440 | tf_op jit(solution)/shard_map/ppermute | solution.py:102
  14.9 4.5 %collective-permute-start.1 = (f32[6,2,128]{2,1,0:T(2,128)S(1)}, f32[6,2,128]{2,1,0:T(2,128)S(1)}, u32[]{:S(2)}, u32[]{:S(2)}) collective-permute-start(f32[6,2,128]{2,1,0:T(2,128)S(1)} %pad_maximum_fusion.5), channel_id=1, source_target_pairs={{16,0},{32,16},{48,32},{64,48},{80,64},{96,80},{112,96},{0,112},{1... | collective-permute-start | bytes 18440 | tf_op jit(solution)/shard_map/ppermute | solution.py:102
  19.3 0.0 collective-permute-start
  19.3 0.1 broadcast_bitcast_fusion
  19.4 0.7 %convert_element_type.100 = f32[3,3]{1,0:T(4,128)S(1)} convert(s32[3,3]{1,0:T(4,128)} %param.18) | non-fusion elementwise | flops 9 | bytes 72 | tf_op jit(solution)/shard_map/convert_element_type | solution.py:181
  20.1 0.0 collective-permute-done.3
  20.1 0.0 collective-permute-done.2
  20.1 0.0 collective-permute-done.1
  20.1 3.8 %collective-permute-done = f32[6,2,128]{2,1,0:T(2,128)S(1)} collective-permute-done((f32[6,2,128]{2,1,0:T(2,128)S(1)}, f32[6,2,128]{2,1,0:T(2,128)S(1)}, u32[]{:S(2)}, u32[]{:S(2)}) %collective-permute-start) | collective-permute-done | bytes 6176 | tf_op jit(solution)/shard_map/ppermute | solution.py:102
  24.0 0.1 select_reduce_fusion.2
  24.2 0.1 fusion.8
  24.5 0.1 mul.161
  24.6 0.3 fusion.31
  25.0 0.1 copy.24
  25.1 0.1 copy.25
  25.2 0.8 %pad_maximum_fusion.send_ref = f32[8,16,2,128]{3,2,1,0:T(2,128)} fusion(f32[8,16,1,128]{3,2,1,0:T(1,128)S(1)} %bitcast.82, f32[8,16,1,128]{3,2,1,0:T(1,128)S(1)} %bitcast.81), kind=kLoop, calls=%fused_computation.19 | loop fusion | flops 32768 | bytes 262144 | tf_op jit(solution)/shard_map/stack | solution.py:197
  26.0 15.4 %shard_map.85 = f32[8,16,2,128]{3,2,1,0:T(2,128)} custom-call(f32[8,16,2,128]{3,2,1,0:T(2,128)} %pad_maximum_fusion.send_ref), custom_call_target="tpu_custom_call" | custom-call | tf_op jit(solution)/shard_map/pallas_call | solution.py:85
  41.4 0.9 %copy.37 = bf16[128,2,128]{2,0,1:T(8,128)(2,1)S(1)} copy(f32[128,2,128]{2,1,0:T(2,128)} %bitcast.76) | data formatting | bytes 196608 | tf_op jit(solution)/shard_map/reshape | solution.py:98
  42.3 0.9 %copy.26 = f32[128,2,128]{2,0,1:T(8,128)S(1)} copy(f32[128,2,128]{2,1,0:T(2,128)} %bitcast.77) | data formatting | bytes 262144 | tf_op jit(solution)/shard_map/reshape | solution.py:98
  43.3 0.1 fusion.24
  43.4 0.1 convert_element_type.104
  43.5 0.1 slice_convert_fusion
  43.6 0.1 convert_element_type.102
  43.7 0.4 fusion
  44.1 0.6 %copy.39 = f32[1,3,20,128]{3,1,2,0:T(4,128)} copy(f32[1,3,20,128]{3,2,1,0:T(8,128)S(1)} %bitcast.79) | data formatting | bytes 61440
  44.8 0.6 %copy.40 = f32[1,3,20,128]{3,1,2,0:T(4,128)} copy(f32[1,3,20,128]{3,2,1,0:T(8,128)S(1)} %bitcast.80) | data formatting | bytes 61440
  45.4 0.4 broadcast_multiply_fusion
  45.8 2.7 %fusion.1 = f32[64,384]{1,0:T(8,128)} fusion(bf16[8192,384]{0,1:T(8,128)(2,1)S(1)} %bitcast.75, s32[8192]{0:T(1024)S(1)} %get-tuple-element.96), kind=kOutput, calls=%fused_computation.5 | convolution fusion | flops 403177472 | bytes 6422528 | tf_op jit(solution)/shard_map/dot_general | solution.py:215
  (44 shorter events, 0.6 us)
Async XLA Ops:
  10.4 9.7 %collective-permute-start.3 = (f32[6,2,128]{2,1,0:T(2,128)S(1)}, f32[6,2,128]{2,1,0:T(2,128)S(1)}, u32[]{:S(2)}, u32[]{:S(2)}) collective-permute-start(f32[6,2,128]{2,1,0:T(2,128)S(1)} %pad_maximum_fusion.7), channel_id=1, source_target_pairs={{1,0},{2,1},{3,2},{4,3},{5,4},{6,5},{7,6},{8,7},{9,8},{10,9},{11,1... | collective-permute-start | bytes 18440 | tf_op jit(solution)/shard_map/ppermute | solution.py:102
  11.9 8.2 %collective-permute-start.2 = (f32[6,2,128]{2,1,0:T(2,128)S(1)}, f32[6,2,128]{2,1,0:T(2,128)S(1)}, u32[]{:S(2)}, u32[]{:S(2)}) collective-permute-start(f32[6,2,128]{2,1,0:T(2,128)S(1)} %pad_maximum_fusion.6), channel_id=1, source_target_pairs={{15,0},{0,1},{1,2},{2,3},{3,4},{4,5},{5,6},{6,7},{7,8},{8,9},{9,10... | collective-permute-start | bytes 18440 | tf_op jit(solution)/shard_map/ppermute | solution.py:102
  14.9 5.3 %collective-permute-start.1 = (f32[6,2,128]{2,1,0:T(2,128)S(1)}, f32[6,2,128]{2,1,0:T(2,128)S(1)}, u32[]{:S(2)}, u32[]{:S(2)}) collective-permute-start(f32[6,2,128]{2,1,0:T(2,128)S(1)} %pad_maximum_fusion.5), channel_id=1, source_target_pairs={{16,0},{32,16},{48,32},{64,48},{80,64},{96,80},{112,96},{0,112},{1... | collective-permute-start | bytes 18440 | tf_op jit(solution)/shard_map/ppermute | solution.py:102
  19.3 4.6 %collective-permute-start = (f32[6,2,128]{2,1,0:T(2,128)S(1)}, f32[6,2,128]{2,1,0:T(2,128)S(1)}, u32[]{:S(2)}, u32[]{:S(2)}) collective-permute-start(f32[6,2,128]{2,1,0:T(2,128)S(1)} %pad_maximum_fusion.4), channel_id=1, source_target_pairs={{112,0},{0,16},{16,32},{32,48},{48,64},{64,80},{80,96},{96,112},{1... | collective-permute-start | bytes 18440 | tf_op jit(solution)/shard_map/ppermute | solution.py:102

commit v8 on v7

--- a/solution.py
+++ b/solution.py
@@ -76,6 +76,54 @@
         recv.at[pl.ds(0, count_x - 1)], recv.at[pl.ds(0, count_x - 1)], send_sems.at[1]
     ).wait()
     out_ref[...] = recv[...]
+
+
+def migrate_kernel(send_ref, out_ref, recv, send_sem, recv_sem):
+    count_x = lax.axis_size("gx")
+    count_y = lax.axis_size("gy")
+    x = lax.axis_index("gx")
+    y = lax.axis_index("gy")
+    faces = (
+        (lax.rem(x + 1, count_x), y),
+        (lax.rem(x + count_x - 1, count_x), y),
+        (x, lax.rem(y + 1, count_y)),
+        (x, lax.rem(y + count_y - 1, count_y)),
+    )
+    barrier = pltpu.get_barrier_semaphore()
+    for where in faces:
+        pl.semaphore_signal(barrier, 1, device_id=where, device_id_type=MESH)
+    pl.semaphore_wait(barrier, len(faces))
+    copies = []
+    for face, where in enumerate(faces):
+        copy = pltpu.make_async_remote_copy(
+            src_ref=send_ref.at[face],
+            dst_ref=recv.at[face],
+            send_sem=send_sem.at[face],
+            recv_sem=recv_sem.at[face],
+            device_id=where,
+            device_id_type=MESH,
+        )
+        copy.start()
+        copies.append(copy)
+    for copy in copies:
+        copy.wait()
+    out_ref[...] = recv[...]
+
+
+def migrate(leaving):
+    faces = leaving.shape[0]
+    return pl.pallas_call(
+        migrate_kernel,
+        out_shape=jax.ShapeDtypeStruct(leaving.shape, jnp.float32),
+        in_specs=[pl.BlockSpec(memory_space=pltpu.VMEM)],
+        out_specs=pl.BlockSpec(memory_space=pltpu.VMEM),
+        scratch_shapes=[
+            pltpu.VMEM(leaving.shape, jnp.float32),
+            pltpu.SemaphoreType.DMA((faces,)),
+            pltpu.SemaphoreType.DMA((faces,)),
+        ],
+        compiler_params=pltpu.CompilerParams(collective_id=1, has_side_effects=True),
+    )(leaving)
 
 
 def exchange(send, count_x, count_y):
@@ -96,12 +144,6 @@
         compiler_params=pltpu.CompilerParams(collective_id=0, has_side_effects=True),
     )(grid)
     return got.reshape(send.shape)
-def passed_along(block, axis, distance):
-    devices = range(lax.axis_size(axis))
-    route = [((i - distance) % len(devices), i) for i in devices]
-    return lax.ppermute(block, axis, route)
-
-
 def sky_terms(shifted, speeds, live_mask):
     radius = jnp.sum(shifted * shifted, axis=1)
     weight = 1.0 / (1.0 + radius)
@@ -164,8 +206,7 @@
     outgoing, places, speeds, dest_hits, rank_hits, where_in_strip, live_mask = lax.optimization_barrier(
         (outgoing, places, speeds, dest_hits, rank_hits, where_in_strip, live_mask)
     )
-    routes = (("gx", 1), ("gx", -1), ("gy", 1), ("gy", -1))
-    arrived = [passed_along(block, *route) for block, route in zip(outgoing, routes)]
+    arrived = migrate(jnp.stack(outgoing).reshape(4, 6, MOVERS * width)).reshape(4, 6, MOVERS, width)
     new_places = jnp.concatenate([places[:, 4 * MOVERS :]] + [got[:3] for got in arrived], axis=1)
     new_speeds = jnp.concatenate([speeds[:, 4 * MOVERS :]] + [got[3:] for got in arrived], axis=1)
     picked_pos = pick(new_places, chosen_hits)

time: 48.9 us -> 48.7 us (level)
  Pallas kernels: 15.4 us -> 26.2 us
  starting transfers between devices: 8.92 us -> 0 us
  waiting for transfers between devices: 3.79 us -> 0 us
  local copies, waits for them, and re-layouts: 6.29 us -> 7.25 us
  other arithmetic: 10.1 us -> 10.7 us
    pallas_call x0 -> x1, Pallas kernels: none -> 12.3 us  [migrate(): pl.pallas_call(migrate_kernel, out_shape=jax.ShapeDtypeStruct(leaving.sha...]
    ppermute x4 -> x0, starting transfers between devices: 8.92 us -> none  [passed_along(): return lax.ppermute(block, axis, route)]
    ppermute x4 -> x0, waiting for transfers between devices: 3.79 us -> none  [passed_along(): return lax.ppermute(block, axis, route)]
    pallas_call x1, Pallas kernels: 15.4 us -> 13.9 us  [exchange(): pl.pallas_call(exchange_kernel, out_shape=jax.ShapeDtypeStruct(grid.shape...]
    slice x4 -> x5, local copies, waits for them, and re-layouts: 0.01 us -> 0.88 us  [on_device(): got[3:]]
    another operation x1 -> x2, other arithmetic: 0.01 us -> 0.63 us  [the longest x1 0.62 us: on_device(): jnp.stack(outgoing).reshape(4, 6, MOVERS * width)]
  transfers between devices with their start and end apart: 4 -> 0, of which waited for: 1 -> 0; matrix products, arithmetic and copies ran while one was open for 2% -> 0% of each run, Pallas kernels for 0% -> 0%
where the time goes in v8:
time: 48.7 us; the launch traced here: 48.2 us
  Pallas kernels  26.2 us (54%)
  other arithmetic  10.7 us (22%)
  local copies, waits for them, and re-layouts  7.25 us (15%)
  matrix products  2.97 us (6%)
  between operations  1.02 us (2%)
    pallas_call x1, Pallas kernels, exchange(): pl.pallas_call(exchange_kernel, out_shape=jax.ShapeDtypeStruct(grid.shape...  13.9 us
    pallas_call x1, Pallas kernels, migrate(): pl.pallas_call(migrate_kernel, out_shape=jax.ShapeDtypeStruct(leaving.sha...  12.3 us
    dot_general x1, matrix products, on_device(): maps = jnp.dot(row_hits, spread, preferred_element_type=jnp.float32)  2.68 us
    reshape x2, local copies, waits for them, and re-layouts, exchange(): return got.reshape(send.shape)  1.83 us
    reduce_sum x1, other arithmetic, on_device(): rank = jnp.sum(same.astype(jnp.int32), axis=2)  1.32 us
    eq x2, other arithmetic, on_device(): place[None, :] == jnp.arange(CROSS_MAX, dtype=jnp.int32)[:, None]  1.32 us
    reduce_sum x1, other arithmetic, on_device(): flagged = jnp.sum(flag_row)  1.3 us
    unnamed x2, local copies, waits for them, and re-layouts  1.26 us

profile of v8, /device:TPU:1, one launch (start us, length us, event | category | flops | bytes accessed | tf_op | source)
XLA Modules:
  0.0 48.2 jit_solution(8697726070497401694)
XLA Ops:
  0.6 0.8 %reshape.607 = f32[3,20,128]{2,1,0:T(8,128)S(1)} reshape(f32[3,2560]{1,0:T(4,128)} %param.15) | data formatting | bytes 61440 | tf_op jit(solution)/shard_map/reshape | solution.py:167
  1.4 0.8 %reshape.606 = f32[3,20,128]{2,1,0:T(8,128)S(1)} reshape(f32[3,2560]{1,0:T(4,128)} %param.14) | data formatting | bytes 61440 | tf_op jit(solution)/shard_map/reshape | solution.py:167
  2.2 0.7 %iota_compare_fusion.9 = pred[20,20]{1,0:T(8,128)(4,1)S(1)} fusion(s32[20]{0:T(128)} %bitcast.86), kind=kLoop, calls=%fused_computation.67 | loop fusion | flops 400 | bytes 480 | tf_op jit(solution)/shard_map/eq | solution.py:166
  3.0 0.4 select_reduce_fusion.1
  3.4 0.8 %select_reduce_fusion.5 = s32[20]{0:T(128)S(1)} fusion(s32[20]{0:T(128)} %bitcast.88), kind=kLoop, calls=%fused_computation.65 | loop fusion | flops 1180 | bytes 160 | tf_op jit(solution)/shard_map/reduce_sum | solution.py:172
  4.2 1.3 %reduce_sum.114 = s32[]{:T(128)} reduce(s32[1,20]{1,0:T(1,128)} %param.17, s32[]{:T(128)} %constant.174.clone.1), dimensions={0,1}, to_apply=%region_3.4 | reduce | flops 19 | bytes 88 | tf_op jit(solution)/shard_map/reduce_sum | solution.py:173
  5.5 1.3 %fusion.23 = s32[20]{0:T(128)S(1)} fusion(s32[1,20]{1,0:T(1,128)} %param.17, s32[20]{0:T(128)S(1)} %select_reduce_fusion.5, s32[]{:T(128)} %reduce_sum.114), kind=kLoop, calls=%fused_computation.105 | loop fusion | flops 100 | bytes 244 | tf_op jit(solution)/shard_map/eq | solution.py:175
  6.8 0.8 %broadcast_in_dim.145 = s32[3,20,128]{2,1,0:T(8,128)S(1)} reshape(s32[3,2560]{1,0:T(4,128)} %param.19) | data formatting | bytes 61440 | tf_op jit(solution)/shard_map/jit(_where)/broadcast_in_dim | solution.py:158
  7.6 0.1 select_reduce_fusion.4
  7.8 0.1 iota_compare_fusion.3
  8.0 1.3 %convert_reduce_fusion = s32[3,640]{1,0:T(4,128)S(1)} fusion(s32[3,640]{1,0:T(4,128)S(1)} %add_select_fusion.5, pred[640,640]{1,0:T(8,128)(4,1)S(1)} %iota_compare_fusion.3), kind=kLoop, calls=%fused_computation | loop fusion | flops 4913280 | bytes 424960 | tf_op jit(solution)/shard_map/reduce_sum | solution.py:193
  9.3 0.3 fusion.3
  9.6 0.8 %select_reduce_fusion.6 = s32[5]{0:T(128)S(1)} fusion(s32[20]{0:T(128)} %bitcast.89, s32[20]{0:T(128)S(1)} %fusion.23), kind=kLoop, calls=%fused_computation.93 | loop fusion | flops 295 | bytes 180 | tf_op jit(solution)/shard_map/reduce_sum | solution.py:176
  10.5 0.6 %pad_maximum_fusion.1.send_ref = f32[4,6,256]{2,1,0:T(8,128)} fusion(f32[1,6,256]{2,1,0:T(8,128)S(1)} %stack.48, f32[1,6,256]{2,1,0:T(8,128)S(1)} %stack.47, f32[1,6,256]{2,1,0:T(8,128)S(1)} %stack.46, f32[1,6,256]{2,1,0:T(8,128)S(1)} %stack.45), kind=kLoop, calls=%fused_computation.42 | loop fusion | flops 18432 | bytes 49152 | tf_op jit(solution)/shard_map/stack | solution.py:209
  11.1 12.3 %shard_map.85 = f32[4,6,256]{2,1,0:T(8,128)} custom-call(f32[4,6,256]{2,1,0:T(8,128)} %pad_maximum_fusion.1.send_ref), custom_call_target="tpu_custom_call" | custom-call | tf_op jit(solution)/shard_map/pallas_call | solution.py:115
  23.4 0.8 %fusion.27 = (f32[1,3,256]{2,1,0:T(4,128)S(1)}, f32[1,3,256]{2,1,0:T(4,128)S(1)}, f32[1,3,256]{2,1,0:T(4,128)S(1)}, f32[1,3,256]{2,1,0:T(4,128)S(1)}, f32[1,3,25...) fusion(f32[4,6,256]{2,1,0:T(8,128)} %shard_map.85), kind=kLoop, calls=%fused_computation.113 | loop fusion | bytes 49152 | tf_op jit(solution)/shard_map/slice | solution.py:211
  24.4 0.1 select_reduce_fusion.2
  24.6 0.7 %convert_element_type.100 = f32[3,3]{1,0:T(4,128)S(1)} convert(s32[3,3]{1,0:T(4,128)} %param.18) | non-fusion elementwise | flops 9 | bytes 72 | tf_op jit(solution)/shard_map/convert_element_type | solution.py:222
  25.3 0.1 fusion.8
  25.5 0.1 broadcast_bitcast_fusion
  25.7 0.1 mul.161
  25.8 0.3 fusion.28
  26.2 0.1 copy.24
  26.3 0.1 copy.25
  26.4 0.8 %pad_maximum_fusion.send_ref = f32[8,16,2,128]{3,2,1,0:T(2,128)} fusion(f32[8,16,1,128]{3,2,1,0:T(1,128)S(1)} %bitcast.82, f32[8,16,1,128]{3,2,1,0:T(1,128)S(1)} %bitcast.81), kind=kLoop, calls=%fused_computation.19 | loop fusion | flops 32768 | bytes 262144 | tf_op jit(solution)/shard_map/stack | solution.py:238
  27.2 13.9 %shard_map.86 = f32[8,16,2,128]{3,2,1,0:T(2,128)} custom-call(f32[8,16,2,128]{3,2,1,0:T(2,128)} %pad_maximum_fusion.send_ref), custom_call_target="tpu_custom_call" | custom-call | tf_op jit(solution)/shard_map/pallas_call | solution.py:133
  41.1 0.9 %copy.37 = bf16[128,2,128]{2,0,1:T(8,128)(2,1)S(1)} copy(f32[128,2,128]{2,1,0:T(2,128)} %bitcast.76) | data formatting | bytes 196608 | tf_op jit(solution)/shard_map/reshape | solution.py:146
  42.0 0.1 fusion.24
  42.1 0.1 convert_element_type.104
  42.2 0.9 %copy.26 = f32[128,2,128]{2,0,1:T(8,128)S(1)} copy(f32[128,2,128]{2,1,0:T(2,128)} %bitcast.77) | data formatting | bytes 262144 | tf_op jit(solution)/shard_map/reshape | solution.py:146
  43.1 0.1 slice_convert_fusion
  43.2 0.1 convert_element_type.102
  43.3 0.4 fusion
  43.8 0.4 broadcast_multiply_fusion
  44.2 2.7 %fusion.1 = f32[64,384]{1,0:T(8,128)} fusion(bf16[8192,384]{0,1:T(8,128)(2,1)S(1)} %bitcast.75, s32[8192]{0:T(1024)S(1)} %get-tuple-element.96), kind=kOutput, calls=%fused_computation.5 | convolution fusion | flops 403177472 | bytes 6422528 | tf_op jit(solution)/shard_map/dot_general | solution.py:256
  46.9 0.6 %copy.39 = f32[1,3,20,128]{3,1,2,0:T(4,128)} copy(f32[1,3,20,128]{3,2,1,0:T(8,128)S(1)} %bitcast.79) | data formatting | bytes 61440
  47.5 0.6 %copy.40 = f32[1,3,20,128]{3,1,2,0:T(4,128)} copy(f32[1,3,20,128]{3,2,1,0:T(8,128)S(1)} %bitcast.80) | data formatting | bytes 61440
  (52 shorter events, 0.7 us)

commit v9 on v8

--- a/solution.py
+++ b/solution.py
@@ -75,7 +75,8 @@
     pltpu.make_async_copy(
         recv.at[pl.ds(0, count_x - 1)], recv.at[pl.ds(0, count_x - 1)], send_sems.at[1]
     ).wait()
-    out_ref[...] = recv[...]
+    for row in range(out_ref.shape[0]):
+        out_ref[row] = recv[:, :, row, :]
 
 
 def migrate_kernel(send_ref, out_ref, recv, send_sem, recv_sem):
@@ -132,7 +133,7 @@
     middle = (count_y, count_x) + send.shape[1:]
     got = pl.pallas_call(
         exchange_kernel,
-        out_shape=jax.ShapeDtypeStruct(grid.shape, jnp.float32),
+        out_shape=jax.ShapeDtypeStruct((send.shape[1], count_x, count_y, send.shape[2]), jnp.float32),
         in_specs=[pl.BlockSpec(memory_space=pltpu.VMEM)],
         out_specs=pl.BlockSpec(memory_space=pltpu.VMEM),
         scratch_shapes=[
@@ -143,7 +144,7 @@
         ],
         compiler_params=pltpu.CompilerParams(collective_id=0, has_side_effects=True),
     )(grid)
-    return got.reshape(send.shape)
+    return got.reshape(send.shape[1], devices, send.shape[2])
 def sky_terms(shifted, speeds, live_mask):
     radius = jnp.sum(shifted * shifted, axis=1)
     weight = 1.0 / (1.0 + radius)
@@ -243,9 +244,9 @@
         axis=1,
     )
     got = exchange(send, count_x, count_y)
-    got_values = jnp.stack([got[:, 0, :half], got[:, 0, half:], got[:, 1, :half]], axis=1)
+    got_values = jnp.stack([got[0, :, :half], got[0, :, half:], got[1, :, :half]], axis=1)
     got_values = got_values.reshape(devices, 3, half).transpose(0, 2, 1).reshape(devices * half, 3)
-    got_pixel = got[:, 1, half:].reshape(devices * half).astype(jnp.int32)
+    got_pixel = got[1, :, half:].reshape(devices * half).astype(jnp.int32)
     rows = got_pixel // lane_count
     lanes = got_pixel % lane_count
     row_hits = (rows[None, :] == jnp.arange(STRIP_ROWS, dtype=jnp.int32)[:, None]).astype(jnp.bfloat16)

time: 48.7 us -> 48.7 us (level)
  local copies, waits for them, and re-layouts: 7.25 us -> 5.42 us
  other arithmetic: 10.7 us -> 12.5 us
    reshape x2 -> x0, local copies, waits for them, and re-layouts: 1.83 us -> none  [exchange(): return got.reshape(send.shape)]
    another operation x1 -> x2, other arithmetic: 0.01 us -> 0.93 us
    convert_element_type x1, other arithmetic: 0.08 us -> 0.92 us  [on_device(): got_pixel = got[1, :, half:].reshape(devices * half).astype(jnp.int32)]
where the time goes in v9:
time: 48.7 us; the launch traced here: 48.2 us
  Pallas kernels  26.3 us (54%)
  other arithmetic  12.5 us (26%)
  local copies, waits for them, and re-layouts  5.42 us (11%)
  matrix products  2.95 us (6%)
  between operations  1.02 us (2%)
    pallas_call x1, Pallas kernels, exchange(): pl.pallas_call(exchange_kernel, out_shape=jax.ShapeDtypeStruct((send.shap...  14 us
    pallas_call x1, Pallas kernels, migrate(): pl.pallas_call(migrate_kernel, out_shape=jax.ShapeDtypeStruct(leaving.sha...  12.3 us
    dot_general x1, matrix products, on_device(): maps = jnp.dot(row_hits, spread, preferred_element_type=jnp.float32)  2.68 us
    reduce_sum x1, other arithmetic, on_device(): rank = jnp.sum(same.astype(jnp.int32), axis=2)  1.33 us
    eq x2, other arithmetic, on_device(): place[None, :] == jnp.arange(CROSS_MAX, dtype=jnp.int32)[:, None]  1.31 us
    reduce_sum x1, other arithmetic, on_device(): flagged = jnp.sum(flag_row)  1.3 us
    unnamed x2, local copies, waits for them, and re-layouts  1.26 us

profile of v9, /device:TPU:1, one launch (start us, length us, event | category | flops | bytes accessed | tf_op | source)
XLA Modules:
  0.0 48.2 jit_solution(2608387062912162698)
XLA Ops:
  0.6 0.8 %reshape.607 = f32[3,20,128]{2,1,0:T(8,128)S(1)} reshape(f32[3,2560]{1,0:T(4,128)} %param.15) | data formatting | bytes 61440 | tf_op jit(solution)/shard_map/reshape | solution.py:168
  1.4 0.8 %reshape.606 = f32[3,20,128]{2,1,0:T(8,128)S(1)} reshape(f32[3,2560]{1,0:T(4,128)} %param.14) | data formatting | bytes 61440 | tf_op jit(solution)/shard_map/reshape | solution.py:168
  2.2 0.7 %iota_compare_fusion.9 = pred[20,20]{1,0:T(8,128)(4,1)S(1)} fusion(s32[20]{0:T(128)} %bitcast.90), kind=kLoop, calls=%fused_computation.70 | loop fusion | flops 400 | bytes 480 | tf_op jit(solution)/shard_map/eq | solution.py:167
  3.0 0.4 select_reduce_fusion.1
  3.4 0.8 %select_reduce_fusion.5 = s32[20]{0:T(128)S(1)} fusion(s32[20]{0:T(128)} %bitcast.92), kind=kLoop, calls=%fused_computation.68 | loop fusion | flops 1180 | bytes 160 | tf_op jit(solution)/shard_map/reduce_sum | solution.py:173
  4.2 1.3 %reduce_sum.114 = s32[]{:T(128)} reduce(s32[1,20]{1,0:T(1,128)} %param.17, s32[]{:T(128)} %constant.174.clone.1), dimensions={0,1}, to_apply=%region_3.4 | reduce | flops 19 | bytes 88 | tf_op jit(solution)/shard_map/reduce_sum | solution.py:174
  5.5 1.3 %fusion.23 = s32[20]{0:T(128)S(1)} fusion(s32[1,20]{1,0:T(1,128)} %param.17, s32[20]{0:T(128)S(1)} %select_reduce_fusion.5, s32[]{:T(128)} %reduce_sum.114), kind=kLoop, calls=%fused_computation.108 | loop fusion | flops 100 | bytes 244 | tf_op jit(solution)/shard_map/eq | solution.py:176
  6.8 0.8 %broadcast_in_dim.145 = s32[3,20,128]{2,1,0:T(8,128)S(1)} reshape(s32[3,2560]{1,0:T(4,128)} %param.19) | data formatting | bytes 61440 | tf_op jit(solution)/shard_map/jit(_where)/broadcast_in_dim | solution.py:159
  7.6 0.1 select_reduce_fusion.4
  7.8 0.1 iota_compare_fusion.3
  8.0 1.3 %convert_reduce_fusion = s32[3,640]{1,0:T(4,128)S(1)} fusion(s32[3,640]{1,0:T(4,128)S(1)} %add_select_fusion.5, pred[640,640]{1,0:T(8,128)(4,1)S(1)} %iota_compare_fusion.3), kind=kLoop, calls=%fused_computation | loop fusion | flops 4913280 | bytes 424960 | tf_op jit(solution)/shard_map/reduce_sum | solution.py:194
  9.3 0.3 fusion.3
  9.6 0.8 %select_reduce_fusion.6 = s32[5]{0:T(128)S(1)} fusion(s32[20]{0:T(128)} %bitcast.93, s32[20]{0:T(128)S(1)} %fusion.23), kind=kLoop, calls=%fused_computation.96 | loop fusion | flops 295 | bytes 180 | tf_op jit(solution)/shard_map/reduce_sum | solution.py:177
  10.5 0.6 %pad_maximum_fusion.1.send_ref = f32[4,6,256]{2,1,0:T(8,128)} fusion(f32[1,6,256]{2,1,0:T(8,128)S(1)} %stack.48, f32[1,6,256]{2,1,0:T(8,128)S(1)} %stack.47, f32[1,6,256]{2,1,0:T(8,128)S(1)} %stack.46, f32[1,6,256]{2,1,0:T(8,128)S(1)} %stack.45), kind=kLoop, calls=%fused_computation.45 | loop fusion | flops 18432 | bytes 49152 | tf_op jit(solution)/shard_map/stack | solution.py:210
  11.1 12.3 %shard_map.85 = f32[4,6,256]{2,1,0:T(8,128)} custom-call(f32[4,6,256]{2,1,0:T(8,128)} %pad_maximum_fusion.1.send_ref), custom_call_target="tpu_custom_call" | custom-call | tf_op jit(solution)/shard_map/pallas_call | solution.py:116
  23.4 0.8 %fusion.26 = (f32[1,3,256]{2,1,0:T(4,128)S(1)}, f32[1,3,256]{2,1,0:T(4,128)S(1)}, f32[1,3,256]{2,1,0:T(4,128)S(1)}, f32[1,3,256]{2,1,0:T(4,128)S(1)}, f32[1,3,25...) fusion(f32[4,6,256]{2,1,0:T(8,128)} %shard_map.85), kind=kLoop, calls=%fused_computation.115 | loop fusion | bytes 49152 | tf_op jit(solution)/shard_map/slice | solution.py:212
  24.5 0.1 select_reduce_fusion.2
  24.6 0.7 %convert_element_type.100 = f32[3,3]{1,0:T(4,128)S(1)} convert(s32[3,3]{1,0:T(4,128)} %param.18) | non-fusion elementwise | flops 9 | bytes 72 | tf_op jit(solution)/shard_map/convert_element_type | solution.py:223
  25.3 0.1 fusion.8
  25.5 0.1 broadcast_bitcast_fusion
  25.7 0.1 mul.161
  25.8 0.3 fusion.27
  26.2 0.1 copy.23
  26.3 0.1 copy.24
  26.4 0.8 %pad_maximum_fusion.send_ref = f32[8,16,2,128]{3,2,1,0:T(2,128)} fusion(f32[8,16,1,128]{3,2,1,0:T(1,128)S(1)} %bitcast.86, f32[8,16,1,128]{3,2,1,0:T(1,128)S(1)} %bitcast.85), kind=kLoop, calls=%fused_computation.19 | loop fusion | flops 32768 | bytes 262144 | tf_op jit(solution)/shard_map/stack | solution.py:239
  27.2 14.0 %shard_map.86 = f32[2,8,16,128]{3,2,1,0:T(8,128)} custom-call(f32[8,16,2,128]{3,2,1,0:T(2,128)} %pad_maximum_fusion.send_ref), custom_call_target="tpu_custom_call" | custom-call | tf_op jit(solution)/shard_map/pallas_call | solution.py:134
  41.1 0.9 %bitcast_convert_fusion = bf16[2,128,128]{2,1,0:T(8,128)(2,1)S(1)} fusion(f32[2,8,16,128]{3,2,1,0:T(8,128)} %shard_map.86), kind=kLoop, calls=%fused_computation.112 | loop fusion | flops 32768 | bytes 196608 | tf_op jit(solution)/shard_map/convert.8
  42.1 0.1 slice_bitcast_fusion.2
  42.2 0.1 convert_element_type.104
  42.3 0.9 %slice_convert_fusion = s32[1,128,64]{2,1,0:T(8,128)S(1)} fusion(f32[2,128,128]{2,1,0:T(8,128)} %bitcast.81), kind=kLoop, calls=%fused_computation.21 | loop fusion | flops 8192 | bytes 65536 | tf_op jit(solution)/shard_map/convert_element_type | solution.py:249
  43.2 0.1 convert_element_type.102
  43.3 0.4 fusion
  43.8 0.4 broadcast_multiply_fusion
  44.2 2.7 %fusion.1 = f32[64,384]{1,0:T(8,128)} fusion(bf16[8192,384]{0,1:T(8,128)(2,1)S(1)} %bitcast.80, s32[8192]{0:T(1024)S(1)} %get-tuple-element.96), kind=kOutput, calls=%fused_computation.5 | convolution fusion | flops 403177472 | bytes 6422528 | tf_op jit(solution)/shard_map/dot_general | solution.py:257
  46.9 0.6 %copy.34 = f32[1,3,20,128]{3,1,2,0:T(4,128)} copy(f32[1,3,20,128]{3,2,1,0:T(8,128)S(1)} %bitcast.83) | data formatting | bytes 61440
  47.5 0.6 %copy.35 = f32[1,3,20,128]{3,1,2,0:T(4,128)} copy(f32[1,3,20,128]{3,2,1,0:T(8,128)S(1)} %bitcast.84) | data formatting | bytes 61440
  (52 shorter events, 0.7 us)

commit v10 on v9

--- a/solution.py
+++ b/solution.py
@@ -204,9 +204,6 @@
         return jnp.concatenate([moved_pos, speeds[:, first_block : first_block + MOVERS]], axis=0)
 
     outgoing = [leaving(0, 0, -1.0), leaving(1, 0, 1.0), leaving(2, 1, -1.0), leaving(3, 1, 1.0)]
-    outgoing, places, speeds, dest_hits, rank_hits, where_in_strip, live_mask = lax.optimization_barrier(
-        (outgoing, places, speeds, dest_hits, rank_hits, where_in_strip, live_mask)
-    )
     arrived = migrate(jnp.stack(outgoing).reshape(4, 6, MOVERS * width)).reshape(4, 6, MOVERS, width)
     new_places = jnp.concatenate([places[:, 4 * MOVERS :]] + [got[:3] for got in arrived], axis=1)
     new_speeds = jnp.concatenate([speeds[:, 4 * MOVERS :]] + [got[3:] for got in arrived], axis=1)

time: 48.7 us -> 49.1 us (level)
  matrix products: 2.95 us -> 3.64 us
    dot_general x1, matrix products: 0.28 us -> 0.96 us  [on_device(): lax.dot_general(dest_hits, placed, (((1,), (1,)), ((0,), (0,))), preferre...]
where the time goes in v10:
time: 49.1 us; the launch traced here: 48.5 us
  Pallas kernels  26.3 us (54%)
  other arithmetic  12.2 us (25%)
  local copies, waits for them, and re-layouts  5.43 us (11%)
  matrix products  3.64 us (7%)
  between operations  1.01 us (2%)
    pallas_call x1, Pallas kernels, exchange(): pl.pallas_call(exchange_kernel, out_shape=jax.ShapeDtypeStruct((send.shap...  14 us
    pallas_call x1, Pallas kernels, migrate(): pl.pallas_call(migrate_kernel, out_shape=jax.ShapeDtypeStruct(leaving.sha...  12.3 us
    dot_general x1, matrix products, on_device(): maps = jnp.dot(row_hits, spread, preferred_element_type=jnp.float32)  2.68 us
    reduce_sum x1, other arithmetic, on_device(): rank = jnp.sum(same.astype(jnp.int32), axis=2)  1.33 us
    eq x2, other arithmetic, on_device(): place[None, :] == jnp.arange(CROSS_MAX, dtype=jnp.int32)[:, None]  1.31 us
    reduce_sum x1, other arithmetic, on_device(): flagged = jnp.sum(flag_row)  1.3 us
    unnamed x2, local copies, waits for them, and re-layouts  1.26 us

profile of v10, /device:TPU:1, one launch (start us, length us, event | category | flops | bytes accessed | tf_op | source)
XLA Modules:
  0.0 48.5 jit_solution(6428524122416631781)
XLA Ops:
  0.6 0.8 %reshape.605 = f32[3,20,128]{2,1,0:T(8,128)S(1)} reshape(f32[3,2560]{1,0:T(4,128)} %param.15) | data formatting | bytes 61440 | tf_op jit(solution)/shard_map/reshape | solution.py:168
  1.4 0.8 %reshape.604 = f32[3,20,128]{2,1,0:T(8,128)S(1)} reshape(f32[3,2560]{1,0:T(4,128)} %param.14) | data formatting | bytes 61440 | tf_op jit(solution)/shard_map/reshape | solution.py:168
  2.2 0.7 %iota_compare_fusion.10 = pred[20,20]{1,0:T(8,128)(4,1)S(1)} fusion(s32[20]{0:T(128)} %bitcast.86), kind=kLoop, calls=%fused_computation.71 | loop fusion | flops 400 | bytes 480 | tf_op jit(solution)/shard_map/eq | solution.py:167
  3.0 0.3 select_reduce_fusion
  3.5 0.6 %pad_maximum_fusion.1.send_ref = f32[4,6,256]{2,1,0:T(8,128)} fusion(f32[1,6,256]{2,1,0:T(8,128)S(1)} %stack.44, f32[1,6,256]{2,1,0:T(8,128)S(1)} %stack.43, f32[1,6,256]{2,1,0:T(8,128)S(1)} %stack.42, f32[1,6,256]{2,1,0:T(8,128)S(1)} %stack.41), kind=kLoop, calls=%fused_computation.46 | loop fusion | flops 18432 | bytes 49152 | tf_op jit(solution)/shard_map/stack | solution.py:207
  4.1 12.3 %shard_map.85 = f32[4,6,256]{2,1,0:T(8,128)} custom-call(f32[4,6,256]{2,1,0:T(8,128)} %pad_maximum_fusion.1.send_ref), custom_call_target="tpu_custom_call" | custom-call | tf_op jit(solution)/shard_map/pallas_call | solution.py:116
  16.4 0.8 %fusion.27 = (f32[1,3,256]{2,1,0:T(4,128)S(1)}, f32[1,3,256]{2,1,0:T(4,128)S(1)}, f32[1,3,256]{2,1,0:T(4,128)S(1)}, f32[1,3,256]{2,1,0:T(4,128)S(1)}, f32[1,3,25...) fusion(f32[4,6,256]{2,1,0:T(8,128)} %shard_map.85), kind=kLoop, calls=%fused_computation.114 | loop fusion | bytes 49152 | tf_op jit(solution)/shard_map/slice | solution.py:209
  17.5 0.8 %select_reduce_fusion.5 = s32[20]{0:T(128)S(1)} fusion(s32[20]{0:T(128)} %bitcast.87), kind=kLoop, calls=%fused_computation.69 | loop fusion | flops 1180 | bytes 160 | tf_op jit(solution)/shard_map/reduce_sum | solution.py:173
  18.2 1.3 %reduce_sum.114 = s32[]{:T(128)} reduce(s32[1,20]{1,0:T(1,128)} %param.17, s32[]{:T(128)} %constant.174.clone.1), dimensions={0,1}, to_apply=%region_3.4 | reduce | flops 19 | bytes 88 | tf_op jit(solution)/shard_map/reduce_sum | solution.py:174
  19.5 1.3 %fusion.24 = s32[20]{0:T(128)S(1)} fusion(s32[1,20]{1,0:T(1,128)} %param.17, s32[20]{0:T(128)S(1)} %select_reduce_fusion.5, s32[]{:T(128)} %reduce_sum.114), kind=kLoop, calls=%fused_computation.108 | loop fusion | flops 100 | bytes 244 | tf_op jit(solution)/shard_map/eq | solution.py:176
  20.8 0.1 select_reduce_fusion.2
  21.0 0.7 %convert_element_type.89 = f32[3,3]{1,0:T(4,128)S(1)} convert(s32[3,3]{1,0:T(4,128)} %param.18) | non-fusion elementwise | flops 9 | bytes 72 | tf_op jit(solution)/shard_map/convert_element_type | solution.py:220
  21.7 0.1 fusion.9
  21.9 0.8 %select_reduce_fusion.6 = s32[5]{0:T(128)S(1)} fusion(s32[20]{0:T(128)} %bitcast.88, s32[20]{0:T(128)S(1)} %fusion.24), kind=kLoop, calls=%fused_computation.96 | loop fusion | flops 295 | bytes 180 | tf_op jit(solution)/shard_map/reduce_sum | solution.py:177
  22.7 0.1 broadcast_bitcast_fusion
  22.8 0.8 %broadcast_in_dim.145 = s32[3,20,128]{2,1,0:T(8,128)S(1)} reshape(s32[3,2560]{1,0:T(4,128)} %param.19) | data formatting | bytes 61440 | tf_op jit(solution)/shard_map/jit(_where)/broadcast_in_dim | solution.py:159
  23.6 0.1 select_reduce_fusion.4
  23.8 0.1 iota_compare_fusion.3
  24.0 1.3 %convert_reduce_fusion = s32[3,640]{1,0:T(4,128)S(1)} fusion(s32[3,640]{1,0:T(4,128)S(1)} %add_select_fusion.5, pred[640,640]{1,0:T(8,128)(4,1)S(1)} %iota_compare_fusion.3), kind=kLoop, calls=%fused_computation | loop fusion | flops 4913280 | bytes 424960 | tf_op jit(solution)/shard_map/reduce_sum | solution.py:194
  25.4 0.1 mul.158
  25.5 1.0 %fusion.3 = f32[3,128,100]{1,2,0:T(8,128)S(1)} fusion(bf16[3,640,100]{1,2,0:T(8,128)(2,1)S(1)} %mul.158, s32[3,640]{1,0:T(4,128)S(1)} %add_select_fusion.5), kind=kOutput, calls=%fused_computation.9 | convolution fusion | flops 49397760 | bytes 545280 | tf_op jit(solution)/shard_map/dot_general | solution.py:228
  26.5 0.1 copy.23
  26.6 0.1 copy.24
  26.7 0.8 %pad_maximum_fusion.send_ref = f32[8,16,2,128]{3,2,1,0:T(2,128)} fusion(f32[8,16,1,128]{3,2,1,0:T(1,128)S(1)} %bitcast.82, f32[8,16,1,128]{3,2,1,0:T(1,128)S(1)} %bitcast.81), kind=kLoop, calls=%fused_computation.20 | loop fusion | flops 32768 | bytes 262144 | tf_op jit(solution)/shard_map/stack | solution.py:236
  27.5 14.0 %shard_map.86 = f32[2,8,16,128]{3,2,1,0:T(8,128)} custom-call(f32[8,16,2,128]{3,2,1,0:T(2,128)} %pad_maximum_fusion.send_ref), custom_call_target="tpu_custom_call" | custom-call | tf_op jit(solution)/shard_map/pallas_call | solution.py:134
  41.5 0.9 %bitcast_convert_fusion = bf16[2,128,128]{2,1,0:T(8,128)(2,1)S(1)} fusion(f32[2,8,16,128]{3,2,1,0:T(8,128)} %shard_map.86), kind=kLoop, calls=%fused_computation.111 | loop fusion | flops 32768 | bytes 196608 | tf_op jit(solution)/shard_map/convert.8
  42.4 0.1 slice_bitcast_fusion.2
  42.5 0.1 convert_element_type.98
  42.6 0.9 %slice_convert_fusion = s32[1,128,64]{2,1,0:T(8,128)S(1)} fusion(f32[2,128,128]{2,1,0:T(8,128)} %bitcast.77), kind=kLoop, calls=%fused_computation.22 | loop fusion | flops 8192 | bytes 65536 | tf_op jit(solution)/shard_map/convert_element_type | solution.py:246
  43.6 0.1 convert_element_type.96
  43.7 0.4 fusion
  44.1 0.5 broadcast_multiply_fusion
  44.6 2.7 %fusion.1 = f32[64,384]{1,0:T(8,128)} fusion(bf16[8192,384]{0,1:T(8,128)(2,1)S(1)} %bitcast.76, s32[8192]{0:T(1024)S(1)} %get-tuple-element.76), kind=kOutput, calls=%fused_computation.5 | convolution fusion | flops 403177472 | bytes 6422528 | tf_op jit(solution)/shard_map/dot_general | solution.py:254
  47.2 0.6 %copy.34 = f32[1,3,20,128]{3,1,2,0:T(4,128)} copy(f32[1,3,20,128]{3,2,1,0:T(8,128)S(1)} %bitcast.79) | data formatting | bytes 61440
  47.9 0.6 %copy.35 = f32[1,3,20,128]{3,1,2,0:T(4,128)} copy(f32[1,3,20,128]{3,2,1,0:T(8,128)S(1)} %bitcast.80) | data formatting | bytes 61440
  (51 shorter events, 0.7 us)

commit v11 on v10

--- a/solution.py
+++ b/solution.py
@@ -127,6 +127,91 @@
     )(leaving)
 
 
+def bucket_kernel(flags_ref, offsets_ref, places_ref, speeds_ref, pixels_ref, send_ref):
+    blocks = flags_ref.shape[1]
+    devices = send_ref.shape[0]
+    count_x = lax.axis_size("gx")
+    count_y = lax.axis_size("gy")
+    cell_x = lax.axis_index("gx").astype(jnp.float32)
+    cell_y = lax.axis_index("gy").astype(jnp.float32)
+    strip_size = STRIP_ROWS * lane_count
+    half = lane_count // 2
+
+    flag = [flags_ref[0, b] for b in range(blocks)]
+    flagged = sum(flag)
+    place, upto = [], 0
+    for b in range(blocks):
+        upto = upto + flag[b]
+        place.append(jnp.where(flag[b] == 1, upto - 1, flagged + b - upto))
+    chosen = [sum(jnp.where(place[b] == k, b, 0) for b in range(blocks)) for k in range(CROSS_MAX)]
+    live = [sum(jnp.where(place[b] == k, flag[b], 0) for b in range(blocks)) for k in range(CROSS_MAX)]
+
+    dest_iota = lax.broadcasted_iota(jnp.int32, (devices, lane_count), 0)
+    slot_iota = lax.broadcasted_iota(jnp.int32, (lane_count, lane_count), 0)
+    before = (
+        lax.broadcasted_iota(jnp.int32, (lane_count, lane_count), 0)
+        < lax.broadcasted_iota(jnp.int32, (lane_count, lane_count), 1)
+    ).astype(jnp.bfloat16)
+    nt = (((1,), (1,)), ((), ()))
+    values_part = jnp.zeros((devices, lane_count), jnp.float32)
+    strip_part = jnp.zeros((devices, lane_count), jnp.float32)
+    lane_part = jnp.zeros((devices, lane_count), jnp.float32)
+    for replica in range(REPLICAS):
+        shift = [offsets_ref[replica, c].astype(jnp.float32) for c in range(3)]
+        seen = jnp.zeros((devices, 1), jnp.float32)
+        for k in range(CROSS_MAX):
+            columns = pl.ds(pl.multiple_of(chosen[k] * lane_count, lane_count), lane_count)
+            pos = places_ref[:, columns]
+            vel = speeds_ref[:, columns]
+            ids = pixels_ref[replica : replica + 1, columns]
+            mask = live[k].astype(jnp.float32)
+            s0 = (cell_x + pos[0:1]) / count_x + shift[0]
+            s1 = (cell_y + pos[1:2]) / count_y + shift[1]
+            s2 = pos[2:3] + shift[2]
+            radius = s0 * s0 + s1 * s1 + s2 * s2
+            weight = 1.0 / (1.0 + radius)
+            radial = (vel[0:1] * s0 + vel[1:2] * s1 + vel[2:3] * s2) / jnp.sqrt(1.0 + radius)
+            energy = (vel[0:1] * vel[0:1] + vel[1:2] * vel[1:2] + vel[2:3] * vel[2:3]) / 3.0
+            value = [
+                (weight * mask).astype(jnp.bfloat16).astype(jnp.float32),
+                (weight * radial * mask).astype(jnp.bfloat16).astype(jnp.float32),
+                (weight * energy * mask).astype(jnp.bfloat16).astype(jnp.float32),
+            ]
+            dest = ids // strip_size
+            inside = ids % strip_size
+            dest_hits = (dest == dest_iota).astype(jnp.bfloat16)
+            counted = seen + jnp.dot(dest_hits, before, preferred_element_type=jnp.float32)
+            rank = jnp.sum(dest_hits.astype(jnp.float32) * counted, axis=0, keepdims=True)
+            seen = seen + jnp.sum(dest_hits.astype(jnp.float32), axis=1, keepdims=True)
+            slot = rank.astype(jnp.int32) + replica * blocks
+            low = slot_iota == slot
+            high = slot_iota == slot + half
+            first = (jnp.where(low, value[0], 0.0) + jnp.where(high, value[1], 0.0)).astype(jnp.bfloat16)
+            second = jnp.where(low, value[2], 0.0) + jnp.where(high, (inside // lane_count).astype(jnp.float32), 0.0)
+            third = jnp.where(high, (inside % lane_count).astype(jnp.float32), 0.0)
+            values_part += lax.dot_general(dest_hits, first, nt, preferred_element_type=jnp.float32)
+            strip_part += lax.dot_general(
+                dest_hits, second.astype(jnp.bfloat16), nt, preferred_element_type=jnp.float32
+            )
+            lane_part += lax.dot_general(
+                dest_hits, third.astype(jnp.bfloat16), nt, preferred_element_type=jnp.float32
+            )
+    scale = jnp.where(lax.broadcasted_iota(jnp.int32, (1, lane_count), 1) < half, 1.0, float(lane_count))
+    send_ref[:, 0, :] = values_part
+    send_ref[:, 1, :] = strip_part * scale + lane_part
+
+
+def bucket(flags, offsets, places, speeds, pixels, devices):
+    smem = pl.BlockSpec(memory_space=pltpu.SMEM)
+    vmem = pl.BlockSpec(memory_space=pltpu.VMEM)
+    return pl.pallas_call(
+        bucket_kernel,
+        out_shape=jax.ShapeDtypeStruct((devices, 2, lane_count), jnp.float32),
+        in_specs=[smem, smem, vmem, vmem, vmem],
+        out_specs=vmem,
+    )(flags, offsets, places, speeds, pixels)
+
+
 def exchange(send, count_x, count_y):
     devices = send.shape[0]
     grid = send.reshape(count_x, count_y, *send.shape[1:])
@@ -168,35 +253,9 @@
     places = pick(positions.reshape(3, blocks, width) + time_step * velocities.reshape(3, blocks, width), order_hits)
     speeds = pick(velocities.reshape(3, blocks, width), order_hits)
 
-    flag_row = flags[0]
-    earlier = block_ids[None, :] <= block_ids[:, None]
-    flagged_upto = jnp.sum(jnp.where(earlier, flag_row[None, :], 0), axis=1)
-    flagged = jnp.sum(flag_row)
-    place = jnp.where(flag_row == 1, flagged_upto - 1, flagged + block_ids - flagged_upto)
-    chosen_hits = place[None, :] == jnp.arange(CROSS_MAX, dtype=jnp.int32)[:, None]
-    live_mask = jnp.sum(jnp.where(chosen_hits, flag_row[None, :], 0), axis=1)
-    live_mask = live_mask.astype(jnp.float32).reshape(1, CROSS_MAX, 1)
-    picked_ids = pick(pixels.reshape(REPLICAS, blocks, width), chosen_hits)
-
     count_x = lax.axis_size("gx")
     count_y = lax.axis_size("gy")
     devices = count_x * count_y
-    cell_x = lax.axis_index("gx")
-    cell_y = lax.axis_index("gy")
-
-    strip_size = STRIP_ROWS * lane_count
-    per_replica = CROSS_MAX * width
-    ids = picked_ids.reshape(REPLICAS, per_replica)
-    dest = ids // strip_size
-    inside = ids % strip_size
-    order = jnp.arange(per_replica, dtype=jnp.int32)
-    same = (dest[:, :, None] == dest[:, None, :]) & (order[None, None, :] < order[None, :, None])
-    rank = jnp.sum(same.astype(jnp.int32), axis=2)
-    dest_hits = (dest[:, :, None] == jnp.arange(devices, dtype=jnp.int32)).astype(jnp.bfloat16)
-    rank_hits = (rank[:, :, None] == block_ids).astype(jnp.bfloat16)
-    where_in_strip = jnp.stack(
-        [(inside // lane_count).astype(jnp.bfloat16), (inside % lane_count).astype(jnp.bfloat16)], axis=2
-    )
 
     def leaving(which_set, component, sign_step):
         first_block = which_set * MOVERS
@@ -207,39 +266,10 @@
     arrived = migrate(jnp.stack(outgoing).reshape(4, 6, MOVERS * width)).reshape(4, 6, MOVERS, width)
     new_places = jnp.concatenate([places[:, 4 * MOVERS :]] + [got[:3] for got in arrived], axis=1)
     new_speeds = jnp.concatenate([speeds[:, 4 * MOVERS :]] + [got[3:] for got in arrived], axis=1)
-    picked_pos = pick(new_places, chosen_hits)
-    picked_vel = pick(new_speeds, chosen_hits)
-    global_pos = jnp.stack(
-        [
-            (cell_x.astype(jnp.float32) + picked_pos[0]) / count_x,
-            (cell_y.astype(jnp.float32) + picked_pos[1]) / count_y,
-            picked_pos[2],
-        ],
-        axis=0,
-    )
-    shifted = global_pos[None] + offsets.astype(jnp.float32)[:, :, None, None]
-    values = sky_terms(shifted, picked_vel, live_mask)
-
-    slots = REPLICAS * blocks
-    fields = jnp.concatenate(
-        [jnp.transpose(values.reshape(3, REPLICAS, per_replica), (1, 2, 0)), where_in_strip], axis=2
-    )
-    placed = (fields[:, :, :, None] * rank_hits[:, :, None, :]).reshape(REPLICAS, per_replica, 5 * blocks)
-    send = lax.dot_general(
-        dest_hits, placed, (((1,), (1,)), ((0,), (0,))), preferred_element_type=jnp.float32
-    )
-    send = jnp.transpose(send.reshape(REPLICAS, devices, 5, blocks), (1, 2, 0, 3))
-    send = send.reshape(devices, 5, slots)
-    pixel = send[:, 3] * lane_count + send[:, 4]
+    new_places = new_places.reshape(3, blocks * width)
+    new_speeds = new_speeds.reshape(3, blocks * width)
+    send = bucket(flags, offsets, new_places, new_speeds, pixels, devices)
     half = lane_count // 2
-    pad = ((0, 0), (0, half - slots))
-    send = jnp.stack(
-        [
-            jnp.concatenate([jnp.pad(send[:, 0], pad), jnp.pad(send[:, 1], pad)], axis=1),
-            jnp.concatenate([jnp.pad(send[:, 2], pad), jnp.pad(pixel, pad)], axis=1),
-        ],
-        axis=1,
-    )
     got = exchange(send, count_x, count_y)
     got_values = jnp.stack([got[0, :, :half], got[0, :, half:], got[1, :, :half]], axis=1)
     got_values = got_values.reshape(devices, 3, half).transpose(0, 2, 1).reshape(devices * half, 3)
@@ -252,7 +282,7 @@
         devices * half, 3 * lane_count
     )
     maps = jnp.dot(row_hits, spread, preferred_element_type=jnp.float32)
-    return (new_places.reshape(3, blocks * width), new_speeds.reshape(3, blocks * width), maps)
+    return (new_places, new_speeds, maps)
 
 
 def solution(mesh):

time: 49.1 us -> 43.9 us (0.89)
  other arithmetic: 12.2 us -> 4.51 us
  Pallas kernels: 26.3 us -> 31.2 us
  local copies, waits for them, and re-layouts: 5.43 us -> 4.22 us
  matrix products: 3.64 us -> 2.68 us
    pallas_call x0 -> x1, Pallas kernels: none -> 4.92 us  [bucket(): pl.pallas_call(bucket_kernel, out_shape=jax.ShapeDtypeStruct((devices, 2,...]
    reduce_sum x6 -> x0, other arithmetic: 4.3 us -> none  [the longest x1 1.33 us: on_device(): rank = jnp.sum(same.astype(jnp.int32), axis=2)]
    eq x2 -> x0, other arithmetic: 1.31 us -> none  [on_device(): place[None, :] == jnp.arange(CROSS_MAX, dtype=jnp.int32)[:, None]]
    dot_general x1 -> x0, matrix products: 0.96 us -> none  [on_device(): lax.dot_general(dest_hits, placed, (((1,), (1,)), ((0,), (0,))), preferre...]
    broadcast_in_dim x1 -> x0, local copies, waits for them, and re-layouts: 0.8 us -> none  [pick(): jnp.where(hits[:, :, None], data[..., None, :, :], jnp.zeros((), data.dty...]
    another operation x4 -> x1, other arithmetic: 1.7 us -> 0.92 us
    convert_element_type x4 -> x0, other arithmetic: 0.75 us -> none  [the longest x1 0.69 us: on_device(): shifted = global_pos[None] + offsets.astype(jnp.float32)[:, :, None, None]]
where the time goes in v11:
time: 43.9 us; the launch traced here: 43.4 us
  Pallas kernels  31.2 us (71%)
  other arithmetic  4.51 us (10%)
  local copies, waits for them, and re-layouts  4.22 us (10%)
  matrix products  2.68 us (6%)
  between operations  0.79 us (2%)
    pallas_call x1, Pallas kernels, exchange(): pl.pallas_call(exchange_kernel, out_shape=jax.ShapeDtypeStruct((send.shap...  14 us
    pallas_call x1, Pallas kernels, migrate(): pl.pallas_call(migrate_kernel, out_shape=jax.ShapeDtypeStruct(leaving.sha...  12.3 us
    pallas_call x1, Pallas kernels, bucket(): pl.pallas_call(bucket_kernel, out_shape=jax.ShapeDtypeStruct((devices, 2,...  4.92 us
    dot_general x1, matrix products, on_device(): maps = jnp.dot(row_hits, spread, preferred_element_type=jnp.float32)  2.68 us
    unnamed x2, local copies, waits for them, and re-layouts  1.26 us
    convert_element_type x1, other arithmetic, on_device(): got_pixel = got[1, :, half:].reshape(devices * half).astype(jnp.int32)  0.92 us
    another operation x1, other arithmetic  0.92 us
    slice x5, local copies, waits for them, and re-layouts, on_device(): got[3:]  0.88 us

profile of v11, /device:TPU:1, one launch (start us, length us, event | category | flops | bytes accessed | tf_op | source)
XLA Modules:
  0.0 43.4 jit_solution(1997334152559229564)
XLA Ops:
  0.6 0.7 %iota_compare_fusion.3 = pred[20,20]{1,0:T(8,128)(4,1)S(1)} fusion(s32[20]{0:T(128)} %bitcast.33), kind=kLoop, calls=%fused_computation.25 | loop fusion | flops 400 | bytes 480 | tf_op jit(solution)/shard_map/eq | solution.py:252
  1.4 0.8 %reshape.229 = f32[3,20,128]{2,1,0:T(8,128)S(1)} reshape(f32[3,2560]{1,0:T(4,128)} %param.15) | data formatting | bytes 61440 | tf_op jit(solution)/shard_map/reshape | solution.py:253
  2.2 0.8 %reshape.228 = f32[3,20,128]{2,1,0:T(8,128)S(1)} reshape(f32[3,2560]{1,0:T(4,128)} %param.14) | data formatting | bytes 61440 | tf_op jit(solution)/shard_map/reshape | solution.py:253
  3.0 0.3 select_reduce_fusion
  3.5 0.6 %pad_maximum_fusion.send_ref = f32[4,6,256]{2,1,0:T(8,128)} fusion(f32[1,6,256]{2,1,0:T(8,128)S(1)} %stack.22, f32[1,6,256]{2,1,0:T(8,128)S(1)} %stack.21, f32[1,6,256]{2,1,0:T(8,128)S(1)} %stack.20, f32[1,6,256]{2,1,0:T(8,128)S(1)} %stack.19), kind=kLoop, calls=%fused_computation.21 | loop fusion | flops 18432 | bytes 49152 | tf_op jit(solution)/shard_map/stack | solution.py:266
  4.1 12.3 %shard_map.85 = f32[4,6,256]{2,1,0:T(8,128)} custom-call(f32[4,6,256]{2,1,0:T(8,128)} %pad_maximum_fusion.send_ref), custom_call_target="tpu_custom_call" | custom-call | tf_op jit(solution)/shard_map/pallas_call | solution.py:116
  16.4 0.8 %fusion.11 = (f32[1,3,256]{2,1,0:T(4,128)S(1)}, f32[1,3,256]{2,1,0:T(4,128)S(1)}, f32[1,3,256]{2,1,0:T(4,128)S(1)}, f32[1,3,256]{2,1,0:T(4,128)S(1)}, f32[1,3,25...) fusion(f32[4,6,256]{2,1,0:T(8,128)} %shard_map.85), kind=kLoop, calls=%fused_computation.41 | loop fusion | bytes 49152 | tf_op jit(solution)/shard_map/slice | solution.py:268
  17.5 0.6 %copy.15 = f32[1,3,20,128]{3,1,2,0:T(4,128)} copy(f32[1,3,20,128]{3,2,1,0:T(8,128)S(1)} %bitcast.32) | data formatting | bytes 61440
  18.1 0.6 %copy.14 = f32[1,3,20,128]{3,1,2,0:T(4,128)} copy(f32[1,3,20,128]{3,2,1,0:T(8,128)S(1)} %bitcast.31) | data formatting | bytes 61440
  18.7 4.9 %shard_map.86 = f32[128,2,128]{2,1,0:T(2,128)} custom-call(s32[1,20]{1,0:T(1,128)} %flags_ref.1, s32[3,3]{1,0:T(4,128)} %offsets_ref.1, f32[3,2560]{1,0:T(4,128)} %bitcast.27, f32[3,2560]{1,0:T(4,128)} %bitcast.29, s32[3,2560]{1,0:T(4,128)} %pixels_ref.1), custom_call_target="tpu_custom_call" | custom-call | tf_op jit(solution)/shard_map/pallas_call | solution.py:207
  23.7 14.0 %shard_map.87 = f32[2,8,16,128]{3,2,1,0:T(8,128)} custom-call(f32[8,16,2,128]{3,2,1,0:T(2,128)} %bitcast.26), custom_call_target="tpu_custom_call" | custom-call | tf_op jit(solution)/shard_map/pallas_call | solution.py:219
  37.6 0.9 %slice_convert_fusion = s32[1,128,64]{2,1,0:T(8,128)S(1)} fusion(f32[2,128,128]{2,1,0:T(8,128)} %bitcast.25), kind=kLoop, calls=%fused_computation.9 | loop fusion | flops 8192 | bytes 65536 | tf_op jit(solution)/shard_map/convert_element_type | solution.py:276
  38.6 0.1 convert_element_type.34
  38.7 0.9 %bitcast_convert_fusion = bf16[2,128,128]{2,1,0:T(8,128)(2,1)S(1)} fusion(f32[2,8,16,128]{3,2,1,0:T(8,128)} %shard_map.87), kind=kLoop, calls=%fused_computation.38 | loop fusion | flops 32768 | bytes 196608 | tf_op jit(solution)/shard_map/convert.8
  39.6 0.1 slice_bitcast_fusion.2
  39.7 0.1 convert_element_type.36
  39.8 0.4 fusion
  40.3 0.4 %broadcast_multiply_fusion = bf16[8192,3,128]{0,2,1:T(8,128)(2,1)S(1)} fusion(bf16[8192,128]{0,1:T(8,128)(2,1)S(1)} %fusion, bf16[8192,3]{0,1:T(4,128)(2,1)S(1)} %convert_element_type.36), kind=kLoop, calls=%fused_computation.2 | loop fusion | flops 3145728 | bytes 8437760 | tf_op jit(solution)/shard_map/mul | solution.py:281
  40.7 2.7 %fusion.1 = f32[64,384]{1,0:T(8,128)} fusion(bf16[8192,384]{0,1:T(8,128)(2,1)S(1)} %bitcast.24, s32[8192]{0:T(1024)S(1)} %get-tuple-element.68), kind=kOutput, calls=%fused_computation.4 | convolution fusion | flops 403177472 | bytes 6422528 | tf_op jit(solution)/shard_map/dot_general | solution.py:284
  (25 shorter events, 0.4 us)

commit v12 on v11

--- a/solution.py
+++ b/solution.py
@@ -16,7 +16,7 @@
 MESH = pl.DeviceIdType.MESH
 
 
-def exchange_kernel(send_ref, out_ref, middle, recv, send_sems, recv_sems):
+def exchange_kernel(flags_ref, offsets_ref, places_ref, speeds_ref, pixels_ref, out_ref, send_ref, middle, recv, send_sems, recv_sems):
     count_x, count_y = send_ref.shape[0], send_ref.shape[1]
     x = lax.axis_index("gx")
     y = lax.axis_index("gy")
@@ -34,6 +34,11 @@
 
     lax.fori_loop(1, count_y, greet_y, 0)
     lax.fori_loop(1, count_x, greet_x, 0)
+    first, second = fill_send(flags_ref, offsets_ref, places_ref, speeds_ref, pixels_ref, count_x * count_y)
+    for row in range(count_x):
+        rows = slice(row * count_y, (row + 1) * count_y)
+        send_ref[row, :, 0, :] = first[rows]
+        send_ref[row, :, 1, :] = second[rows]
     pl.semaphore_wait(barrier, count_x + count_y - 2)
 
     pltpu.make_async_copy(send_ref.at[:, y], middle.at[y], recv_sems.at[0]).start()
@@ -127,9 +132,8 @@
     )(leaving)
 
 
-def bucket_kernel(flags_ref, offsets_ref, places_ref, speeds_ref, pixels_ref, send_ref):
+def fill_send(flags_ref, offsets_ref, places_ref, speeds_ref, pixels_ref, devices):
     blocks = flags_ref.shape[1]
-    devices = send_ref.shape[0]
     count_x = lax.axis_size("gx")
     count_y = lax.axis_size("gy")
     cell_x = lax.axis_index("gx").astype(jnp.float32)
@@ -146,6 +150,17 @@
     chosen = [sum(jnp.where(place[b] == k, b, 0) for b in range(blocks)) for k in range(CROSS_MAX)]
     live = [sum(jnp.where(place[b] == k, flag[b], 0) for b in range(blocks)) for k in range(CROSS_MAX)]
 
+    def picked(ref, k):
+        total = None
+        for b in range(blocks):
+            block = ref[:, b * lane_count : (b + 1) * lane_count]
+            term = jnp.where(chosen[k] == b, block, jnp.zeros((), block.dtype))
+            total = term if total is None else total + term
+        return total
+
+    picked_pos = [picked(places_ref, k) for k in range(CROSS_MAX)]
+    picked_vel = [picked(speeds_ref, k) for k in range(CROSS_MAX)]
+    picked_ids = [picked(pixels_ref, k) for k in range(CROSS_MAX)]
     dest_iota = lax.broadcasted_iota(jnp.int32, (devices, lane_count), 0)
     slot_iota = lax.broadcasted_iota(jnp.int32, (lane_count, lane_count), 0)
     before = (
@@ -160,10 +175,7 @@
         shift = [offsets_ref[replica, c].astype(jnp.float32) for c in range(3)]
         seen = jnp.zeros((devices, 1), jnp.float32)
         for k in range(CROSS_MAX):
-            columns = pl.ds(pl.multiple_of(chosen[k] * lane_count, lane_count), lane_count)
-            pos = places_ref[:, columns]
-            vel = speeds_ref[:, columns]
-            ids = pixels_ref[replica : replica + 1, columns]
+            pos, vel, ids = picked_pos[k], picked_vel[k], picked_ids[k][replica : replica + 1]
             mask = live[k].astype(jnp.float32)
             s0 = (cell_x + pos[0:1]) / count_x + shift[0]
             s1 = (cell_y + pos[1:2]) / count_y + shift[1]
@@ -197,47 +209,30 @@
                 dest_hits, third.astype(jnp.bfloat16), nt, preferred_element_type=jnp.float32
             )
     scale = jnp.where(lax.broadcasted_iota(jnp.int32, (1, lane_count), 1) < half, 1.0, float(lane_count))
-    send_ref[:, 0, :] = values_part
-    send_ref[:, 1, :] = strip_part * scale + lane_part
-
-
-def bucket(flags, offsets, places, speeds, pixels, devices):
+    return values_part, strip_part * scale + lane_part
+
+
+def exchange(flags, offsets, places, speeds, pixels, count_x, count_y):
+    devices = count_x * count_y
+    grid = (count_x, count_y, 2, lane_count)
+    middle = (count_y, count_x, 2, lane_count)
     smem = pl.BlockSpec(memory_space=pltpu.SMEM)
     vmem = pl.BlockSpec(memory_space=pltpu.VMEM)
-    return pl.pallas_call(
-        bucket_kernel,
-        out_shape=jax.ShapeDtypeStruct((devices, 2, lane_count), jnp.float32),
+    got = pl.pallas_call(
+        exchange_kernel,
+        out_shape=jax.ShapeDtypeStruct((2, count_x, count_y, lane_count), jnp.float32),
         in_specs=[smem, smem, vmem, vmem, vmem],
         out_specs=vmem,
-    )(flags, offsets, places, speeds, pixels)
-
-
-def exchange(send, count_x, count_y):
-    devices = send.shape[0]
-    grid = send.reshape(count_x, count_y, *send.shape[1:])
-    middle = (count_y, count_x) + send.shape[1:]
-    got = pl.pallas_call(
-        exchange_kernel,
-        out_shape=jax.ShapeDtypeStruct((send.shape[1], count_x, count_y, send.shape[2]), jnp.float32),
-        in_specs=[pl.BlockSpec(memory_space=pltpu.VMEM)],
-        out_specs=pl.BlockSpec(memory_space=pltpu.VMEM),
         scratch_shapes=[
+            pltpu.VMEM(grid, jnp.float32),
             pltpu.VMEM(middle, jnp.float32),
-            pltpu.VMEM(grid.shape, jnp.float32),
+            pltpu.VMEM(grid, jnp.float32),
             pltpu.SemaphoreType.DMA((2,)),
             pltpu.SemaphoreType.DMA((2,)),
         ],
         compiler_params=pltpu.CompilerParams(collective_id=0, has_side_effects=True),
-    )(grid)
-    return got.reshape(send.shape[1], devices, send.shape[2])
-def sky_terms(shifted, speeds, live_mask):
-    radius = jnp.sum(shifted * shifted, axis=1)
-    weight = 1.0 / (1.0 + radius)
-    radial = jnp.sum(speeds[None] * shifted, axis=1) / jnp.sqrt(1.0 + radius)
-    energy = jnp.sum(speeds * speeds, axis=0) / 3.0
-    return jnp.stack(
-        [weight * live_mask, weight * radial * live_mask, weight * energy[None] * live_mask], axis=0
-    ).astype(jnp.bfloat16)
+    )(flags, offsets, places, speeds, pixels)
+    return got.reshape(2, devices, lane_count)
 
 
 def pick(data, hits):
@@ -268,9 +263,8 @@
     new_speeds = jnp.concatenate([speeds[:, 4 * MOVERS :]] + [got[3:] for got in arrived], axis=1)
     new_places = new_places.reshape(3, blocks * width)
     new_speeds = new_speeds.reshape(3, blocks * width)
-    send = bucket(flags, offsets, new_places, new_speeds, pixels, devices)
     half = lane_count // 2
-    got = exchange(send, count_x, count_y)
+    got = exchange(flags, offsets, new_places, new_speeds, pixels, count_x, count_y)
     got_values = jnp.stack([got[0, :, :half], got[0, :, half:], got[1, :, :half]], axis=1)
     got_values = got_values.reshape(devices, 3, half).transpose(0, 2, 1).reshape(devices * half, 3)
     got_pixel = got[1, :, half:].reshape(devices * half).astype(jnp.int32)

time: 43.9 us -> 39.3 us (0.90)
  Pallas kernels: 31.2 us -> 26.6 us
    pallas_call x2 -> x1, Pallas kernels: 18.9 us -> 14.3 us  [exchange(): pl.pallas_call(exchange_kernel, out_shape=jax.ShapeDtypeStruct((2, count_...]
where the time goes in v12:
time: 39.3 us; the launch traced here: 38.8 us
  Pallas kernels  26.6 us (68%)
  other arithmetic  4.51 us (11%)
  local copies, waits for them, and re-layouts  4.22 us (11%)
  matrix products  2.68 us (7%)
  between operations  0.79 us (2%)
    pallas_call x1, Pallas kernels, exchange(): pl.pallas_call(exchange_kernel, out_shape=jax.ShapeDtypeStruct((2, count_...  14.3 us
    pallas_call x1, Pallas kernels, migrate(): pl.pallas_call(migrate_kernel, out_shape=jax.ShapeDtypeStruct(leaving.sha...  12.3 us
    dot_general x1, matrix products, on_device(): maps = jnp.dot(row_hits, spread, preferred_element_type=jnp.float32)  2.68 us
    unnamed x2, local copies, waits for them, and re-layouts  1.26 us
    convert_element_type x1, other arithmetic, on_device(): got_pixel = got[1, :, half:].reshape(devices * half).astype(jnp.int32)  0.92 us
    another operation x1, other arithmetic  0.92 us
    slice x5, local copies, waits for them, and re-layouts, on_device(): got[3:]  0.88 us
    reshape x1, local copies, waits for them, and re-layouts, on_device(): positions.reshape(3, blocks, width)  0.8 us

profile of v12, /device:TPU:1, one launch (start us, length us, event | category | flops | bytes accessed | tf_op | source)
XLA Modules:
  0.0 38.8 jit_solution(10070759994804460628)
XLA Ops:
  0.6 0.7 %iota_compare_fusion.3 = pred[20,20]{1,0:T(8,128)(4,1)S(1)} fusion(s32[20]{0:T(128)} %bitcast.31), kind=kLoop, calls=%fused_computation.25 | loop fusion | flops 400 | bytes 480 | tf_op jit(solution)/shard_map/eq | solution.py:247
  1.4 0.8 %reshape.226 = f32[3,20,128]{2,1,0:T(8,128)S(1)} reshape(f32[3,2560]{1,0:T(4,128)} %param.15) | data formatting | bytes 61440 | tf_op jit(solution)/shard_map/reshape | solution.py:248
  2.2 0.8 %reshape.225 = f32[3,20,128]{2,1,0:T(8,128)S(1)} reshape(f32[3,2560]{1,0:T(4,128)} %param.14) | data formatting | bytes 61440 | tf_op jit(solution)/shard_map/reshape | solution.py:248
  3.0 0.3 select_reduce_fusion
  3.5 0.6 %pad_maximum_fusion.send_ref = f32[4,6,256]{2,1,0:T(8,128)} fusion(f32[1,6,256]{2,1,0:T(8,128)S(1)} %stack.22, f32[1,6,256]{2,1,0:T(8,128)S(1)} %stack.21, f32[1,6,256]{2,1,0:T(8,128)S(1)} %stack.20, f32[1,6,256]{2,1,0:T(8,128)S(1)} %stack.19), kind=kLoop, calls=%fused_computation.21 | loop fusion | flops 18432 | bytes 49152 | tf_op jit(solution)/shard_map/stack | solution.py:261
  4.1 12.3 %shard_map.85 = f32[4,6,256]{2,1,0:T(8,128)} custom-call(f32[4,6,256]{2,1,0:T(8,128)} %pad_maximum_fusion.send_ref), custom_call_target="tpu_custom_call" | custom-call | tf_op jit(solution)/shard_map/pallas_call | solution.py:121
  16.4 0.8 %fusion.11 = (f32[1,3,256]{2,1,0:T(4,128)S(1)}, f32[1,3,256]{2,1,0:T(4,128)S(1)}, f32[1,3,256]{2,1,0:T(4,128)S(1)}, f32[1,3,256]{2,1,0:T(4,128)S(1)}, f32[1,3,25...) fusion(f32[4,6,256]{2,1,0:T(8,128)} %shard_map.85), kind=kLoop, calls=%fused_computation.41 | loop fusion | bytes 49152 | tf_op jit(solution)/shard_map/slice | solution.py:263
  17.5 0.6 %copy.15 = f32[1,3,20,128]{3,1,2,0:T(4,128)} copy(f32[1,3,20,128]{3,2,1,0:T(8,128)S(1)} %bitcast.30) | data formatting | bytes 61440
  18.1 0.6 %copy.14 = f32[1,3,20,128]{3,1,2,0:T(4,128)} copy(f32[1,3,20,128]{3,2,1,0:T(8,128)S(1)} %bitcast.29) | data formatting | bytes 61440
  18.7 14.3 %shard_map.86 = f32[2,8,16,128]{3,2,1,0:T(8,128)} custom-call(s32[1,20]{1,0:T(1,128)} %flags_ref.1, s32[3,3]{1,0:T(4,128)} %offsets_ref.1, f32[3,2560]{1,0:T(4,128)} %bitcast.25, f32[3,2560]{1,0:T(4,128)} %bitcast.27, s32[3,2560]{1,0:T(4,128)} %pixels_ref.1), custom_call_target="tpu_custom_call" | custom-call | tf_op jit(solution)/shard_map/pallas_call | solution.py:221
  33.1 0.9 %slice_convert_fusion = s32[1,128,64]{2,1,0:T(8,128)S(1)} fusion(f32[2,128,128]{2,1,0:T(8,128)} %bitcast.24), kind=kLoop, calls=%fused_computation.9 | loop fusion | flops 8192 | bytes 65536 | tf_op jit(solution)/shard_map/convert_element_type | solution.py:270
  34.0 0.1 convert_element_type.34
  34.1 0.9 %bitcast_convert_fusion = bf16[2,128,128]{2,1,0:T(8,128)(2,1)S(1)} fusion(f32[2,8,16,128]{3,2,1,0:T(8,128)} %shard_map.86), kind=kLoop, calls=%fused_computation.38 | loop fusion | flops 32768 | bytes 196608 | tf_op jit(solution)/shard_map/convert.8
  35.0 0.1 slice_bitcast_fusion.2
  35.1 0.1 convert_element_type.36
  35.3 0.4 %fusion = bf16[8192,128]{0,1:T(8,128)(2,1)S(1)} fusion(s32[8192]{0:T(1024)S(1)} %get-tuple-element.69), kind=kLoop, calls=%fused_computation.1 | loop fusion | flops 2097152 | bytes 2129920 | tf_op jit(solution)/shard_map/convert_element_type | solution.py:274
  35.7 0.4 %broadcast_multiply_fusion = bf16[8192,3,128]{0,2,1:T(8,128)(2,1)S(1)} fusion(bf16[8192,128]{0,1:T(8,128)(2,1)S(1)} %fusion, bf16[8192,3]{0,1:T(4,128)(2,1)S(1)} %convert_element_type.36), kind=kLoop, calls=%fused_computation.2 | loop fusion | flops 3145728 | bytes 8437760 | tf_op jit(solution)/shard_map/mul | solution.py:275
  36.1 2.7 %fusion.1 = f32[64,384]{1,0:T(8,128)} fusion(bf16[8192,384]{0,1:T(8,128)(2,1)S(1)} %bitcast.23, s32[8192]{0:T(1024)S(1)} %get-tuple-element.68), kind=kOutput, calls=%fused_computation.4 | convolution fusion | flops 403177472 | bytes 6422528 | tf_op jit(solution)/shard_map/dot_general | solution.py:278
  (25 shorter events, 0.4 us)

commit v13 on v12

--- a/solution.py
+++ b/solution.py
@@ -84,7 +84,7 @@
         out_ref[row] = recv[:, :, row, :]
 
 
-def migrate_kernel(send_ref, out_ref, recv, send_sem, recv_sem):
+def migrate_kernel(order_ref, positions_ref, velocities_ref, places_ref, speeds_ref, outgoing, recv, send_sem, recv_sem):
     count_x = lax.axis_size("gx")
     count_y = lax.axis_size("gy")
     x = lax.axis_index("gx")
@@ -98,11 +98,38 @@
     barrier = pltpu.get_barrier_semaphore()
     for where in faces:
         pl.semaphore_signal(barrier, 1, device_id=where, device_id_type=MESH)
+
+    blocks = order_ref.shape[1]
+    width = lane_count
+    lanes = lambda b: slice(b * width, (b + 1) * width)
+    drifted = [positions_ref[:, lanes(b)] + time_step * velocities_ref[:, lanes(b)] for b in range(blocks)]
+    moving = [velocities_ref[:, lanes(b)] for b in range(blocks)]
+
+    def ordered(source, k):
+        total = None
+        for b in range(blocks):
+            term = jnp.where(order_ref[0, k] == b, source[b], 0.0)
+            total = term if total is None else total + term
+        return total
+
+    stay = 4 * MOVERS
+    for k in range(stay, blocks):
+        places_ref[:, lanes(k - stay)] = ordered(drifted, k)
+        speeds_ref[:, lanes(k - stay)] = ordered(moving, k)
+    component_row = lax.broadcasted_iota(jnp.int32, (3, width), 0)
+    steps = ((0, -1.0), (0, 1.0), (1, -1.0), (1, 1.0))
+    for face, (component, sign_step) in enumerate(steps):
+        for j in range(MOVERS):
+            k = face * MOVERS + j
+            moved = ordered(drifted, k) + jnp.where(component_row == component, sign_step, 0.0)
+            outgoing[face, 0:3, lanes(j)] = moved
+            outgoing[face, 3:6, lanes(j)] = ordered(moving, k)
     pl.semaphore_wait(barrier, len(faces))
+
     copies = []
     for face, where in enumerate(faces):
         copy = pltpu.make_async_remote_copy(
-            src_ref=send_ref.at[face],
+            src_ref=outgoing.at[face],
             dst_ref=recv.at[face],
             send_sem=send_sem.at[face],
             recv_sem=recv_sem.at[face],
@@ -113,23 +140,33 @@
         copies.append(copy)
     for copy in copies:
         copy.wait()
-    out_ref[...] = recv[...]
-
-
-def migrate(leaving):
-    faces = leaving.shape[0]
+    for face in range(len(faces)):
+        for j in range(MOVERS):
+            k = blocks - stay + face * MOVERS + j
+            places_ref[:, lanes(k)] = recv[face, 0:3, lanes(j)]
+            speeds_ref[:, lanes(k)] = recv[face, 3:6, lanes(j)]
+
+
+def migrate(block_order, positions, velocities):
+    smem = pl.BlockSpec(memory_space=pltpu.SMEM)
+    vmem = pl.BlockSpec(memory_space=pltpu.VMEM)
+    buffer = (4, 6, MOVERS * lane_count)
     return pl.pallas_call(
         migrate_kernel,
-        out_shape=jax.ShapeDtypeStruct(leaving.shape, jnp.float32),
-        in_specs=[pl.BlockSpec(memory_space=pltpu.VMEM)],
-        out_specs=pl.BlockSpec(memory_space=pltpu.VMEM),
+        out_shape=(
+            jax.ShapeDtypeStruct(positions.shape, jnp.float32),
+            jax.ShapeDtypeStruct(velocities.shape, jnp.float32),
+        ),
+        in_specs=[smem, vmem, vmem],
+        out_specs=(vmem, vmem),
         scratch_shapes=[
-            pltpu.VMEM(leaving.shape, jnp.float32),
-            pltpu.SemaphoreType.DMA((faces,)),
-            pltpu.SemaphoreType.DMA((faces,)),
+            pltpu.VMEM(buffer, jnp.float32),
+            pltpu.VMEM(buffer, jnp.float32),
+            pltpu.SemaphoreType.DMA((4,)),
+            pltpu.SemaphoreType.DMA((4,)),
         ],
         compiler_params=pltpu.CompilerParams(collective_id=1, has_side_effects=True),
-    )(leaving)
+    )(block_order, positions, velocities)
 
 
 def fill_send(flags_ref, offsets_ref, places_ref, speeds_ref, pixels_ref, devices):
@@ -241,28 +278,10 @@
 
 
 def on_device(positions, velocities, block_order, flags, offsets, pixels):
-    blocks = block_order.shape[1]
-    width = positions.shape[1] // blocks
-    block_ids = jnp.arange(blocks, dtype=jnp.int32)
-    order_hits = block_order[0][:, None] == block_ids[None, :]
-    places = pick(positions.reshape(3, blocks, width) + time_step * velocities.reshape(3, blocks, width), order_hits)
-    speeds = pick(velocities.reshape(3, blocks, width), order_hits)
-
     count_x = lax.axis_size("gx")
     count_y = lax.axis_size("gy")
     devices = count_x * count_y
-
-    def leaving(which_set, component, sign_step):
-        first_block = which_set * MOVERS
-        moved_pos = places[:, first_block : first_block + MOVERS].at[component].add(sign_step)
-        return jnp.concatenate([moved_pos, speeds[:, first_block : first_block + MOVERS]], axis=0)
-
-    outgoing = [leaving(0, 0, -1.0), leaving(1, 0, 1.0), leaving(2, 1, -1.0), leaving(3, 1, 1.0)]
-    arrived = migrate(jnp.stack(outgoing).reshape(4, 6, MOVERS * width)).reshape(4, 6, MOVERS, width)
-    new_places = jnp.concatenate([places[:, 4 * MOVERS :]] + [got[:3] for got in arrived], axis=1)
-    new_speeds = jnp.concatenate([speeds[:, 4 * MOVERS :]] + [got[3:] for got in arrived], axis=1)
-    new_places = new_places.reshape(3, blocks * width)
-    new_speeds = new_speeds.reshape(3, blocks * width)
+    new_places, new_speeds = migrate(block_order, positions, velocities)
     half = lane_count // 2
     got = exchange(flags, offsets, new_places, new_speeds, pixels, count_x, count_y)
     got_values = jnp.stack([got[0, :, :half], got[0, :, half:], got[1, :, :half]], axis=1)

time: 39.3 us -> 34.8 us (0.89)
  local copies, waits for them, and re-layouts: 4.22 us -> 1.53 us
  other arithmetic: 4.51 us -> 2.76 us
    reshape x2 -> x0, local copies, waits for them, and re-layouts: 1.59 us -> none  [the longest x1 0.8 us: on_device(): positions.reshape(3, blocks, width)]
    slice x12 -> x0, local copies, waits for them, and re-layouts: 0.96 us -> none  [the longest x5 0.88 us: on_device(): got[3:]]
    eq x1 -> x0, other arithmetic: 0.73 us -> none  [on_device(): order_hits = block_order[0][:, None] == block_ids[None, :]]
    another operation x2 -> x1, other arithmetic: 1.54 us -> 0.92 us
    unnamed x2 -> x6, local copies, waits for them, and re-layouts: 1.26 us -> 1.24 us
where the time goes in v13:
time: 34.8 us; the launch traced here: 34.5 us
  Pallas kernels  26.9 us (77%)
  other arithmetic  2.76 us (8%)
  matrix products  2.68 us (8%)
  local copies, waits for them, and re-layouts  1.53 us (4%)
  between operations  0.7 us (2%)
    pallas_call x1, Pallas kernels, exchange(): pl.pallas_call(exchange_kernel, out_shape=jax.ShapeDtypeStruct((2, count_...  14.4 us
    pallas_call x1, Pallas kernels, migrate(): pl.pallas_call(migrate_kernel, out_shape=(jax.ShapeDtypeStruct(positions....  12.5 us
    dot_general x1, matrix products, on_device(): maps = jnp.dot(row_hits, spread, preferred_element_type=jnp.float32)  2.68 us
    unnamed x6, local copies, waits for them, and re-layouts  1.24 us
    convert_element_type x1, other arithmetic, on_device(): got_pixel = got[1, :, half:].reshape(devices * half).astype(jnp.int32)  0.92 us
    another operation x1, other arithmetic  0.92 us

profile of v13, /device:TPU:1, one launch (start us, length us, event | category | flops | bytes accessed | tf_op | source)
XLA Modules:
  0.0 34.5 jit_solution(6049322787296281732)
XLA Ops:
  0.6 12.5 %shard_map.85 = (f32[3,2560]{1,0:T(4,128)}, f32[3,2560]{1,0:T(4,128)}) custom-call(s32[1,20]{1,0:T(1,128)} %order_ref.1, f32[3,2560]{1,0:T(4,128)} %positions_ref.1, f32[3,2560]{1,0:T(4,128)} %velocities_ref.1), custom_call_target="tpu_custom_call" | custom-call | tf_op jit(solution)/shard_map/pallas_call | solution.py:154
  13.1 14.4 %shard_map.86 = f32[2,8,16,128]{3,2,1,0:T(8,128)} custom-call(s32[1,20]{1,0:T(1,128)} %flags_ref.1, s32[3,3]{1,0:T(4,128)} %offsets_ref.1, f32[3,2560]{1,0:T(4,128)} %get-tuple-element.15.places_ref, f32[3,2560]{1,0:T(4,128)} %get-tuple-element.16.speeds_ref, s32[3,2560]{1,0:T(4,128)} %pixels_ref.1), custom_call_target="tpu_custom_call" | custom-call | tf_op jit(solution)/shard_map/pallas_call | solution.py:258
  27.5 0.9 %slice_convert_fusion = s32[1,128,64]{2,1,0:T(8,128)S(1)} fusion(f32[2,128,128]{2,1,0:T(8,128)} %bitcast.15), kind=kLoop, calls=%fused_computation.7 | loop fusion | flops 8192 | bytes 65536 | tf_op jit(solution)/shard_map/convert_element_type | solution.py:289
  28.4 0.1 convert_element_type.34
  28.6 0.9 %bitcast_convert_fusion = bf16[2,128,128]{2,1,0:T(8,128)(2,1)S(1)} fusion(f32[2,8,16,128]{3,2,1,0:T(8,128)} %shard_map.86), kind=kLoop, calls=%fused_computation.19 | loop fusion | flops 32768 | bytes 196608 | tf_op jit(solution)/shard_map/convert.8
  29.5 0.1 slice_bitcast_fusion.2
  29.6 0.1 convert_element_type.36
  29.7 0.4 %fusion = bf16[8192,128]{0,1:T(8,128)(2,1)S(1)} fusion(s32[8192]{0:T(1024)S(1)} %get-tuple-element.11), kind=kLoop, calls=%fused_computation.1 | loop fusion | flops 2097152 | bytes 2129920 | tf_op jit(solution)/shard_map/convert_element_type | solution.py:293
  30.1 0.0 copy-start.1
  30.2 0.0 copy-start
  30.2 0.4 %broadcast_multiply_fusion = bf16[8192,3,128]{0,2,1:T(8,128)(2,1)S(1)} fusion(bf16[8192,128]{0,1:T(8,128)(2,1)S(1)} %fusion, bf16[8192,3]{0,1:T(4,128)(2,1)S(1)} %convert_element_type.36), kind=kLoop, calls=%fused_computation.2 | loop fusion | flops 3145728 | bytes 8437760 | tf_op jit(solution)/shard_map/mul | solution.py:294
  30.6 2.7 %fusion.1 = f32[64,384]{1,0:T(8,128)} fusion(bf16[8192,384]{0,1:T(8,128)(2,1)S(1)} %bitcast.14, s32[8192]{0:T(1024)S(1)} %get-tuple-element.10), kind=kOutput, calls=%fused_computation.4 | convolution fusion | flops 403177472 | bytes 6422528 | tf_op jit(solution)/shard_map/dot_general | solution.py:297
  33.3 0.0 copy-done.1
  33.3 0.6 %copy.12 = f32[3,2560]{1,0:T(4,128)} copy(f32[3,2560]{1,0:T(4,128)S(1)} %copy-done.1) | data formatting | bytes 61440
  33.9 0.0 copy-done
  33.9 0.6 %copy.13 = f32[3,2560]{1,0:T(4,128)} copy(f32[3,2560]{1,0:T(4,128)S(1)} %copy-done) | data formatting | bytes 61440
  (2 shorter events, 0.1 us)
Async XLA Ops:
  30.1 3.1 %copy-start.1 = (f32[3,2560]{1,0:T(4,128)S(1)}, f32[3,2560]{1,0:T(4,128)}, u32[]{:S(2)}) copy-start(f32[3,2560]{1,0:T(4,128)} %get-tuple-element.15.places_ref) | copy-start | bytes 92164
  30.2 3.8 %copy-start = (f32[3,2560]{1,0:T(4,128)S(1)}, f32[3,2560]{1,0:T(4,128)}, u32[]{:S(2)}) copy-start(f32[3,2560]{1,0:T(4,128)} %get-tuple-element.16.speeds_ref) | copy-start | bytes 92164

commit v14 on v13

--- a/solution.py
+++ b/solution.py
@@ -16,7 +16,7 @@
 MESH = pl.DeviceIdType.MESH
 
 
-def exchange_kernel(flags_ref, offsets_ref, places_ref, speeds_ref, pixels_ref, out_ref, send_ref, middle, recv, send_sems, recv_sems):
+def exchange_kernel(flags_ref, offsets_ref, places_ref, speeds_ref, pixels_ref, out_ref, pixel_ref, send_ref, middle, recv, send_sems, recv_sems):
     count_x, count_y = send_ref.shape[0], send_ref.shape[1]
     x = lax.axis_index("gx")
     y = lax.axis_index("gy")
@@ -81,7 +81,8 @@
         recv.at[pl.ds(0, count_x - 1)], recv.at[pl.ds(0, count_x - 1)], send_sems.at[1]
     ).wait()
     for row in range(out_ref.shape[0]):
-        out_ref[row] = recv[:, :, row, :]
+        out_ref[row] = recv[:, :, row, :].astype(out_ref.dtype)
+    pixel_ref[...] = recv[:, :, 1, :].astype(jnp.int32)
 
 
 def migrate_kernel(order_ref, positions_ref, velocities_ref, places_ref, speeds_ref, outgoing, recv, send_sem, recv_sem):
@@ -257,9 +258,12 @@
     vmem = pl.BlockSpec(memory_space=pltpu.VMEM)
     got = pl.pallas_call(
         exchange_kernel,
-        out_shape=jax.ShapeDtypeStruct((2, count_x, count_y, lane_count), jnp.float32),
+        out_shape=(
+            jax.ShapeDtypeStruct((2, count_x, count_y, lane_count), jnp.bfloat16),
+            jax.ShapeDtypeStruct((count_x, count_y, lane_count), jnp.int32),
+        ),
         in_specs=[smem, smem, vmem, vmem, vmem],
-        out_specs=vmem,
+        out_specs=(vmem, vmem),
         scratch_shapes=[
             pltpu.VMEM(grid, jnp.float32),
             pltpu.VMEM(middle, jnp.float32),
@@ -269,7 +273,7 @@
         ],
         compiler_params=pltpu.CompilerParams(collective_id=0, has_side_effects=True),
     )(flags, offsets, places, speeds, pixels)
-    return got.reshape(2, devices, lane_count)
+    return got[0].reshape(2, devices, lane_count), got[1].reshape(devices, lane_count)
 
 
 def pick(data, hits):
@@ -283,10 +287,10 @@
     devices = count_x * count_y
     new_places, new_speeds = migrate(block_order, positions, velocities)
     half = lane_count // 2
-    got = exchange(flags, offsets, new_places, new_speeds, pixels, count_x, count_y)
+    got, got_pixel = exchange(flags, offsets, new_places, new_speeds, pixels, count_x, count_y)
     got_values = jnp.stack([got[0, :, :half], got[0, :, half:], got[1, :, :half]], axis=1)
     got_values = got_values.reshape(devices, 3, half).transpose(0, 2, 1).reshape(devices * half, 3)
-    got_pixel = got[1, :, half:].reshape(devices * half).astype(jnp.int32)
+    got_pixel = got_pixel[:, half:].reshape(devices * half)
     rows = got_pixel // lane_count
     lanes = got_pixel % lane_count
     row_hits = (rows[None, :] == jnp.arange(STRIP_ROWS, dtype=jnp.int32)[:, None]).astype(jnp.bfloat16)

time: 34.8 us -> 34.9 us (level)
  other arithmetic: 2.76 us -> 0.93 us
  local copies, waits for them, and re-layouts: 1.53 us -> 3.28 us
    convert_element_type x2 -> x0, other arithmetic: 0.95 us -> none  [the longest x1 0.92 us: on_device(): got_pixel = got[1, :, half:].reshape(devices * half).astype(jnp.int32)]
    slice x0 -> x1, local copies, waits for them, and re-layouts: none -> 0.92 us  [on_device(): got_pixel = got_pixel[:, half:].reshape(devices * half)]
    another operation x1 -> x0, other arithmetic: 0.92 us -> none
    another operation x1, local copies, waits for them, and re-layouts: 0.08 us -> 0.92 us  [on_device(): jnp.stack([got[0, :, :half], got[0, :, half:], got[1, :, :half]], axis=1)]
where the time goes in v14:
time: 34.9 us; the launch traced here: 34.5 us
  Pallas kernels  26.9 us (77%)
  local copies, waits for them, and re-layouts  3.28 us (9%)
  matrix products  2.67 us (8%)
  other arithmetic  0.93 us (3%)
  between operations  0.69 us (2%)
    pallas_call x1, Pallas kernels, exchange(): pl.pallas_call(exchange_kernel, out_shape=(jax.ShapeDtypeStruct((2, count...  14.5 us
    pallas_call x1, Pallas kernels, migrate(): pl.pallas_call(migrate_kernel, out_shape=(jax.ShapeDtypeStruct(positions....  12.5 us
    dot_general x1, matrix products, on_device(): maps = jnp.dot(row_hits, spread, preferred_element_type=jnp.float32)  2.67 us
    unnamed x6, local copies, waits for them, and re-layouts  1.24 us
    another operation x1, local copies, waits for them, and re-layouts, on_device(): jnp.stack([got[0, :, :half], got[0, :, half:], got[1, :, :half]], axis=1)  0.92 us
    slice x1, local copies, waits for them, and re-layouts, on_device(): got_pixel = got_pixel[:, half:].reshape(devices * half)  0.92 us

profile of v14, /device:TPU:1, one launch (start us, length us, event | category | flops | bytes accessed | tf_op | source)
XLA Modules:
  0.0 34.5 jit_solution(16003738000079750414)
XLA Ops:
  0.6 12.5 %shard_map.85 = (f32[3,2560]{1,0:T(4,128)}, f32[3,2560]{1,0:T(4,128)}) custom-call(s32[1,20]{1,0:T(1,128)} %order_ref.1, f32[3,2560]{1,0:T(4,128)} %positions_ref.1, f32[3,2560]{1,0:T(4,128)} %velocities_ref.1), custom_call_target="tpu_custom_call" | custom-call | tf_op jit(solution)/shard_map/pallas_call | solution.py:155
  13.1 14.5 %shard_map.86 = (bf16[2,8,16,128]{3,2,1,0:T(8,128)(2,1)}, s32[8,16,128]{2,1,0:T(8,128)}) custom-call(s32[1,20]{1,0:T(1,128)} %flags_ref.1, s32[3,3]{1,0:T(4,128)} %offsets_ref.1, f32[3,2560]{1,0:T(4,128)} %get-tuple-element.19.places_ref, f32[3,2560]{1,0:T(4,128)} %get-tuple-element.20.speeds_ref, s32[3,2560]{1,0:T(4,128)} %pixels_ref.1), custom_call_target="tpu_custom_call" | custom-call | tf_op jit(solution)/shard_map/pallas_call | solution.py:259
  27.6 0.9 %slice.16 = s32[128,64]{1,0:T(8,128)S(1)} slice(s32[128,128]{1,0:T(8,128)} %bitcast.16), slice={[0:128], [64:128]} | slice | bytes 65536 | tf_op jit(solution)/shard_map/slice | solution.py:293
  28.5 0.1 reshape.88
  28.6 0.9 %slice_bitcast_fusion.2 = (bf16[128,1,64]{2,0,1:T(8,128)(2,1)S(1)}, bf16[128,1,64]{2,0,1:T(8,128)(2,1)S(1)}, bf16[128,1,64]{2,0,1:T(8,128)(2,1)S(1)}) fusion(bf16[2,128,128]{2,1,0:T(8,128)(2,1)} %bitcast.15), kind=kLoop, calls=%fused_computation.14 | loop fusion | bytes 98304 | tf_op jit(solution)/shard_map/stack;squeeze | solution.py:291
  29.5 0.1 mul.19
  29.7 0.4 %fusion = bf16[8192,128]{0,1:T(8,128)(2,1)S(1)} fusion(s32[8192]{0:T(1024)S(1)} %get-tuple-element.15), kind=kLoop, calls=%fused_computation.1 | loop fusion | flops 2097152 | bytes 2129920 | tf_op jit(solution)/shard_map/convert_element_type | solution.py:297
  30.1 0.0 copy-start.1
  30.1 0.0 copy-start
  30.1 0.4 %broadcast_multiply_fusion = bf16[8192,3,128]{0,2,1:T(8,128)(2,1)S(1)} fusion(bf16[8192,128]{0,1:T(8,128)(2,1)S(1)} %fusion, bf16[8192,3]{0,1:T(4,128)(2,1)S(1)} %mul.19), kind=kLoop, calls=%fused_computation.2 | loop fusion | flops 3145728 | bytes 8437760 | tf_op jit(solution)/shard_map/mul | solution.py:298
  30.6 2.7 %fusion.1 = f32[64,384]{1,0:T(8,128)} fusion(bf16[8192,384]{0,1:T(8,128)(2,1)S(1)} %bitcast.14, s32[8192]{0:T(1024)S(1)} %get-tuple-element.14), kind=kOutput, calls=%fused_computation.4 | convolution fusion | flops 403177472 | bytes 6422528 | tf_op jit(solution)/shard_map/dot_general | solution.py:301
  33.3 0.0 copy-done.1
  33.3 0.6 %copy.12 = f32[3,2560]{1,0:T(4,128)} copy(f32[3,2560]{1,0:T(4,128)S(1)} %copy-done.1) | data formatting | bytes 61440
  33.9 0.0 copy-done
  33.9 0.6 %copy.13 = f32[3,2560]{1,0:T(4,128)} copy(f32[3,2560]{1,0:T(4,128)S(1)} %copy-done) | data formatting | bytes 61440
  (2 shorter events, 0.1 us)
Async XLA Ops:
  30.1 3.1 %copy-start.1 = (f32[3,2560]{1,0:T(4,128)S(1)}, f32[3,2560]{1,0:T(4,128)}, u32[]{:S(2)}) copy-start(f32[3,2560]{1,0:T(4,128)} %get-tuple-element.19.places_ref) | copy-start | bytes 92164
  30.1 3.8 %copy-start = (f32[3,2560]{1,0:T(4,128)S(1)}, f32[3,2560]{1,0:T(4,128)}, u32[]{:S(2)}) copy-start(f32[3,2560]{1,0:T(4,128)} %get-tuple-element.20.speeds_ref) | copy-start | bytes 92164

commit v15 on v13

--- a/solution.py
+++ b/solution.py
@@ -32,8 +32,10 @@
         pl.semaphore_signal(barrier, 1, device_id=where, device_id_type=MESH)
         return carry
 
-    lax.fori_loop(1, count_y, greet_y, 0)
-    lax.fori_loop(1, count_x, greet_x, 0)
+    for offset in range(1, count_y):
+        greet_y(offset, None)
+    for offset in range(1, count_x):
+        greet_x(offset, None)
     first, second = fill_send(flags_ref, offsets_ref, places_ref, speeds_ref, pixels_ref, count_x * count_y)
     for row in range(count_x):
         rows = slice(row * count_y, (row + 1) * count_y)
@@ -55,7 +57,8 @@
         ).start()
         return carry
 
-    lax.fori_loop(1, count_y, post_y, 0)
+    for offset in range(1, count_y):
+        post_y(offset, None)
     pltpu.make_async_copy(middle, middle, recv_sems.at[0]).wait()
 
     pltpu.make_async_copy(middle.at[:, x], recv.at[x], recv_sems.at[1]).start()
@@ -72,7 +75,8 @@
         ).start()
         return carry
 
-    lax.fori_loop(1, count_x, post_x, 0)
+    for offset in range(1, count_x):
+        post_x(offset, None)
     pltpu.make_async_copy(recv, recv, recv_sems.at[1]).wait()
     pltpu.make_async_copy(
         middle.at[pl.ds(0, count_y - 1)], middle.at[pl.ds(0, count_y - 1)], send_sems.at[0]

time: 34.8 us -> 34.7 us (level)
  no operation moved by 1% of the time
where the time goes in v15:
time: 34.7 us; the launch traced here: 34.4 us
  Pallas kernels  26.7 us (77%)
  other arithmetic  2.76 us (8%)
  matrix products  2.68 us (8%)
  local copies, waits for them, and re-layouts  1.53 us (4%)
  between operations  0.7 us (2%)
    pallas_call x1, Pallas kernels, exchange(): pl.pallas_call(exchange_kernel, out_shape=jax.ShapeDtypeStruct((2, count_...  14.3 us
    pallas_call x1, Pallas kernels, migrate(): pl.pallas_call(migrate_kernel, out_shape=(jax.ShapeDtypeStruct(positions....  12.5 us
    dot_general x1, matrix products, on_device(): maps = jnp.dot(row_hits, spread, preferred_element_type=jnp.float32)  2.68 us
    unnamed x6, local copies, waits for them, and re-layouts  1.24 us
    convert_element_type x1, other arithmetic, on_device(): got_pixel = got[1, :, half:].reshape(devices * half).astype(jnp.int32)  0.92 us
    another operation x1, other arithmetic  0.92 us

profile of v15, /device:TPU:1, one launch (start us, length us, event | category | flops | bytes accessed | tf_op | source)
XLA Modules:
  0.0 34.4 jit_solution(14256622898508219200)
XLA Ops:
  0.6 12.5 %shard_map.85 = (f32[3,2560]{1,0:T(4,128)}, f32[3,2560]{1,0:T(4,128)}) custom-call(s32[1,20]{1,0:T(1,128)} %order_ref.1, f32[3,2560]{1,0:T(4,128)} %positions_ref.1, f32[3,2560]{1,0:T(4,128)} %velocities_ref.1), custom_call_target="tpu_custom_call" | custom-call | tf_op jit(solution)/shard_map/pallas_call | solution.py:158
  13.1 14.3 %shard_map.86 = f32[2,8,16,128]{3,2,1,0:T(8,128)} custom-call(s32[1,20]{1,0:T(1,128)} %flags_ref.1, s32[3,3]{1,0:T(4,128)} %offsets_ref.1, f32[3,2560]{1,0:T(4,128)} %get-tuple-element.15.places_ref, f32[3,2560]{1,0:T(4,128)} %get-tuple-element.16.speeds_ref, s32[3,2560]{1,0:T(4,128)} %pixels_ref.1), custom_call_target="tpu_custom_call" | custom-call | tf_op jit(solution)/shard_map/pallas_call | solution.py:262
  27.4 0.9 %slice_convert_fusion = s32[1,128,64]{2,1,0:T(8,128)S(1)} fusion(f32[2,128,128]{2,1,0:T(8,128)} %bitcast.15), kind=kLoop, calls=%fused_computation.7 | loop fusion | flops 8192 | bytes 65536 | tf_op jit(solution)/shard_map/convert_element_type | solution.py:293
  28.3 0.1 convert_element_type.34
  28.4 0.9 %bitcast_convert_fusion = bf16[2,128,128]{2,1,0:T(8,128)(2,1)S(1)} fusion(f32[2,8,16,128]{3,2,1,0:T(8,128)} %shard_map.86), kind=kLoop, calls=%fused_computation.19 | loop fusion | flops 32768 | bytes 196608 | tf_op jit(solution)/shard_map/convert.8
  29.3 0.1 slice_bitcast_fusion.2
  29.5 0.1 convert_element_type.36
  29.6 0.4 %fusion = bf16[8192,128]{0,1:T(8,128)(2,1)S(1)} fusion(s32[8192]{0:T(1024)S(1)} %get-tuple-element.11), kind=kLoop, calls=%fused_computation.1 | loop fusion | flops 2097152 | bytes 2129920 | tf_op jit(solution)/shard_map/convert_element_type | solution.py:297
  30.0 0.0 copy-start.1
  30.0 0.0 copy-start
  30.0 0.4 %broadcast_multiply_fusion = bf16[8192,3,128]{0,2,1:T(8,128)(2,1)S(1)} fusion(bf16[8192,128]{0,1:T(8,128)(2,1)S(1)} %fusion, bf16[8192,3]{0,1:T(4,128)(2,1)S(1)} %convert_element_type.36), kind=kLoop, calls=%fused_computation.2 | loop fusion | flops 3145728 | bytes 8437760 | tf_op jit(solution)/shard_map/mul | solution.py:298
  30.5 2.7 %fusion.1 = f32[64,384]{1,0:T(8,128)} fusion(bf16[8192,384]{0,1:T(8,128)(2,1)S(1)} %bitcast.14, s32[8192]{0:T(1024)S(1)} %get-tuple-element.10), kind=kOutput, calls=%fused_computation.4 | convolution fusion | flops 403177472 | bytes 6422528 | tf_op jit(solution)/shard_map/dot_general | solution.py:301
  33.2 0.0 copy-done.1
  33.2 0.6 %copy.12 = f32[3,2560]{1,0:T(4,128)} copy(f32[3,2560]{1,0:T(4,128)S(1)} %copy-done.1) | data formatting | bytes 61440
  33.8 0.0 copy-done
  33.8 0.6 %copy.13 = f32[3,2560]{1,0:T(4,128)} copy(f32[3,2560]{1,0:T(4,128)S(1)} %copy-done) | data formatting | bytes 61440
  (2 shorter events, 0.1 us)
Async XLA Ops:
  30.0 3.2 %copy-start.1 = (f32[3,2560]{1,0:T(4,128)S(1)}, f32[3,2560]{1,0:T(4,128)}, u32[]{:S(2)}) copy-start(f32[3,2560]{1,0:T(4,128)} %get-tuple-element.15.places_ref) | copy-start | bytes 92164
  30.0 3.8 %copy-start = (f32[3,2560]{1,0:T(4,128)S(1)}, f32[3,2560]{1,0:T(4,128)}, u32[]{:S(2)}) copy-start(f32[3,2560]{1,0:T(4,128)} %get-tuple-element.16.speeds_ref) | copy-start | bytes 92164
